TPU v7x, 256 devices: a whole 4x4x8 slice. The times are simulated.
256 devices in a mesh: shot: 128 (over x, y, z), freq: 2 (over core).
Axes of the slice: x: 4, y: 4, z: 8, core: 2. Of those that a mesh axis runs over, the one named last changes fastest.
Arguments:
- traces: bfloat16 [256, 1024, 1024], P('shot', None, 'freq'), may hold values from -6 to 6
- frequency_bins: int32 [8], replicated, may hold values from 1 to 511
- aperture: int32 [256, 1024, 32], P(None, 'shot'), may hold values from 0 to 255, as said below
- lengths: int32 [256, 1024], P(None, 'shot'), may hold values from 1 to 32, as said below
- filters: bfloat16 [256, 31], P('shot'), may hold values from -1 to 1
Outputs:
- multiples: bfloat16 [256, 1024, 1024], P('shot', None, 'freq')
Inputs may be any that keep to these rules, and one draw needn't show every extreme that they name: aperture[s, r, k] names a shot whose source lies at receiver station 4 times that number; only entries with k below lengths[s, r] are used. The lengths of the shots held by one device along `shot` (one index of the `shot` axis) and the receivers of one index of shot sum to at most 264; in every draw the shots of some index reach 264 with the receivers of every index.
All inputs are finite; a program needn't handle non-finite values.
Results may differ from a plain program's by a relative error of at most 0.015.
Values may be sent and summed in bfloat16 or wider, within the bound.
A program may use at most 192 MiB of HBM per device.

v0:
```python
import math

import jax
import jax.numpy as jnp
from jax import lax
from jax.sharding import PartitionSpec as P

NT = 1024
NF = 8
KMAX = 32
TAPS = 31


def extended(shard, sides, width):
    for axis, dim in sides:
        devices, length = (lax.axis_size(axis), shard.shape[dim])
        up = [(i, (i + 1) % devices) for i in range(devices - 1)]
        down = [(j, i) for i, j in up]
        last = lax.slice_in_dim(shard, length - width, length, axis=dim)
        leading = lax.slice_in_dim(shard, 0, width, axis=dim)
        before = lax.ppermute(last, axis, up)
        after = lax.ppermute(leading, axis, down)
        shard = jnp.concatenate([before, shard, after], axis=dim)
    return shard


def fourier_rows(bin_rows, first_time, sample_count, period):
    sample_times = first_time + jnp.arange(sample_count, dtype=jnp.int32)
    phases = bin_rows[:, None] * sample_times[None, :] % period
    angles = phases.astype(jnp.float32) * (2.0 * math.pi / period)
    return (jnp.cos(angles), jnp.sin(angles))


def pair_product(first_leg, second):
    first_leg = first_leg.astype(jnp.float32)
    second = second.astype(jnp.float32)
    real_part = first_leg[:, 0] * second[:, 0] - first_leg[:, 1] * second[:, 1]
    imag_part = first_leg[:, 0] * second[:, 1] + first_leg[:, 1] * second[:, 0]
    return jnp.stack([real_part, imag_part], axis=1)


def pick_columns(table, codes):
    block_width = 2048
    column_count = table.shape[1]
    wanted = codes.shape[0]
    block_count = -(-wanted // block_width)
    extra = block_count * block_width - wanted
    codes = jnp.concatenate([codes.astype(jnp.int32), jnp.full((extra,), -1, jnp.int32)]).reshape(
        block_count, block_width
    )
    column_ids = jnp.arange(column_count, dtype=jnp.int32)[:, None]

    def one_block(block_codes):
        onehot = (column_ids == block_codes[None, :]).astype(jnp.bfloat16)
        return jnp.dot(table, onehot, preferred_element_type=jnp.float32).astype(jnp.bfloat16)

    picked = lax.map(one_block, codes)
    picked = picked.transpose(1, 0, 2).reshape(table.shape[0], block_count * block_width)
    return picked


def pick_each(tables, codes):

    def one_table(inputs):
        return pick_columns(inputs[0], inputs[1])

    return lax.map(one_table, (tables, codes))


def shards(traces, frequency_bins, aperture, lengths, filters):
    shot_dev, receivers, time_dev = traces.shape
    groups = lax.axis_size("shot")
    shots = shot_dev * groups
    receiver_dev = receivers // groups
    stride = receivers // shots
    local_bins = NF // lax.axis_size("freq")
    start_time = lax.axis_index("freq") * time_dev
    half_taps = (TAPS - 1) // 2
    flat_traces = traces.reshape(shot_dev * receivers, time_dev)
    bin_rows = frequency_bins
    cosines, sines = fourier_rows(bin_rows, start_time, time_dev, NT)
    basis_rows = (jnp.stack([cosines, -sines], axis=1) * NT ** (-0.5)).astype(jnp.bfloat16)
    basis_rows = basis_rows.reshape(lax.axis_size("freq") * local_bins * 2, time_dev)
    term = lax.dot_general(
        basis_rows, flat_traces, (((1,), (1,)), ((), ())), preferred_element_type=jnp.float32
    )
    spectra = lax.psum_scatter(
        term.reshape(lax.axis_size("freq") * local_bins, 2, shot_dev, receivers),
        "freq",
        scatter_dimension=0,
        tiled=True,
    ).astype(jnp.bfloat16)
    gathers = lax.all_to_all(spectra, "shot", split_axis=3, concat_axis=2, tiled=True)
    valid_mask = jnp.arange(KMAX, dtype=jnp.int32)[None, None, :] < lengths[:, :, None]
    station_rows = spectra[:, :, :, ::stride].reshape(local_bins * 2, shot_dev * shots)
    receiver_tables = gathers.reshape(local_bins * 2, shots, receiver_dev).transpose(2, 0, 1)
    list_width = receiver_dev * KMAX
    used_codes = (
        jnp.where(valid_mask, aperture, -1).transpose(1, 0, 2).reshape(receiver_dev, shots * KMAX)
    )
    second = pick_each(receiver_tables, used_codes).reshape(
        receiver_dev, local_bins * 2, shots, KMAX
    )
    second = second.transpose(1, 2, 0, 3).reshape(local_bins * 2, groups, shot_dev, list_width)
    labels = aperture.reshape(1, groups, shot_dev, list_width)
    second, labels = (
        lax.all_to_all(second, "shot", split_axis=1, concat_axis=1, tiled=True),
        lax.all_to_all(labels, "shot", split_axis=1, concat_axis=1, tiled=True),
    )
    station_tables = station_rows.reshape(local_bins * 2, shot_dev, shots).transpose(1, 0, 2)
    station_codes = labels[0].transpose(1, 0, 2).reshape(shot_dev, groups * list_width)
    first_leg = pick_each(station_tables, station_codes).reshape(
        shot_dev, local_bins * 2, groups, list_width
    )
    first_leg = first_leg.transpose(1, 2, 0, 3)
    block_shape = (local_bins, 2, groups, shot_dev, list_width)
    product_terms = pair_product(first_leg.reshape(block_shape), second.reshape(block_shape))
    product_terms = product_terms.reshape(local_bins, 2, groups, shot_dev, receiver_dev, KMAX).sum(
        axis=-1
    )
    summed = product_terms.transpose(0, 1, 3, 2, 4).reshape(local_bins, 2, shot_dev, receivers)
    multiples_spectra = (summed * KMAX ** (-0.5)).astype(jnp.bfloat16)
    piece = lax.all_gather(multiples_spectra, "freq", axis=0, tiled=True)
    row_count = piece.shape[0]
    bin_rows = frequency_bins
    cosines, sines = fourier_rows(bin_rows, start_time, time_dev, NT)
    basis_rows = (
        jnp.stack([cosines, -sines], axis=1).astype(jnp.bfloat16).reshape(row_count * 2, time_dev)
    )
    flat_piece = piece.reshape(row_count * 2, shot_dev * receivers)
    synthesized = lax.dot_general(
        flat_piece, basis_rows, (((0,), (0,)), ((), ())), preferred_element_type=jnp.float32
    )
    predicted = synthesized.astype(jnp.bfloat16).reshape(shot_dev, receivers, time_dev)
    padded = extended(predicted, (("freq", 2),), half_taps)
    padded_width = time_dev + 2 * half_taps
    lag_table = (
        jnp.arange(time_dev, dtype=jnp.int32)[None, :]
        + 2 * half_taps
        - jnp.arange(padded_width, dtype=jnp.int32)[:, None]
    )
    tap_onehot = (lag_table[None] == jnp.arange(TAPS, dtype=jnp.int32)[:, None, None]).astype(
        jnp.bfloat16
    )
    toeplitz = jnp.einsum(
        "sj,jut->sut", filters, tap_onehot, preferred_element_type=jnp.float32
    ).astype(jnp.bfloat16)
    filtered = jnp.einsum("sru,sut->srt", padded, toeplitz, preferred_element_type=jnp.float32)
    return filtered.astype(jnp.bfloat16)


def solution(mesh):
    in_specs = (
        P("shot", None, "freq"),
        P(),
        P(None, "shot", None),
        P(None, "shot"),
        P("shot", None),
    )
    out_specs = P("shot", None, "freq")
    return jax.shard_map(shards, mesh=mesh, in_specs=in_specs, out_specs=out_specs, check_vma=False)
```

profile of v0, /device:TPU:1, one launch (start us, length us, event | category | flops | bytes accessed | tf_op | source)
XLA Modules:
  0.0 197.0 jit_solution(6553147078118205570)
XLA Ops:
  2.2 7.1 %all-reduce.2 = bf16[8,2,2,1024]{3,0,2,1:T(8,128)(2,1)S(1)} all-reduce(f32[8,2,2,1024]{3,0,2,1:T(8,128)S(1)} %fusion.18), channel_id=2, replica_groups=mesh['shot'=128,'freq'=2] {'freq'}, use_global_device_ids=true, to_apply=%region_0.1.clone | all-reduce | flops 32768 | bytes 196608
  10.6 2.1 %copy.49 = bf16[4,2,2,1024]{0,2,1,3:T(2,128)(2,1)} copy(bf16[4,2,2,1024]{3,0,2,1:T(4,128)(2,1)S(1)} %dynamic-slice_convert_fusion) | data formatting | bytes 65536 | tf_op jit(solution)/shard_map/convert_element_type | solution.py:92
  12.7 14.3 %all-to-all-start.1 = ((bf16[4,2,2,1024]{0,2,1,3:T(2,128)(2,1)}), bf16[4,2,2,1024]{0,2,1,3:T(2,128)(2,1)}, u32[]{:S(2)}, u32[]{:S(2)}) async-start(bf16[4,2,2,1024]{0,2,1,3:T(2,128)(2,1)} %copy.49), calls=%async_computation.1 | async-start | bytes 2097152 | tf_op jit(solution)/shard_map/all_to_all | solution.py:93
  28.7 2.3 %copy.48 = s32[8,256,32]{2,1,0:T(8,128)} copy(s32[8,256,32]{1,2,0:T(8,128)} %select_bitcast_fusion) | data formatting | bytes 524288 | tf_op jit(solution)/shard_map/transpose | solution.py:99
  31.0 2.4 %reshape.222 = s32[8,8192]{1,0:T(8,128)} reshape(s32[8,256,32]{2,1,0:T(8,128)} %copy.48) | data formatting | bytes 524288 | tf_op jit(solution)/shard_map/reshape | solution.py:99
  36.5 21.0 %all-to-all-done.1 = bf16[4,2,2,1024]{0,2,1,3:T(2,128)(2,1)} async-done(((bf16[4,2,2,1024]{0,2,1,3:T(2,128)(2,1)}), bf16[4,2,2,1024]{0,2,1,3:T(2,128)(2,1)}, u32[]{:S(2)}, u32[]{:S(2)}) %all-to-all-start.1) | async-done | bytes 32800 | tf_op jit(solution)/shard_map/all_to_all | solution.py:93
  57.5 6.4 %all-to-all-start = ((s32[1,128,2,256]{3,2,0,1:T(2,128)}), s32[1,128,2,256]{3,2,0,1:T(2,128)S(1)}, u32[]{:S(2)}, u32[]{:S(2)}) async-start(s32[1,128,2,256]{3,2,0,1:T(2,128)} %bitcast.6), calls=%async_computation | async-start | bytes 524288 | tf_op jit(solution)/shard_map/all_to_all | solution.py:108
  63.9 5.0 %copy.65 = bf16[4,2,2,128,8]{4,3,2,1,0:T(8,128)(2,1)S(1)} copy(bf16[4,2,2,128,8]{0,2,1,4,3:T(2,128)(2,1)} %bitcast.18) | data formatting | bytes 65536 | tf_op jit(solution)/shard_map/all_to_all | solution.py:93
  69.6 28.5 %while.45 = (s32[]{:T(128)}, bf16[8,8,8192]{2,1,0:T(8,128)(2,1)}, s32[8,8192]{1,0:T(8,128)}, bf16[8,8,256]{2,1,0:T(8,128)(2,1)S(1)}, s32[]{:T(128)}, /*index=5*/s32[]{:T(128)}, s32[]{:T(128)}) while((s32[]{:T(128)}, bf16[8,8,8192]{2,1,0:T(8,128)(2,1)}, s32[8,8192]{1,0:T(8,128)}, bf16[8,8,256]{2,1,0:T(8,128)(2,1)S(1)}, s32[]{:T(128)}, ...), condition=%wide.region_8.9_spmd, body=%wide.region_5.8_spmd.sunk | while | flops 8929284 | bytes 463562 | solution.py:67
  98.1 5.6 %reshape.224 = bf16[8,8,256,32]{3,2,1,0:T(8,128)(2,1)} reshape(bf16[8,8,8192]{2,1,0:T(8,128)(2,1)} %get-tuple-element.104) | data formatting | bytes 2097152 | tf_op jit(solution)/shard_map/reshape | solution.py:101
  103.7 6.8 %copy.53 = bf16[8,256,8,32]{3,2,0,1:T(8,128)(2,1)} copy(bf16[8,256,8,32]{3,1,0,2:T(8,128)(2,1)} %bitcast.104) | data formatting | bytes 2097152 | tf_op jit(solution)/shard_map/transpose | solution.py:104
  110.6 6.2 %reshape.225 = bf16[8,128,2,256]{3,0,2,1:T(8,128)(2,1)} reshape(bf16[8,256,8,32]{3,2,0,1:T(8,128)(2,1)} %copy.53) | data formatting | bytes 2097152 | tf_op jit(solution)/shard_map/reshape | solution.py:104
  116.7 13.6 %all-to-all-start.2 = ((bf16[8,128,2,256]{3,0,2,1:T(8,128)(2,1)}), bf16[8,128,2,256]{3,0,2,1:T(8,128)(2,1)}, u32[]{:S(2)}, u32[]{:S(2)}) async-start(bf16[8,128,2,256]{3,0,2,1:T(8,128)(2,1)} %reshape.225), calls=%async_computation.2 | async-start | bytes 2097152 | tf_op jit(solution)/shard_map/all_to_all | solution.py:107
  130.4 16.9 %while.43 = (s32[]{:T(128)}, bf16[2,8,32768]{2,1,0:T(8,128)(2,1)}, s32[2,32768]{1,0:T(2,128)S(1)}, bf16[2,8,256]{2,1,0:T(8,128)(2,1)S(1)}, s32[]{:T(128)}, /*index=5*/s32[]{:T(128)}, s32[]{:T(128)}) while((s32[]{:T(128)}, bf16[2,8,32768]{2,1,0:T(8,128)(2,1)}, s32[2,32768]{1,0:T(2,128)S(1)}, bf16[2,8,256]{2,1,0:T(8,128)(2,1)S(1)}, s32[]{:T(128)}, ...), condition=%wide.region_4.5_spmd, body=%wide.region_1.4_spmd.sunk | while | flops 8929284 | bytes 1643210 | solution.py:67
  130.8 7.2 %while.46 = (s32[]{:T(128)}, bf16[16,8,2048]{2,1,0:T(8,128)(2,1)S(1)}, s32[16,2048]{1,0:T(8,128)S(1)}, bf16[8,256]{1,0:T(8,128)(2,1)S(1)}, s32[]{:T(128)}) while((s32[]{:T(128)}, bf16[16,8,2048]{2,1,0:T(8,128)(2,1)S(1)}, s32[16,2048]{1,0:T(8,128)S(1)}, bf16[8,256]{1,0:T(8,128)(2,1)S(1)}, s32[]{:T(128)}) %tuple.81), condition=%wide.region_3.3_spmd.clone, body=%wide.region_2.2_spmd.clone.sunk | while | flops 8929282 | bytes 61509 | solution.py:57
  139.2 7.2 %while.46 = (s32[]{:T(128)}, bf16[16,8,2048]{2,1,0:T(8,128)(2,1)S(1)}, s32[16,2048]{1,0:T(8,128)S(1)}, bf16[8,256]{1,0:T(8,128)(2,1)S(1)}, s32[]{:T(128)}) while((s32[]{:T(128)}, bf16[16,8,2048]{2,1,0:T(8,128)(2,1)S(1)}, s32[16,2048]{1,0:T(8,128)S(1)}, bf16[8,256]{1,0:T(8,128)(2,1)S(1)}, s32[]{:T(128)}) %tuple.81), condition=%wide.region_3.3_spmd.clone, body=%wide.region_2.2_spmd.clone.sunk | while | flops 8929282 | bytes 61509 | solution.py:57
  150.2 8.3 %all-to-all-done.2 = bf16[8,128,2,256]{3,0,2,1:T(8,128)(2,1)} async-done(((bf16[8,128,2,256]{3,0,2,1:T(8,128)(2,1)}), bf16[8,128,2,256]{3,0,2,1:T(8,128)(2,1)}, u32[]{:S(2)}, u32[]{:S(2)}) %all-to-all-start.2) | async-done | bytes 1048608 | tf_op jit(solution)/shard_map/all_to_all | solution.py:107
  163.6 2.5 %copy.56 = f32[4,1,128,2,256]{2,4,3,0,1:T(8,128)} copy(f32[4,1,128,2,256]{4,2,3,1,0:T(8,128)} %get-tuple-element.182) | data formatting | bytes 2097152 | tf_op jit(solution)/shard_map/add | solution.py:38
  168.5 6.0 %all_gather.3 = bf16[8,2,2,1024]{3,2,1,0:T(2,128)(2,1)S(1)} all-gather(bf16[4,2,2,1024]{3,2,1,0:T(2,128)(2,1)S(1)} %convert_element_type.101), channel_id=1, replica_groups=mesh['shot'=128,'freq'=2] {'freq'}, dimensions={0}, use_global_device_ids=true | all-gather | bytes 98304 | tf_op jit(solution)/shard_map/all_gather | solution.py:123
  174.6 2.1 %convolution_convert_fusion.2 = bf16[2048,512]{1,0:T(8,128)(2,1)} fusion(bf16[16,2048]{1,0:T(8,128)(2,1)S(1)} %bitcast.118, bf16[16,512]{1,0:T(8,128)(2,1)S(1)} %copy-done.5), kind=kOutput, calls=%fused_computation.23 | convolution fusion | flops 34603008 | bytes 2179072 | tf_op jit(solution)/shard_map/dot_general | solution.py:131
  176.6 4.1 %copy.59 = bf16[2,1024,512]{1,2,0:T(8,128)(2,1)} copy(bf16[2,1024,512]{2,1,0:T(8,128)(2,1)} %bitcast.108) | data formatting | bytes 4194304 | tf_op jit(solution)/shard_map/reshape | solution.py:134
  182.9 3.2 %collective-permute-start.1 = (bf16[2,1024,15]{1,2,0:T(8,128)(2,1)S(1)}, bf16[2,1024,15]{1,2,0:T(8,128)(2,1)S(1)}, u32[]{:S(2)}, u32[]{:S(2)}) collective-permute-start(bf16[2,1024,15]{1,2,0:T(8,128)(2,1)S(1)} %get-tuple-element.184), channel_id=1, source_target_pairs={{1,0},{3,2},{5,4},{7,6},{9,8},{11,10},{13,12},{15,14},{17,16},{19,... | collective-permute-start | bytes 184328 | tf_op jit(solution)/shard_map/ppermute | solution.py:22
  186.1 7.7 %fusion.24 = bf16[2,542,512]{2,0,1:T(2,128)(2,1)S(1)} fusion(s32[542,512]{1,0:T(8,128)S(1)} %copy-done.3, bf16[2,31]{1,0:T(2,128)(2,1)S(1)} %copy-done.7), kind=kOutput, calls=%fused_computation.36 | convolution fusion | flops 43568128 | bytes 2220156 | tf_op jit(solution)/shard_map/sj,jut->sut/dot_general | solution.py:145
  193.8 3.2 %fusion.20 = bf16[2,1024,512]{2,1,0:T(8,128)(2,1)} fusion(bf16[2,1024,15]{1,2,0:T(8,128)(2,1)S(1)} %collective-permute-done.1, bf16[2,1024,512]{1,2,0:T(8,128)(2,1)S(1)} %copy-done.2, bf16[2,1024,15]{1,2,0:T(8,128)(2,1)S(1)} %collective-permute-done, bf16[2,542,512]{2,0,1:T(2,128)(2,1)S(1)} %fusion.24), kind=kOutput, calls=%fused_computation.34 | convolution fusion | flops 1144365056 | bytes 5427200 | tf_op jit(solution)/shard_map/sru,sut->srt/dot_general | solution.py:148
  (239 shorter events, 79.9 us)
Async XLA Ops:
  0.0 1.6 copy-start
  0.0 9.3 %copy-start.8 = (u32[256]{0:T(256)S(1)}, u32[256]{0:T(256)}, u32[]{:S(2)}) copy-start(u32[256]{0:T(256)} %constant.92) | copy-start | bytes 3076
  2.2 25.3 %copy-start.4 = (s32[256,8,32]{0,2,1:T(8,128)S(1)}, s32[256,8,32]{0,2,1:T(8,128)}, u32[]{:S(2)}) copy-start(s32[256,8,32]{0,2,1:T(8,128)} %param.15) | copy-start | bytes 786436
  10.6 17.4 %copy-start.6 = (s32[256,8]{0,1:T(8,128)S(1)}, s32[256,8]{0,1:T(8,128)}, u32[]{:S(2)}) copy-start(s32[256,8]{0,1:T(8,128)} %param.16) | copy-start | bytes 24580
  12.7 44.8 %all-to-all-start.1 = ((bf16[4,2,2,1024]{0,2,1,3:T(2,128)(2,1)}), bf16[4,2,2,1024]{0,2,1,3:T(2,128)(2,1)}, u32[]{:S(2)}, u32[]{:S(2)}) async-start(bf16[4,2,2,1024]{0,2,1,3:T(2,128)(2,1)} %copy.49), calls=%async_computation.1 | async-start | bytes 2097152 | tf_op jit(solution)/shard_map/all_to_all | solution.py:93
  57.5 59.2 %all-to-all-start = ((s32[1,128,2,256]{3,2,0,1:T(2,128)}), s32[1,128,2,256]{3,2,0,1:T(2,128)S(1)}, u32[]{:S(2)}, u32[]{:S(2)}) async-start(s32[1,128,2,256]{3,2,0,1:T(2,128)} %bitcast.6), calls=%async_computation | async-start | bytes 524288 | tf_op jit(solution)/shard_map/all_to_all | solution.py:108
  116.7 41.8 %all-to-all-start.2 = ((bf16[8,128,2,256]{3,0,2,1:T(8,128)(2,1)}), bf16[8,128,2,256]{3,0,2,1:T(8,128)(2,1)}, u32[]{:S(2)}, u32[]{:S(2)}) async-start(bf16[8,128,2,256]{3,0,2,1:T(8,128)(2,1)} %reshape.225), calls=%async_computation.2 | async-start | bytes 2097152 | tf_op jit(solution)/shard_map/all_to_all | solution.py:107
  158.5 1.9 copy-start.1
  166.1 8.5 %copy-start.5 = (bf16[16,512]{1,0:T(8,128)(2,1)S(1)}, bf16[16,512]{1,0:T(8,128)(2,1)}, u32[]{:S(2)}) copy-start(bf16[16,512]{1,0:T(8,128)(2,1)} %convert_element_type.103) | copy-start | bytes 49156
  176.6 9.4 %copy-start.3 = (s32[542,512]{1,0:T(8,128)S(1)}, s32[542,512]{1,0:T(8,128)}, u32[]{:S(2)}) copy-start(s32[542,512]{1,0:T(8,128)} %iota_subtract_fusion) | copy-start | bytes 3330052
  176.6 9.4 %copy-start.7 = (bf16[2,31]{1,0:T(2,128)(2,1)S(1)}, bf16[2,31]{1,0:T(2,128)(2,1)}, u32[]{:S(2)}) copy-start(bf16[2,31]{1,0:T(2,128)(2,1)} %param.17) | copy-start | bytes 376
  181.6 12.2 %collective-permute-start = (bf16[2,1024,15]{1,2,0:T(8,128)(2,1)S(1)}, bf16[2,1024,15]{1,2,0:T(8,128)(2,1)S(1)}, u32[]{:S(2)}, u32[]{:S(2)}) collective-permute-start(bf16[2,1024,15]{1,2,0:T(8,128)(2,1)S(1)} %get-tuple-element.183), channel_id=1, source_target_pairs={{0,1},{2,3},{4,5},{6,7},{8,9},{10,11},{12,13},{14,15},{16,17},{18,... | collective-permute-start | bytes 184328 | tf_op jit(solution)/shard_map/ppermute | solution.py:21
  182.9 10.9 %copy-start.2 = (bf16[2,1024,512]{1,2,0:T(8,128)(2,1)S(1)}, bf16[2,1024,512]{1,2,0:T(8,128)(2,1)}, u32[]{:S(2)}) copy-start(bf16[2,1024,512]{1,2,0:T(8,128)(2,1)} %copy.59) | copy-start | bytes 6291460
  182.9 10.9 %collective-permute-start.1 = (bf16[2,1024,15]{1,2,0:T(8,128)(2,1)S(1)}, bf16[2,1024,15]{1,2,0:T(8,128)(2,1)S(1)}, u32[]{:S(2)}, u32[]{:S(2)}) collective-permute-start(bf16[2,1024,15]{1,2,0:T(8,128)(2,1)S(1)} %get-tuple-element.184), channel_id=1, source_target_pairs={{1,0},{3,2},{5,4},{7,6},{9,8},{11,10},{13,12},{15,14},{17,16},{19,... | collective-permute-start | bytes 184328 | tf_op jit(solution)/shard_map/ppermute | solution.py:22
where the time goes:
time: 198 us; the launch traced here: 197 us
  local copies, waits for them, and re-layouts  66.8 us (34%)
  matrix products  41 us (21%)
  starting transfers between devices  38.7 us (20%)
  waiting for transfers between devices  29.3 us (15%)
  blocking collectives  13.1 us (7%)
  other arithmetic  6.15 us (3%)
    dot_general x64, matrix products, one_block(): jnp.dot(table, onehot, preferred_element_type=jnp.float32)  27.5 us
    all_to_all x1, waiting for transfers between devices, shards(): lax.all_to_all(spectra, 'shot', split_axis=3, concat_axis=2, tiled=True)  21 us
    all_to_all x1, starting transfers between devices, shards(): lax.all_to_all(spectra, 'shot', split_axis=3, concat_axis=2, tiled=True)  14.3 us
    all_to_all x1, starting transfers between devices, shards(): lax.all_to_all(second, 'shot', split_axis=1, concat_axis=1, tiled=True)  13.6 us
    dynamic_slice x10, local copies, waits for them, and re-layouts, pick_each(): return lax.map(one_table, (tables, codes))  9.08 us
    all_to_all x1, waiting for transfers between devices, shards(): lax.all_to_all(second, 'shot', split_axis=1, concat_axis=1, tiled=True)  8.31 us
    dot_general x1, matrix products, shards(): jnp.einsum('sj,jut->sut', filters, tap_onehot, preferred_element_type=jnp...  7.66 us
    unnamed x1, blocking collectives  7.06 us
  transfers between devices with their start and end apart: 5, of which 2 were waited for; matrix products, arithmetic and copies ran while one was open for 45% of the time, Pallas kernels for 0%

commit v1 on v0

v1 whole, which is shorter than its diff:
```python
import math

import jax
import jax.numpy as jnp
from jax import lax
from jax.sharding import PartitionSpec as P

NT = 1024
NF = 8
KMAX = 32
TAPS = 31


def extended(shard, sides, width):
    for axis, dim in sides:
        devices, length = (lax.axis_size(axis), shard.shape[dim])
        up = [(i, (i + 1) % devices) for i in range(devices - 1)]
        down = [(j, i) for i, j in up]
        last = lax.slice_in_dim(shard, length - width, length, axis=dim)
        leading = lax.slice_in_dim(shard, 0, width, axis=dim)
        before = lax.ppermute(last, axis, up)
        after = lax.ppermute(leading, axis, down)
        shard = jnp.concatenate([before, shard, after], axis=dim)
    return shard


def fourier_rows(bin_rows, first_time, sample_count, period):
    sample_times = first_time + jnp.arange(sample_count, dtype=jnp.int32)
    phases = bin_rows[:, None] * sample_times[None, :] % period
    angles = phases.astype(jnp.float32) * (2.0 * math.pi / period)
    return (jnp.cos(angles), jnp.sin(angles))


def shards(traces, frequency_bins, aperture, lengths, filters):
    shot_dev, receivers, time_dev = traces.shape
    groups = lax.axis_size("shot")
    shots = shot_dev * groups
    receiver_dev = receivers // groups
    stride = receivers // shots
    freq_dev = lax.axis_size("freq")
    local_bins = NF // freq_dev
    start_time = lax.axis_index("freq") * time_dev
    half_taps = (TAPS - 1) // 2
    flat_traces = traces.reshape(shot_dev * receivers, time_dev)
    cosines, sines = fourier_rows(frequency_bins, start_time, time_dev, NT)
    basis_rows = (jnp.stack([cosines, -sines], axis=1) * NT ** (-0.5)).astype(jnp.bfloat16)
    basis_rows = basis_rows.reshape(NF * 2, time_dev)
    term = lax.dot_general(
        basis_rows, flat_traces, (((1,), (1,)), ((), ())), preferred_element_type=jnp.float32
    )
    spectra = lax.psum_scatter(
        term.reshape(NF, 2, shot_dev, receivers), "freq", scatter_dimension=0, tiled=True
    ).astype(jnp.bfloat16)
    rows = local_bins * 2 * shot_dev
    near = spectra.reshape(rows, groups, receiver_dev).transpose(1, 0, 2).reshape(groups, rows * receiver_dev)
    stations = spectra[:, :, :, ::stride].reshape(1, rows * shots)
    outgoing = jnp.concatenate([near, jnp.broadcast_to(stations, (groups, rows * shots))], axis=1)
    incoming = lax.all_to_all(outgoing, "shot", 0, 0, tiled=True)
    q_part = incoming[:, : rows * receiver_dev].reshape(groups, local_bins, 2, shot_dev, receiver_dev)
    q_part = q_part.transpose(1, 2, 0, 3, 4).reshape(local_bins, 2, shots, receiver_dev).astype(jnp.float32)
    p_part = incoming[:, rows * receiver_dev :].reshape(groups, local_bins, 2, shot_dev, shots)
    p_part = p_part.transpose(1, 2, 0, 3, 4).reshape(local_bins, 2, shots, shots).astype(jnp.float32)
    used = jnp.arange(KMAX, dtype=jnp.int32)[None, None, :] < lengths[:, :, None]
    codes = jnp.where(used, aperture, -1)
    counts = jnp.sum(
        (codes[:, :, :, None] == jnp.arange(shots, dtype=jnp.int32)[None, None, None, :]).astype(jnp.float32),
        axis=2,
    )
    pr, pi = p_part[:, 0][:, :, None, :], p_part[:, 1][:, :, None, :]
    qr = q_part[:, 0].transpose(0, 2, 1)[:, None, :, :]
    qi = q_part[:, 1].transpose(0, 2, 1)[:, None, :, :]
    weight = counts[None]
    real_part = jnp.sum(weight * (pr * qr - pi * qi), axis=-1)
    imag_part = jnp.sum(weight * (pr * qi + pi * qr), axis=-1)
    summed = jnp.stack([real_part, imag_part], axis=1)
    multiples_spectra = (summed * KMAX ** (-0.5)).astype(jnp.bfloat16)
    back = multiples_spectra.reshape(local_bins, 2, groups, shot_dev, receiver_dev).transpose(2, 0, 1, 3, 4)
    back = lax.all_to_all(back.reshape(groups, rows * receiver_dev), "shot", 0, 0, tiled=True)
    piece = back.reshape(groups, local_bins, 2, shot_dev, receiver_dev).transpose(1, 2, 3, 0, 4)
    piece = piece.reshape(local_bins, 2, shot_dev, receivers)
    piece = lax.all_gather(piece, "freq", axis=0, tiled=True)
    synthesis_rows = jnp.stack([cosines, -sines], axis=1).astype(jnp.bfloat16).reshape(NF * 2, time_dev)
    flat_piece = piece.reshape(NF * 2, shot_dev * receivers)
    synthesized = lax.dot_general(
        flat_piece, synthesis_rows, (((0,), (0,)), ((), ())), preferred_element_type=jnp.float32
    )
    predicted = synthesized.astype(jnp.bfloat16).reshape(shot_dev, receivers, time_dev)
    padded = extended(predicted, (("freq", 2),), half_taps)
    padded_width = time_dev + 2 * half_taps
    lag_table = (
        jnp.arange(time_dev, dtype=jnp.int32)[None, :]
        + 2 * half_taps
        - jnp.arange(padded_width, dtype=jnp.int32)[:, None]
    )
    tap_onehot = (lag_table[None] == jnp.arange(TAPS, dtype=jnp.int32)[:, None, None]).astype(
        jnp.bfloat16
    )
    toeplitz = jnp.einsum(
        "sj,jut->sut", filters, tap_onehot, preferred_element_type=jnp.float32
    ).astype(jnp.bfloat16)
    filtered = jnp.einsum("sru,sut->srt", padded, toeplitz, preferred_element_type=jnp.float32)
    return filtered.astype(jnp.bfloat16)


def solution(mesh):
    in_specs = (
        P("shot", None, "freq"),
        P(),
        P(None, "shot", None),
        P(None, "shot"),
        P("shot", None),
    )
    out_specs = P("shot", None, "freq")
    return jax.shard_map(shards, mesh=mesh, in_specs=in_specs, out_specs=out_specs, check_vma=False)
```

time: 198 us -> 144 us (0.73)
  other arithmetic: 6.15 us -> 34.7 us
  matrix products: 41 us -> 13.5 us
  local copies, waits for them, and re-layouts: 66.8 us -> 39.6 us
  starting transfers between devices: 38.7 us -> 24.6 us
  waiting for transfers between devices: 29.3 us -> 18.6 us
    dot_general x65 -> x1, matrix products: 29.5 us -> 2.05 us  [shards(): lax.dot_general(flat_piece, synthesis_rows, (((0,), (0,)), ((), ())), pre...]
    reduce_sum x1 -> x2, other arithmetic: 1.59 us -> 27.9 us  [the longest x1 20.6 us: shards(): jnp.sum((codes[:, :, :, None] == jnp.arange(shots, dtype=jnp.int32)[None,...]
    reshape x14 -> x3, local copies, waits for them, and re-layouts: 15.6 us -> 1.25 us  [the longest x2 0.74 us: shards(): spectra.reshape(rows, groups, receiver_dev).transpose(1, 0, 2)]
    all_to_all x3 -> x2, starting transfers between devices: 34.3 us -> 20.1 us  [the longest x1 13.8 us: shards(): incoming = lax.all_to_all(outgoing, 'shot', 0, 0, tiled=True)]
    all_to_all x3 -> x2, waiting for transfers between devices: 29.3 us -> 18.6 us  [the longest x1 10.4 us: shards(): lax.all_to_all(back.reshape(groups, rows * receiver_dev), 'shot', 0, 0, t...]
    dynamic_slice x74 -> x0, local copies, waits for them, and re-layouts: 9.74 us -> none  [the longest x10 9.08 us: pick_each(): return lax.map(one_table, (tables, codes))]
    dynamic_update_slice x10 -> x0, local copies, waits for them, and re-layouts: 7.04 us -> none  [pick_each(): return lax.map(one_table, (tables, codes))]
    unnamed x22, local copies, waits for them, and re-layouts: 3.33 us -> 8.99 us
  transfers between devices with their start and end apart: 5 -> 4, of which waited for: 2 -> 2; matrix products, arithmetic and copies ran while one was open for 45% -> 22% of each run, Pallas kernels for 0% -> 0%
where the time goes in v1:
time: 144 us
  local copies, waits for them, and re-layouts  39.6 us (28%)
  other arithmetic  34.7 us (24%)
  starting transfers between devices  24.6 us (17%)
  waiting for transfers between devices  18.6 us (13%)
  matrix products  13.5 us (9%)
  blocking collectives  11.6 us (8%)
    reduce_sum x1, other arithmetic, shards(): jnp.sum((codes[:, :, :, None] == jnp.arange(shots, dtype=jnp.int32)[None,...  20.6 us
    all_to_all x1, starting transfers between devices, shards(): incoming = lax.all_to_all(outgoing, 'shot', 0, 0, tiled=True)  13.8 us
    all_to_all x1, waiting for transfers between devices, shards(): lax.all_to_all(back.reshape(groups, rows * receiver_dev), 'shot', 0, 0, t...  10.4 us
    unnamed x22, local copies, waits for them, and re-layouts  8.99 us
    all_to_all x1, waiting for transfers between devices, shards(): incoming = lax.all_to_all(outgoing, 'shot', 0, 0, tiled=True)  8.19 us
    dot_general x1, matrix products, shards(): jnp.einsum('sj,jut->sut', filters, tap_onehot, preferred_element_type=jnp...  7.66 us
    reduce_sum x1, other arithmetic, shards(): real_part = jnp.sum(weight * (pr * qr - pi * qi), axis=-1)  7.28 us
    unnamed x1, blocking collectives  6.93 us
  transfers between devices with their start and end apart: 4, of which 2 were waited for; matrix products, arithmetic and copies ran while one was open for 22% of the time, Pallas kernels for 0%

profile of v1, /device:TPU:1, one launch (start us, length us, event | category | flops | bytes accessed | tf_op | source)
XLA Modules:
  0.0 143.6 jit_solution(789092980158617794)
XLA Ops:
  2.2 6.9 %all-reduce.2 = bf16[8,2,2,1024]{3,0,2,1:T(8,128)(2,1)S(1)} all-reduce(f32[8,2,2,1024]{3,0,2,1:T(8,128)S(1)} %fusion.8), channel_id=2, replica_groups=mesh['shot'=128,'freq'=2] {'freq'}, use_global_device_ids=true, to_apply=%region_1.2.clone | all-reduce | flops 32768 | bytes 196608
  12.6 2.1 %reduce = bf16[128,4224]{1,0:T(8,128)(2,1)} reduce(bf16[128,1,4224]{2,0,1:T(8,128)(2,1)S(1)} %maximum_bitcast_fusion, bf16[]{:T(256)} %broadcast.164), dimensions={1}, to_apply=%copy.83.reduce_sub_computation | reduce | bytes 2162690 | tf_op jit(solution)/shard_map/all_to_all | solution.py:58
  14.7 2.6 %reshape.234 = bf16[128,2,2112]{2,1,0:T(2,128)(2,1)} reshape(bf16[128,4224]{1,0:T(8,128)(2,1)} %reduce) | data formatting | bytes 2162688
  17.3 13.8 %all-to-all-start = ((bf16[128,2,2112]{2,1,0:T(2,128)(2,1)}), bf16[128,2,2112]{2,1,0:T(2,128)(2,1)S(1)}, u32[]{:S(2)}, u32[]{:S(2)}) async-start(bf16[128,2,2112]{2,1,0:T(2,128)(2,1)} %reshape.234), calls=%async_computation | async-start | bytes 2228224 | tf_op jit(solution)/shard_map/all_to_all | solution.py:58
  32.1 1.3 copy.78
  34.5 20.6 %convert_reduce_fusion = f32[256,8,256]{2,1,0:T(8,128)} fusion(s32[256,8,32]{2,1,0:T(8,128)} %copy.78), kind=kLoop, calls=%fused_computation | loop fusion | flops 49807360 | bytes 2359296 | tf_op jit(solution)/shard_map/reduce_sum | solution.py:65
  55.1 8.2 %all-to-all-done = bf16[128,2,2112]{2,1,0:T(2,128)(2,1)S(1)} async-done(((bf16[128,2,2112]{2,1,0:T(2,128)(2,1)}), bf16[128,2,2112]{2,1,0:T(2,128)(2,1)S(1)}, u32[]{:S(2)}, u32[]{:S(2)}) %all-to-all-start) | async-done | bytes 1081376 | tf_op jit(solution)/shard_map/all_to_all | solution.py:58
  63.3 3.5 %reshape.235 = bf16[128,1,4224]{2,1,0:T(2,128)(2,1)} reshape(bf16[128,2,2112]{2,1,0:T(2,128)(2,1)S(1)} %all-to-all-done) | data formatting | bytes 2162688
  66.9 5.1 %copy.84 = bf16[128,1,4224]{0,2,1:T(8,128)(2,1)S(1)} copy(bf16[128,1,4224]{2,1,0:T(2,128)(2,1)} %reshape.235) | data formatting | bytes 2162688 | tf_op jit(solution)/shard_map/all_to_all | solution.py:58
  74.3 2.3 %slice_bitcast_fusion.1 = (f32[4,8,256]{1,2,0:T(8,128)}, f32[4,8,256]{1,2,0:T(8,128)}) fusion(f32[4,2,256,8]{3,2,1,0:T(8,128)} %bitcast.64), kind=kLoop, calls=%fused_computation.26 | loop fusion | bytes 131072 | tf_op jit(solution)/shard_map/transpose | solution.py:70
  79.0 1.5 %convert_bitcast_fusion = f32[4,2,128,2,256]{2,4,3,1,0:T(8,128)} fusion(bf16[128,4,2,2,256]{0,4,3,2,1:T(8,128)(2,1)S(1)} %bitcast.63), kind=kLoop, calls=%fused_computation.14 | loop fusion | flops 524288 | bytes 3145728 | tf_op jit(solution)/shard_map/convert_element_type | solution.py:62
  80.6 4.1 %copy.85 = f32[4,2,128,2,256]{4,1,3,2,0:T(2,128)} copy(f32[4,2,128,2,256]{2,4,3,1,0:T(8,128)} %convert_bitcast_fusion) | data formatting | bytes 4194304 | tf_op jit(solution)/shard_map/convert_element_type | solution.py:62
  84.7 4.1 %fusion.31 = (f32[4,1,256,256]{3,1,2,0:T(1,128)S(1)}, f32[4,1,256,256]{3,1,2,0:T(1,128)S(1)}) fusion(f32[4,2,256,256]{3,1,2,0:T(2,128)} %bitcast.59), kind=kLoop, calls=%fused_computation.55 | loop fusion | bytes 4194304 | tf_op jit(solution)/shard_map/slice | solution.py:69
  89.0 1.4 copy-done.1
  90.4 7.3 %multiply_reduce_fusion.1 = (f32[4,256,8]{2,1,0:T(8,128)S(1)}, f32[4,256,8]{2,1,0:T(8,128)S(1)}) fusion(f32[4,8,256]{2,1,0:T(8,128)S(1)} %copy.88, f32[4,256,256]{2,1,0:T(8,128)S(1)} %get-tuple-element.15, f32[4,8,256]{2,1,0:T(8,128)S(1)} %copy.87, f32[4,256,256]{2,1,0:T(8,128)S(1)} %get-tuple-element.16, f32[256,8,256]{2,1,0:T(8,128)S(1)} %copy-done.1), kind=kLoop, calls=%fused_computation.6 | loop fusion | flops 20955136 | bytes 4325376 | tf_op jit(solution)/shard_map/reduce_sum | solution.py:73
  98.8 6.3 %all-to-all-start.1 = ((bf16[128,1,128]{2,1,0:T(2,128)(2,1)}), bf16[128,1,128]{2,1,0:T(2,128)(2,1)S(1)}, u32[]{:S(2)}, u32[]{:S(2)}) async-start(bf16[128,1,128]{2,1,0:T(2,128)(2,1)} %copy.91), calls=%async_computation.1 | async-start | bytes 131072 | tf_op jit(solution)/shard_map/all_to_all | solution.py:78
  105.2 10.4 %all-to-all-done.1 = bf16[128,1,128]{2,1,0:T(2,128)(2,1)S(1)} async-done(((bf16[128,1,128]{2,1,0:T(2,128)(2,1)}), bf16[128,1,128]{2,1,0:T(2,128)(2,1)S(1)}, u32[]{:S(2)}, u32[]{:S(2)}) %all-to-all-start.1) | async-done | bytes 32800 | tf_op jit(solution)/shard_map/all_to_all | solution.py:78
  116.5 4.7 %all_gather.3 = bf16[8,2,2,1024]{3,2,1,0:T(2,128)(2,1)S(1)} all-gather(bf16[4,2,2,1024]{3,2,1,0:T(2,128)(2,1)S(1)} %reshape.220), channel_id=1, replica_groups=mesh['shot'=128,'freq'=2] {'freq'}, dimensions={0}, use_global_device_ids=true | all-gather | bytes 98304 | tf_op jit(solution)/shard_map/all_gather | solution.py:81
  121.2 2.1 %convolution_convert_fusion = bf16[2048,512]{1,0:T(8,128)(2,1)} fusion(bf16[16,2048]{1,0:T(8,128)(2,1)S(1)} %bitcast.68, bf16[16,512]{1,0:T(8,128)(2,1)S(1)} %convert_element_type.93), kind=kOutput, calls=%fused_computation.7 | convolution fusion | flops 34603008 | bytes 2179072 | tf_op jit(solution)/shard_map/dot_general | solution.py:84
  123.3 4.1 %copy.95 = bf16[2,1024,512]{1,2,0:T(8,128)(2,1)} copy(bf16[2,1024,512]{2,1,0:T(8,128)(2,1)} %bitcast.60) | data formatting | bytes 4194304 | tf_op jit(solution)/shard_map/reshape | solution.py:87
  128.2 1.3 collective-permute-start
  129.5 3.2 %collective-permute-start.1 = (bf16[2,1024,15]{1,2,0:T(8,128)(2,1)S(1)}, bf16[2,1024,15]{1,2,0:T(8,128)(2,1)S(1)}, u32[]{:S(2)}, u32[]{:S(2)}) collective-permute-start(bf16[2,1024,15]{1,2,0:T(8,128)(2,1)S(1)} %get-tuple-element.8), channel_id=1, source_target_pairs={{1,0},{3,2},{5,4},{7,6},{9,8},{11,10},{13,12},{15,14},{17,16},{19,... | collective-permute-start | bytes 184328 | tf_op jit(solution)/shard_map/ppermute | solution.py:22
  132.7 7.7 %fusion.14 = bf16[2,542,512]{2,0,1:T(2,128)(2,1)S(1)} fusion(s32[542,512]{1,0:T(8,128)S(1)} %copy-done.4, bf16[2,31]{1,0:T(2,128)(2,1)S(1)} %copy-done.6), kind=kOutput, calls=%fused_computation.19 | convolution fusion | flops 43568128 | bytes 2220156 | tf_op jit(solution)/shard_map/sj,jut->sut/dot_general | solution.py:98
  140.4 3.2 %fusion.10 = bf16[2,1024,512]{2,1,0:T(8,128)(2,1)} fusion(bf16[2,1024,15]{1,2,0:T(8,128)(2,1)S(1)} %collective-permute-done.1, bf16[2,1024,512]{1,2,0:T(8,128)(2,1)S(1)} %copy-done.3, bf16[2,1024,15]{1,2,0:T(8,128)(2,1)S(1)} %collective-permute-done, bf16[2,542,512]{2,0,1:T(2,128)(2,1)S(1)} %fusion.14), kind=kOutput, calls=%fused_computation.17 | convolution fusion | flops 1144365056 | bytes 5427200 | tf_op jit(solution)/shard_map/sru,sut->srt/dot_general | solution.py:101
  (54 shorter events, 14.9 us)
Async XLA Ops:
  0.0 1.6 %copy-start = (bf16[2,1024,512]{2,1,0:T(8,128)(2,1)S(1)}, bf16[2,1024,512]{2,1,0:T(8,128)(2,1)}, u32[]{:S(2)}) copy-start(bf16[2,1024,512]{2,1,0:T(8,128)(2,1)} %param.5) | copy-start | bytes 6291460
  0.0 9.2 %copy-start.7 = (u32[256]{0:T(256)S(1)}, u32[256]{0:T(256)}, u32[]{:S(2)}) copy-start(u32[256]{0:T(256)} %constant.39) | copy-start | bytes 3076
  14.7 16.4 %copy-start.5 = (s32[256,8]{0,1:T(8,128)S(1)}, s32[256,8]{0,1:T(8,128)}, u32[]{:S(2)}) copy-start(s32[256,8]{0,1:T(8,128)} %param.8) | copy-start | bytes 24580
  17.3 46.0 %all-to-all-start = ((bf16[128,2,2112]{2,1,0:T(2,128)(2,1)}), bf16[128,2,2112]{2,1,0:T(2,128)(2,1)S(1)}, u32[]{:S(2)}, u32[]{:S(2)}) async-start(bf16[128,2,2112]{2,1,0:T(2,128)(2,1)} %reshape.234), calls=%async_computation | async-start | bytes 2228224 | tf_op jit(solution)/shard_map/all_to_all | solution.py:58
  73.1 6.0 %copy-start.2 = (bf16[128,4096]{0,1:T(8,128)(2,1)S(1)}, bf16[128,4096]{0,1:T(8,128)(2,1)}, u32[]{:S(2)}) copy-start(bf16[128,4096]{0,1:T(8,128)(2,1)} %slice.36) | copy-start | bytes 3145732
  88.8 1.6 %copy-start.1 = (f32[256,8,256]{2,1,0:T(8,128)S(1)}, f32[256,8,256]{2,1,0:T(8,128)}, u32[]{:S(2)}) copy-start(f32[256,8,256]{2,1,0:T(8,128)} %convert_reduce_fusion) | copy-start | bytes 6291460
  98.8 16.8 %all-to-all-start.1 = ((bf16[128,1,128]{2,1,0:T(2,128)(2,1)}), bf16[128,1,128]{2,1,0:T(2,128)(2,1)S(1)}, u32[]{:S(2)}, u32[]{:S(2)}) async-start(bf16[128,1,128]{2,1,0:T(2,128)(2,1)} %copy.91), calls=%async_computation.1 | async-start | bytes 131072 | tf_op jit(solution)/shard_map/all_to_all | solution.py:78
  123.3 9.4 %copy-start.4 = (s32[542,512]{1,0:T(8,128)S(1)}, s32[542,512]{1,0:T(8,128)}, u32[]{:S(2)}) copy-start(s32[542,512]{1,0:T(8,128)} %iota_subtract_fusion) | copy-start | bytes 3330052
  123.3 9.4 %copy-start.6 = (bf16[2,31]{1,0:T(2,128)(2,1)S(1)}, bf16[2,31]{1,0:T(2,128)(2,1)}, u32[]{:S(2)}) copy-start(bf16[2,31]{1,0:T(2,128)(2,1)} %param.9) | copy-start | bytes 376
  128.2 12.2 %collective-permute-start = (bf16[2,1024,15]{1,2,0:T(8,128)(2,1)S(1)}, bf16[2,1024,15]{1,2,0:T(8,128)(2,1)S(1)}, u32[]{:S(2)}, u32[]{:S(2)}) collective-permute-start(bf16[2,1024,15]{1,2,0:T(8,128)(2,1)S(1)} %get-tuple-element.7), channel_id=1, source_target_pairs={{0,1},{2,3},{4,5},{6,7},{8,9},{10,11},{12,13},{14,15},{16,17},{18,... | collective-permute-start | bytes 184328 | tf_op jit(solution)/shard_map/ppermute | solution.py:21
  129.5 10.9 %copy-start.3 = (bf16[2,1024,512]{1,2,0:T(8,128)(2,1)S(1)}, bf16[2,1024,512]{1,2,0:T(8,128)(2,1)}, u32[]{:S(2)}) copy-start(bf16[2,1024,512]{1,2,0:T(8,128)(2,1)} %copy.95) | copy-start | bytes 6291460
  129.5 10.9 %collective-permute-start.1 = (bf16[2,1024,15]{1,2,0:T(8,128)(2,1)S(1)}, bf16[2,1024,15]{1,2,0:T(8,128)(2,1)S(1)}, u32[]{:S(2)}, u32[]{:S(2)}) collective-permute-start(bf16[2,1024,15]{1,2,0:T(8,128)(2,1)S(1)} %get-tuple-element.8), channel_id=1, source_target_pairs={{1,0},{3,2},{5,4},{7,6},{9,8},{11,10},{13,12},{15,14},{17,16},{19,... | collective-permute-start | bytes 184328 | tf_op jit(solution)/shard_map/ppermute | solution.py:22

commit v2 on v1

--- a/solution.py
+++ b/solution.py
@@ -57,48 +57,46 @@
     outgoing = jnp.concatenate([near, jnp.broadcast_to(stations, (groups, rows * shots))], axis=1)
     incoming = lax.all_to_all(outgoing, "shot", 0, 0, tiled=True)
     q_part = incoming[:, : rows * receiver_dev].reshape(groups, local_bins, 2, shot_dev, receiver_dev)
-    q_part = q_part.transpose(1, 2, 0, 3, 4).reshape(local_bins, 2, shots, receiver_dev).astype(jnp.float32)
-    p_part = incoming[:, rows * receiver_dev :].reshape(groups, local_bins, 2, shot_dev, shots)
-    p_part = p_part.transpose(1, 2, 0, 3, 4).reshape(local_bins, 2, shots, shots).astype(jnp.float32)
+    q_t = q_part.transpose(1, 2, 4, 0, 3).reshape(local_bins, 2, receiver_dev, shots).astype(jnp.float32)
+    p_in = incoming[:, rows * receiver_dev :].reshape(groups, local_bins, 2, shot_dev, shots)
     used = jnp.arange(KMAX, dtype=jnp.int32)[None, None, :] < lengths[:, :, None]
     codes = jnp.where(used, aperture, -1)
     counts = jnp.sum(
         (codes[:, :, :, None] == jnp.arange(shots, dtype=jnp.int32)[None, None, None, :]).astype(jnp.float32),
         axis=2,
     )
-    pr, pi = p_part[:, 0][:, :, None, :], p_part[:, 1][:, :, None, :]
-    qr = q_part[:, 0].transpose(0, 2, 1)[:, None, :, :]
-    qi = q_part[:, 1].transpose(0, 2, 1)[:, None, :, :]
-    weight = counts[None]
+    weight = counts.reshape(groups, 1, shot_dev, receiver_dev, shots)
+    pr = p_in[:, :, 0, :, None, :].astype(jnp.float32)
+    pi = p_in[:, :, 1, :, None, :].astype(jnp.float32)
+    qr = q_t[None, :, 0, None, :, :]
+    qi = q_t[None, :, 1, None, :, :]
     real_part = jnp.sum(weight * (pr * qr - pi * qi), axis=-1)
     imag_part = jnp.sum(weight * (pr * qi + pi * qr), axis=-1)
-    summed = jnp.stack([real_part, imag_part], axis=1)
+    summed = jnp.stack([real_part, imag_part], axis=2)
     multiples_spectra = (summed * KMAX ** (-0.5)).astype(jnp.bfloat16)
-    back = multiples_spectra.reshape(local_bins, 2, groups, shot_dev, receiver_dev).transpose(2, 0, 1, 3, 4)
-    back = lax.all_to_all(back.reshape(groups, rows * receiver_dev), "shot", 0, 0, tiled=True)
-    piece = back.reshape(groups, local_bins, 2, shot_dev, receiver_dev).transpose(1, 2, 3, 0, 4)
-    piece = piece.reshape(local_bins, 2, shot_dev, receivers)
-    piece = lax.all_gather(piece, "freq", axis=0, tiled=True)
-    synthesis_rows = jnp.stack([cosines, -sines], axis=1).astype(jnp.bfloat16).reshape(NF * 2, time_dev)
-    flat_piece = piece.reshape(NF * 2, shot_dev * receivers)
-    synthesized = lax.dot_general(
-        flat_piece, synthesis_rows, (((0,), (0,)), ((), ())), preferred_element_type=jnp.float32
+    back = lax.all_to_all(multiples_spectra.reshape(groups, rows * receiver_dev), "shot", 0, 0, tiled=True)
+    piece = lax.all_gather(back, "freq", axis=0, tiled=False)
+    piece = piece.reshape(freq_dev, groups, local_bins, 2, shot_dev, receiver_dev)
+    piece = piece.transpose(4, 1, 5, 0, 2, 3).reshape(shot_dev, receivers, NF * 2)
+    wide = time_dev + 2 * half_taps
+    wide_times = start_time - half_taps + jnp.arange(wide, dtype=jnp.int32)
+    inside = (wide_times >= 0) & (wide_times < NT)
+    phases = frequency_bins[:, None] * jnp.clip(wide_times, 0, NT - 1)[None, :] % NT
+    angles = phases.astype(jnp.float32) * (2.0 * math.pi / NT)
+    wide_rows = jnp.stack([jnp.cos(angles), -jnp.sin(angles)], axis=1).astype(jnp.bfloat16)
+    wide_rows = jnp.where(inside[None, None, :], wide_rows.astype(jnp.float32), 0.0).reshape(NF * 2, wide)
+    taps = filters.astype(jnp.float32)
+    shaped = sum(
+        taps[:, tap, None, None] * wide_rows[None, :, 2 * half_taps - tap : 2 * half_taps - tap + time_dev]
+        for tap in range(TAPS)
     )
-    predicted = synthesized.astype(jnp.bfloat16).reshape(shot_dev, receivers, time_dev)
-    padded = extended(predicted, (("freq", 2),), half_taps)
-    padded_width = time_dev + 2 * half_taps
-    lag_table = (
-        jnp.arange(time_dev, dtype=jnp.int32)[None, :]
-        + 2 * half_taps
-        - jnp.arange(padded_width, dtype=jnp.int32)[:, None]
+    filtered = lax.dot_general(
+        piece.astype(jnp.float32),
+        shaped,
+        (((2,), (1,)), ((0,), (0,))),
+        precision=lax.Precision.HIGHEST,
+        preferred_element_type=jnp.float32,
     )
-    tap_onehot = (lag_table[None] == jnp.arange(TAPS, dtype=jnp.int32)[:, None, None]).astype(
-        jnp.bfloat16
-    )
-    toeplitz = jnp.einsum(
-        "sj,jut->sut", filters, tap_onehot, preferred_element_type=jnp.float32
-    ).astype(jnp.bfloat16)
-    filtered = jnp.einsum("sru,sut->srt", padded, toeplitz, preferred_element_type=jnp.float32)
     return filtered.astype(jnp.bfloat16)
 
 

time: 144 us -> 119 us (0.83)
  matrix products: 13.5 us -> 5.18 us
  local copies, waits for them, and re-layouts: 39.6 us -> 31.6 us
  starting transfers between devices: 24.6 us -> 20.2 us
  other arithmetic: 34.7 us -> 31.5 us
  waiting for transfers between devices: 18.6 us -> 16.8 us
    dot_general x3 -> x1, matrix products: 12.9 us -> 4.54 us  [shards(): lax.dot_general(piece.astype(jnp.float32), shaped, (((2,), (1,)), ((0,),...]
    transpose x4 -> x1, local copies, waits for them, and re-layouts: 5 us -> 0.48 us  [shards(): piece.transpose(4, 1, 5, 0, 2, 3).reshape(shot_dev, receivers, NF * 2)]
    ppermute x2 -> x0, starting transfers between devices: 4.46 us -> none  [the longest x1 3.16 us: extended(): after = lax.ppermute(leading, axis, down)]
    mul x0 -> x3, local copies, waits for them, and re-layouts: none -> 3.47 us  [shards(): real_part = jnp.sum(weight * (pr * qr - pi * qi), axis=-1)]
    reshape x2, local copies, waits for them, and re-layouts: 4.56 us -> 1.49 us  [the longest x1 1.47 us: shards(): piece.transpose(4, 1, 5, 0, 2, 3).reshape(shot_dev, receivers, NF * 2)]
    reduce_sum x1, other arithmetic: 7.28 us -> 5.62 us  [shards(): real_part = jnp.sum(weight * (pr * qr - pi * qi), axis=-1)]
    unnamed x22 -> x18, local copies, waits for them, and re-layouts: 8.99 us -> 7.42 us
    slice x2 -> x4, local copies, waits for them, and re-layouts: 5 us -> 3.77 us  [the longest x2 2 us: shards(): taps[:, tap, None, None]]
  transfers between devices with their start and end apart: 4 -> 2, of which waited for: 2 -> 2; matrix products, arithmetic and copies ran while one was open for 22% -> 22% of each run, Pallas kernels for 0% -> 0%
where the time goes in v2:
time: 119 us; the launch traced here: 118 us
  local copies, waits for them, and re-layouts  31.6 us (27%)
  other arithmetic  31.5 us (26%)
  starting transfers between devices  20.2 us (17%)
  waiting for transfers between devices  16.8 us (14%)
  blocking collectives  11.6 us (10%)
  matrix products  5.18 us (4%)
    reduce_sum x1, other arithmetic, shards(): jnp.sum((codes[:, :, :, None] == jnp.arange(shots, dtype=jnp.int32)[None,...  19.5 us
    all_to_all x1, starting transfers between devices, shards(): incoming = lax.all_to_all(outgoing, 'shot', 0, 0, tiled=True)  13.9 us
    all_to_all x1, waiting for transfers between devices, shards(): lax.all_to_all(multiples_spectra.reshape(groups, rows * receiver_dev), 's...  9.53 us
    unnamed x18, local copies, waits for them, and re-layouts  7.42 us
    all_to_all x1, waiting for transfers between devices, shards(): incoming = lax.all_to_all(outgoing, 'shot', 0, 0, tiled=True)  7.28 us
    unnamed x1, blocking collectives  6.93 us
    all_to_all x1, starting transfers between devices, shards(): lax.all_to_all(multiples_spectra.reshape(groups, rows * receiver_dev), 's...  6.33 us
    all_to_all x2, local copies, waits for them, and re-layouts, shards(): incoming = lax.all_to_all(outgoing, 'shot', 0, 0, tiled=True)  5.74 us
  transfers between devices with their start and end apart: 2, of which 2 were waited for; matrix products, arithmetic and copies ran while one was open for 22% of the time, Pallas kernels for 0%

profile of v2, /device:TPU:1, one launch (start us, length us, event | category | flops | bytes accessed | tf_op | source)
XLA Modules:
  0.0 118.0 jit_solution(16383866249274665436)
XLA Ops:
  2.2 6.9 %all-reduce.2 = bf16[8,2,2,1024]{3,0,2,1:T(8,128)(2,1)S(1)} all-reduce(f32[8,2,2,1024]{3,0,2,1:T(8,128)S(1)} %fusion), channel_id=3, replica_groups=mesh['shot'=128,'freq'=2] {'freq'}, use_global_device_ids=true, to_apply=%region_1.2.clone | all-reduce | flops 32768 | bytes 196608
  12.7 2.1 %reduce.62 = bf16[128,4224]{1,0:T(8,128)(2,1)} reduce(bf16[128,1,4224]{2,0,1:T(8,128)(2,1)S(1)} %maximum_bitcast_fusion, bf16[]{:T(256)} %broadcast.372), dimensions={1}, to_apply=%copy.120.reduce_sub_computation | reduce | bytes 2162690 | tf_op jit(solution)/shard_map/all_to_all | solution.py:58
  14.8 2.6 %reshape.449 = bf16[128,2,2112]{2,1,0:T(2,128)(2,1)} reshape(bf16[128,4224]{1,0:T(8,128)(2,1)} %reduce.62) | data formatting | bytes 2162688
  17.4 13.9 %all-to-all-start = ((bf16[128,2,2112]{2,1,0:T(2,128)(2,1)}), bf16[128,2,2112]{2,1,0:T(2,128)(2,1)S(1)}, u32[]{:S(2)}, u32[]{:S(2)}) async-start(bf16[128,2,2112]{2,1,0:T(2,128)(2,1)} %reshape.449), calls=%async_computation | async-start | bytes 2228224 | tf_op jit(solution)/shard_map/all_to_all | solution.py:58
  31.4 1.0 fusion.4
  32.5 1.3 %copy.115 = s32[256,8,32]{2,1,0:T(8,128)} copy(s32[256,8,32]{0,2,1:T(8,128)S(1)} %fusion.4) | data formatting | bytes 524288 | tf_op jit(solution)/shard_map/jit(_where)/select_n | solution.py:63
  34.0 1.1 slice_reduce_fusion.30
  35.8 1.0 fusion.146
  36.8 19.5 %convert_reduce_fusion = f32[256,8,256]{2,1,0:T(8,128)} fusion(s32[256,8,32]{2,1,0:T(8,128)S(1)} %copy-done.1), kind=kLoop, calls=%fused_computation | loop fusion | flops 49807360 | bytes 2359296 | tf_op jit(solution)/shard_map/reduce_sum | solution.py:64
  56.3 7.3 %all-to-all-done = bf16[128,2,2112]{2,1,0:T(2,128)(2,1)S(1)} async-done(((bf16[128,2,2112]{2,1,0:T(2,128)(2,1)}), bf16[128,2,2112]{2,1,0:T(2,128)(2,1)S(1)}, u32[]{:S(2)}, u32[]{:S(2)}) %all-to-all-start) | async-done | bytes 1081376 | tf_op jit(solution)/shard_map/all_to_all | solution.py:58
  63.6 3.6 %reshape.450 = bf16[128,1,4224]{2,1,0:T(2,128)(2,1)} reshape(bf16[128,2,2112]{2,1,0:T(2,128)(2,1)S(1)} %all-to-all-done) | data formatting | bytes 2162688
  67.2 5.1 %copy.121 = bf16[128,1,4224]{0,2,1:T(8,128)(2,1)S(1)} copy(bf16[128,1,4224]{2,1,0:T(2,128)(2,1)} %reshape.450) | data formatting | bytes 2162688 | tf_op jit(solution)/shard_map/all_to_all | solution.py:58
  73.0 1.2 %fusion.3 = (f32[128,4,2,256]{0,3,2,1:T(8,128)}, f32[128,4,2,256]{0,3,2,1:T(8,128)S(1)}) fusion(bf16[128,4,2,2,256]{0,4,3,2,1:T(8,128)(2,1)S(1)} %bitcast.51), kind=kLoop, calls=%fused_computation.13 | loop fusion | flops 524288 | bytes 3145728 | tf_op jit(solution)/shard_map/convert_element_type | solution.py:69
  74.2 2.3 %copy.122 = f32[128,4,2,256]{3,2,1,0:T(2,128)} copy(f32[128,4,2,256]{0,3,2,1:T(8,128)} %get-tuple-element.38) | data formatting | bytes 2097152 | tf_op jit(solution)/shard_map/convert_element_type | solution.py:69
  76.6 1.3 %copy.125 = f32[128,4,2,256]{3,2,1,0:T(2,128)} copy(f32[128,4,2,256]{0,3,2,1:T(8,128)S(1)} %get-tuple-element.39) | data formatting | bytes 2097152 | tf_op jit(solution)/shard_map/convert_element_type | solution.py:70
  79.2 1.1 slice_bitcast_fusion.2
  80.2 1.2 %copy.124 = f32[4,8,256]{2,1,0:T(8,128)S(1)} copy(f32[4,8,256]{1,2,0:T(8,128)} %get-tuple-element.40) | data formatting | bytes 65536 | tf_op jit(solution)/shard_map/mul | solution.py:73
  81.4 1.2 %copy.126 = f32[4,8,256]{2,1,0:T(8,128)S(1)} copy(f32[4,8,256]{1,2,0:T(8,128)} %get-tuple-element.41) | data formatting | bytes 65536 | tf_op jit(solution)/shard_map/mul | solution.py:73
  82.6 5.6 %multiply_reduce_fusion.1 = (f32[128,4,2,8]{3,2,1,0:T(2,128)S(1)}, f32[128,4,2,8]{3,2,1,0:T(2,128)S(1)}) fusion(f32[4,8,256]{2,1,0:T(8,128)S(1)} %copy.126, f32[128,4,2,256]{3,2,1,0:T(2,128)} %copy.125, f32[4,8,256]{2,1,0:T(8,128)S(1)} %copy.124, f32[128,4,2,256]{3,2,1,0:T(2,128)} %copy.122, f32[128,2,8,256]{3,2,1,0:T(8,128)} %bitcast.48), kind=kLoop, calls=%fused_computation.3 | loop fusion | flops 20955136 | bytes 4325376 | tf_op jit(solution)/shard_map/reduce_sum | solution.py:73
  89.7 6.3 %all-to-all-start.1 = ((bf16[128,1,128]{2,1,0:T(2,128)(2,1)}), bf16[128,1,128]{2,1,0:T(2,128)(2,1)S(1)}, u32[]{:S(2)}, u32[]{:S(2)}) async-start(bf16[128,1,128]{2,1,0:T(2,128)(2,1)} %copy.129), calls=%async_computation.1 | async-start | bytes 131072 | tf_op jit(solution)/shard_map/all_to_all | solution.py:77
  97.0 9.5 %all-to-all-done.1 = bf16[128,1,128]{2,1,0:T(2,128)(2,1)S(1)} async-done(((bf16[128,1,128]{2,1,0:T(2,128)(2,1)}), bf16[128,1,128]{2,1,0:T(2,128)(2,1)S(1)}, u32[]{:S(2)}, u32[]{:S(2)}) %all-to-all-start.1) | async-done | bytes 32800 | tf_op jit(solution)/shard_map/all_to_all | solution.py:77
  106.5 4.7 %all-gather = bf16[256,1,128]{2,0,1:T(8,128)(2,1)S(1)} all-gather(bf16[128,1,128]{2,0,1:T(8,128)(2,1)S(1)} %copy.130), channel_id=2, replica_groups=mesh['shot'=128,'freq'=2] {'freq'}, dimensions={0}, use_global_device_ids=true | all-gather | bytes 98304 | tf_op jit(solution)/shard_map/all_gather | solution.py:78
  111.8 1.5 %reshape.404 = bf16[2,1024,16]{1,2,0:T(8,128)(2,1)S(1)} reshape(bf16[2,128,8,2,4,2]{2,1,5,4,3,0:T(8,128)(2,1)S(1)} %copy.132) | data formatting | bytes 131072 | tf_op jit(solution)/shard_map/reshape | solution.py:80
  113.3 4.5 %convolution_convert_fusion = bf16[2,1024,512]{2,1,0:T(8,128)(2,1)} fusion(bf16[2,1024,16]{1,2,0:T(8,128)(2,1)S(1)} %reshape.404, f32[16,512]{1,0:T(8,128)} %get-tuple-element.43, f32[2]{0:T(128)S(1)} %get-tuple-element.8, f32[16,512]{1,0:T(8,128)} %get-tuple-element.44, f32[2]{0:T(128)S(1)} %get-tuple-element.9, f32[16,512]{1,0:T(8,128)} %get-tuple-element.45, ...), kind=kOutput, calls=%fused_computation.6 | convolution fusion | flops 203374592 | bytes 3178744 | tf_op jit(solution)/shard_map/dot_general | solution.py:93
  (51 shorter events, 11.0 us)
Async XLA Ops:
  0.0 1.6 %copy-start = (bf16[2,1024,512]{2,1,0:T(8,128)(2,1)S(1)}, bf16[2,1024,512]{2,1,0:T(8,128)(2,1)}, u32[]{:S(2)}) copy-start(bf16[2,1024,512]{2,1,0:T(8,128)(2,1)} %param.5) | copy-start | bytes 6291460
  0.0 9.2 %copy-start.6 = (u32[256]{0:T(256)S(1)}, u32[256]{0:T(256)}, u32[]{:S(2)}) copy-start(u32[256]{0:T(256)} %constant.53) | copy-start | bytes 3076
  14.8 16.5 %copy-start.2 = (s32[256,8]{0,1:T(8,128)S(1)}, s32[256,8]{0,1:T(8,128)}, u32[]{:S(2)}) copy-start(s32[256,8]{0,1:T(8,128)} %param.8) | copy-start | bytes 24580
  14.8 17.5 %copy-start.3 = (s32[8]{0:T(128)S(1)}, s32[8]{0:T(128)}, u32[]{:S(2)}) copy-start(s32[8]{0:T(128)} %param.6) | copy-start | bytes 100
  17.4 16.5 %copy-start.5 = (bf16[2,31]{1,0:T(2,128)(2,1)S(1)}, bf16[2,31]{1,0:T(2,128)(2,1)}, u32[]{:S(2)}) copy-start(bf16[2,31]{1,0:T(2,128)(2,1)} %param.9) | copy-start | bytes 376
  17.4 46.2 %all-to-all-start = ((bf16[128,2,2112]{2,1,0:T(2,128)(2,1)}), bf16[128,2,2112]{2,1,0:T(2,128)(2,1)S(1)}, u32[]{:S(2)}, u32[]{:S(2)}) async-start(bf16[128,2,2112]{2,1,0:T(2,128)(2,1)} %reshape.449), calls=%async_computation | async-start | bytes 2228224 | tf_op jit(solution)/shard_map/all_to_all | solution.py:58
  33.9 2.9 %copy-start.1 = (s32[256,8,32]{2,1,0:T(8,128)S(1)}, s32[256,8,32]{2,1,0:T(8,128)}, u32[]{:S(2)}) copy-start(s32[256,8,32]{2,1,0:T(8,128)} %copy.115) | copy-start | bytes 786436
  89.7 16.8 %all-to-all-start.1 = ((bf16[128,1,128]{2,1,0:T(2,128)(2,1)}), bf16[128,1,128]{2,1,0:T(2,128)(2,1)S(1)}, u32[]{:S(2)}, u32[]{:S(2)}) async-start(bf16[128,1,128]{2,1,0:T(2,128)(2,1)} %copy.129), calls=%async_computation.1 | async-start | bytes 131072 | tf_op jit(solution)/shard_map/all_to_all | solution.py:77
  97.0 16.3 %copy-start.4 = (f32[2]{0:T(128)S(1)}, f32[2]{0:T(128)}, u32[]{:S(2)}) copy-start(f32[2]{0:T(128)} %get-tuple-element.26) | copy-start | bytes 28

commit v3 on v2

--- a/solution.py
+++ b/solution.py
@@ -1,8 +1,11 @@
+import functools
 import math
 
 import jax
 import jax.numpy as jnp
 from jax import lax
+from jax.experimental import pallas as pl
+from jax.experimental.pallas import tpu as pltpu
 from jax.sharding import PartitionSpec as P
 
 NT = 1024
@@ -31,6 +34,40 @@
     return (jnp.cos(angles), jnp.sin(angles))
 
 
+def multiply_kernel(incoming_ref, counts_ref, out_ref, acc_ref, *, local_bins, shot_dev, receiver_dev, groups):
+    near = local_bins * 2 * shot_dev * receiver_dev
+    q_t = incoming_ref[:, 0:near].astype(jnp.float32).T
+    width = shot_dev * groups
+
+    def q_row(f, c, i, r):
+        row = ((f * 2 + c) * shot_dev + i) * receiver_dev + r
+        return q_t[row : row + 1, :]
+
+    for i in range(shot_dev):
+        for r in range(receiver_dev):
+            weights = [counts_ref[i, r, :, h * groups : (h + 1) * groups] for h in range(shot_dev)]
+            for f in range(local_bins):
+                real_sum = None
+                imag_sum = None
+                for h in range(shot_dev):
+                    base_r = near + ((f * 2 + 0) * shot_dev + i) * width + h * groups
+                    base_i = near + ((f * 2 + 1) * shot_dev + i) * width + h * groups
+                    pr = incoming_ref[:, base_r : base_r + groups].astype(jnp.float32)
+                    pi = incoming_ref[:, base_i : base_i + groups].astype(jnp.float32)
+                    qr = q_row(f, 0, h, r)
+                    qi = q_row(f, 1, h, r)
+                    w = weights[h]
+                    real_term = w * (pr * qr - pi * qi)
+                    imag_term = w * (pr * qi + pi * qr)
+                    real_sum = real_term if real_sum is None else real_sum + real_term
+                    imag_sum = imag_term if imag_sum is None else imag_sum + imag_term
+                col_r = ((f * 2 + 0) * shot_dev + i) * receiver_dev + r
+                col_i = ((f * 2 + 1) * shot_dev + i) * receiver_dev + r
+                acc_ref[:, col_r : col_r + 1] = jnp.sum(real_sum, axis=1, keepdims=True)
+                acc_ref[:, col_i : col_i + 1] = jnp.sum(imag_sum, axis=1, keepdims=True)
+    out_ref[...] = (acc_ref[...] * KMAX ** (-0.5)).astype(out_ref.dtype)
+
+
 def shards(traces, frequency_bins, aperture, lengths, filters):
     shot_dev, receivers, time_dev = traces.shape
     groups = lax.axis_size("shot")
@@ -53,27 +90,30 @@
     ).astype(jnp.bfloat16)
     rows = local_bins * 2 * shot_dev
     near = spectra.reshape(rows, groups, receiver_dev).transpose(1, 0, 2).reshape(groups, rows * receiver_dev)
-    stations = spectra[:, :, :, ::stride].reshape(1, rows * shots)
+    stations = jnp.concatenate(
+        [spectra[:, :, :, 0 :: 2 * stride], spectra[:, :, :, stride :: 2 * stride]], axis=-1
+    ).reshape(1, rows * shots)
     outgoing = jnp.concatenate([near, jnp.broadcast_to(stations, (groups, rows * shots))], axis=1)
     incoming = lax.all_to_all(outgoing, "shot", 0, 0, tiled=True)
-    q_part = incoming[:, : rows * receiver_dev].reshape(groups, local_bins, 2, shot_dev, receiver_dev)
-    q_t = q_part.transpose(1, 2, 4, 0, 3).reshape(local_bins, 2, receiver_dev, shots).astype(jnp.float32)
-    p_in = incoming[:, rows * receiver_dev :].reshape(groups, local_bins, 2, shot_dev, shots)
     used = jnp.arange(KMAX, dtype=jnp.int32)[None, None, :] < lengths[:, :, None]
-    codes = jnp.where(used, aperture, -1)
+    codes = jnp.where(used, (aperture % shot_dev) * groups + aperture // shot_dev, -1)
+    codes = codes.reshape(groups, shot_dev, receiver_dev, KMAX).transpose(1, 2, 0, 3)
     counts = jnp.sum(
-        (codes[:, :, :, None] == jnp.arange(shots, dtype=jnp.int32)[None, None, None, :]).astype(jnp.float32),
-        axis=2,
+        (codes[..., None] == jnp.arange(shots, dtype=jnp.int32)).astype(jnp.float32), axis=3
     )
-    weight = counts.reshape(groups, 1, shot_dev, receiver_dev, shots)
-    pr = p_in[:, :, 0, :, None, :].astype(jnp.float32)
-    pi = p_in[:, :, 1, :, None, :].astype(jnp.float32)
-    qr = q_t[None, :, 0, None, :, :]
-    qi = q_t[None, :, 1, None, :, :]
-    real_part = jnp.sum(weight * (pr * qr - pi * qi), axis=-1)
-    imag_part = jnp.sum(weight * (pr * qi + pi * qr), axis=-1)
-    summed = jnp.stack([real_part, imag_part], axis=2)
-    multiples_spectra = (summed * KMAX ** (-0.5)).astype(jnp.bfloat16)
+    kernel = functools.partial(
+        multiply_kernel, local_bins=local_bins, shot_dev=shot_dev, receiver_dev=receiver_dev, groups=groups
+    )
+    multiples_spectra = pl.pallas_call(
+        kernel,
+        out_shape=jax.ShapeDtypeStruct((groups, rows * receiver_dev), jnp.bfloat16),
+        in_specs=[pl.BlockSpec(memory_space=pltpu.VMEM)] * 2,
+        out_specs=pl.BlockSpec(memory_space=pltpu.VMEM),
+        scratch_shapes=[pltpu.VMEM((groups, rows * receiver_dev), jnp.float32)],
+        cost_estimate=pl.CostEstimate(
+            flops=16 * groups * shots * rows * receiver_dev // 2, transcendentals=0, bytes_accessed=4 * 1024 * 1024
+        ),
+    )(incoming, counts)
     back = lax.all_to_all(multiples_spectra.reshape(groups, rows * receiver_dev), "shot", 0, 0, tiled=True)
     piece = lax.all_gather(back, "freq", axis=0, tiled=False)
     piece = piece.reshape(freq_dev, groups, local_bins, 2, shot_dev, receiver_dev)

time: 119 us -> 107 us (0.90)
  other arithmetic: 31.5 us -> 19.3 us
  local copies, waits for them, and re-layouts: 31.6 us -> 23.9 us
  Pallas kernels: 0 us -> 6.27 us
  waiting for transfers between devices: 16.8 us -> 18.8 us
    reduce_sum x2 -> x1, other arithmetic: 25.1 us -> 14.7 us  [shards(): jnp.sum((codes[..., None] == jnp.arange(shots, dtype=jnp.int32)).astype(j...]
    pallas_call x0 -> x1, Pallas kernels: none -> 6.27 us  [shards(): pl.pallas_call(kernel, out_shape=jax.ShapeDtypeStruct((groups, rows * rec...]
    all_to_all x2 -> x1, local copies, waits for them, and re-layouts: 5.74 us -> 0.59 us  [shards(): incoming = lax.all_to_all(outgoing, 'shot', 0, 0, tiled=True)]
    convert_element_type x4 -> x0, local copies, waits for them, and re-layouts: 4.91 us -> none  [the longest x1 2.31 us: shards(): pr = p_in[:, :, 0, :, None, :].astype(jnp.float32)]
    mul x3 -> x0, local copies, waits for them, and re-layouts: 3.47 us -> none  [shards(): real_part = jnp.sum(weight * (pr * qr - pi * qi), axis=-1)]
    unnamed x18 -> x19, local copies, waits for them, and re-layouts: 7.42 us -> 10.1 us
    transpose x0 -> x1, local copies, waits for them, and re-layouts: none -> 2.58 us  [shards(): codes.reshape(groups, shot_dev, receiver_dev, KMAX).transpose(1, 2, 0, 3)]
    all_to_all x1, waiting for transfers between devices: 7.28 us -> 9.31 us  [shards(): incoming = lax.all_to_all(outgoing, 'shot', 0, 0, tiled=True)]
where the time goes in v3:
time: 107 us; the launch traced here: 106 us
  local copies, waits for them, and re-layouts  23.9 us (22%)
  starting transfers between devices  20.1 us (19%)
  other arithmetic  19.3 us (18%)
  waiting for transfers between devices  18.8 us (18%)
  blocking collectives  11.6 us (11%)
  Pallas kernels  6.27 us (6%)
  matrix products  5.18 us (5%)
    reduce_sum x1, other arithmetic, shards(): jnp.sum((codes[..., None] == jnp.arange(shots, dtype=jnp.int32)).astype(j...  14.7 us
    all_to_all x1, starting transfers between devices, shards(): incoming = lax.all_to_all(outgoing, 'shot', 0, 0, tiled=True)  13.8 us
    unnamed x19, local copies, waits for them, and re-layouts  10.1 us
    all_to_all x1, waiting for transfers between devices, shards(): lax.all_to_all(multiples_spectra.reshape(groups, rows * receiver_dev), 's...  9.53 us
    all_to_all x1, waiting for transfers between devices, shards(): incoming = lax.all_to_all(outgoing, 'shot', 0, 0, tiled=True)  9.31 us
    unnamed x1, blocking collectives  6.93 us
    all_to_all x1, starting transfers between devices, shards(): lax.all_to_all(multiples_spectra.reshape(groups, rows * receiver_dev), 's...  6.33 us
    pallas_call x1, Pallas kernels, shards(): pl.pallas_call(kernel, out_shape=jax.ShapeDtypeStruct((groups, rows * rec...  6.27 us
  transfers between devices with their start and end apart: 2, of which 2 were waited for; matrix products, arithmetic and copies ran while one was open for 22% of the time, Pallas kernels for 0%

profile of v3, /device:TPU:1, one launch (start us, length us, event | category | flops | bytes accessed | tf_op | source)
XLA Modules:
  0.0 106.3 jit_solution(16297205526906678932)
XLA Ops:
  0.0 1.0 fusion.142
  1.6 0.6 fusion
  2.2 6.9 %all-reduce.2 = bf16[8,2,2,1024]{3,0,2,1:T(8,128)(2,1)S(1)} all-reduce(f32[8,2,2,1024]{3,0,2,1:T(8,128)S(1)} %fusion), channel_id=3, replica_groups=mesh['shot'=128,'freq'=2] {'freq'}, use_global_device_ids=true, to_apply=%region_0.1.clone | all-reduce | flops 32768 | bytes 196608
  13.2 2.1 %reduce.62 = bf16[128,4224]{1,0:T(8,128)(2,1)} reduce(bf16[128,1,4224]{2,0,1:T(8,128)(2,1)S(1)} %maximum_bitcast_fusion, bf16[]{:T(256)} %broadcast.375), dimensions={1}, to_apply=%copy.72.reduce_sub_computation | reduce | bytes 2162690 | tf_op jit(solution)/shard_map/all_to_all | solution.py:97
  15.3 2.6 %reshape.399 = bf16[128,2,2112]{2,1,0:T(2,128)(2,1)} reshape(bf16[128,4224]{1,0:T(8,128)(2,1)} %reduce.62) | data formatting | bytes 2162688
  17.9 13.8 %all-to-all-start = ((bf16[128,2,2112]{2,1,0:T(2,128)(2,1)}), bf16[128,2,2112]{2,1,0:T(2,128)(2,1)S(1)}, u32[]{:S(2)}, u32[]{:S(2)}) async-start(bf16[128,2,2112]{2,1,0:T(2,128)(2,1)} %reshape.399), calls=%async_computation | async-start | bytes 2228224 | tf_op jit(solution)/shard_map/all_to_all | solution.py:97
  31.7 1.2 %fusion.4 = s32[256,8,32]{0,2,1:T(8,128)S(1)} fusion(s32[256,8,32]{0,2,1:T(8,128)} %param.7, s32[256,8]{0,1:T(8,128)S(1)} %copy-done.2), kind=kLoop, calls=%fused_computation.14 | loop fusion | flops 1507328 | bytes 532480 | tf_op jit(solution)/shard_map/jit(_where)/select_n | solution.py:99
  33.1 1.3 %copy.73 = s32[256,8,32]{2,1,0:T(8,128)} copy(s32[256,8,32]{0,2,1:T(8,128)S(1)} %fusion.4) | data formatting | bytes 524288 | tf_op jit(solution)/shard_map/jit(_where)/select_n | solution.py:99
  34.5 2.6 %copy.74 = s32[2,8,128,32]{3,2,1,0:T(8,128)} copy(s32[2,8,128,32]{3,1,0,2:T(8,128)} %bitcast.31) | data formatting | bytes 524288 | tf_op jit(solution)/shard_map/transpose | solution.py:100
  37.2 1.0 slice_reduce_fusion.30
  38.2 0.8 fusion.150
  39.0 1.0 fusion.149
  40.0 14.7 %convert_reduce_fusion.counts_ref = f32[2,8,128,256]{3,2,1,0:T(8,128)} fusion(s32[2,8,128,32]{3,2,1,0:T(8,128)S(1)} %copy-done.1), kind=kLoop, calls=%fused_computation | loop fusion | flops 49807360 | bytes 2359296 | tf_op jit(solution)/shard_map/reduce_sum | solution.py:101
  54.7 9.3 %all-to-all-done = bf16[128,2,2112]{2,1,0:T(2,128)(2,1)S(1)} async-done(((bf16[128,2,2112]{2,1,0:T(2,128)(2,1)}), bf16[128,2,2112]{2,1,0:T(2,128)(2,1)S(1)}, u32[]{:S(2)}, u32[]{:S(2)}) %all-to-all-start) | async-done | bytes 1081376 | tf_op jit(solution)/shard_map/all_to_all | solution.py:97
  64.0 3.6 %reshape.400 = bf16[128,1,4224]{2,1,0:T(2,128)(2,1)} reshape(bf16[128,2,2112]{2,1,0:T(2,128)(2,1)S(1)} %all-to-all-done) | data formatting | bytes 2162688
  67.5 2.7 %copy.86 = bf16[128,1,4224]{2,0,1:T(8,128)(2,1)} copy(bf16[128,1,4224]{2,1,0:T(2,128)(2,1)} %reshape.400) | data formatting | bytes 2162688
  70.2 6.3 %shard_map.55 = bf16[128,128]{1,0:T(8,128)(2,1)} custom-call(bf16[128,4224]{1,0:T(8,128)(2,1)} %bitcast.30, f32[2,8,128,256]{3,2,1,0:T(8,128)} %convert_reduce_fusion.counts_ref), custom_call_target="tpu_custom_call" | custom-call | flops 33554432 | bytes 4194304 | tf_op jit(solution)/shard_map/pallas_call | solution.py:107
  76.5 1.4 %copy.75 = bf16[128,1,128]{2,1,0:T(2,128)(2,1)} copy(bf16[128,1,128]{2,0,1:T(8,128)(2,1)} %bitcast.34) | data formatting | bytes 65536 | tf_op jit(solution)/shard_map/all_to_all | solution.py:117
  77.9 6.3 %all-to-all-start.1 = ((bf16[128,1,128]{2,1,0:T(2,128)(2,1)}), bf16[128,1,128]{2,1,0:T(2,128)(2,1)S(1)}, u32[]{:S(2)}, u32[]{:S(2)}) async-start(bf16[128,1,128]{2,1,0:T(2,128)(2,1)} %copy.75), calls=%async_computation.1 | async-start | bytes 131072 | tf_op jit(solution)/shard_map/all_to_all | solution.py:117
  84.3 0.9 slice_reduce_fusion.29
  85.2 9.5 %all-to-all-done.1 = bf16[128,1,128]{2,1,0:T(2,128)(2,1)S(1)} async-done(((bf16[128,1,128]{2,1,0:T(2,128)(2,1)}), bf16[128,1,128]{2,1,0:T(2,128)(2,1)S(1)}, u32[]{:S(2)}, u32[]{:S(2)}) %all-to-all-start.1) | async-done | bytes 32800 | tf_op jit(solution)/shard_map/all_to_all | solution.py:117
  94.8 4.7 %all-gather = bf16[256,1,128]{2,0,1:T(8,128)(2,1)S(1)} all-gather(bf16[128,1,128]{2,0,1:T(8,128)(2,1)S(1)} %copy.76), channel_id=2, replica_groups=mesh['shot'=128,'freq'=2] {'freq'}, dimensions={0}, use_global_device_ids=true | all-gather | bytes 98304 | tf_op jit(solution)/shard_map/all_gather | solution.py:118
  100.1 1.5 %reshape.358 = bf16[2,1024,16]{1,2,0:T(8,128)(2,1)S(1)} reshape(bf16[2,128,8,2,4,2]{2,1,5,4,3,0:T(8,128)(2,1)S(1)} %copy.78) | data formatting | bytes 131072 | tf_op jit(solution)/shard_map/reshape | solution.py:120
  101.6 4.5 %convolution_convert_fusion = bf16[2,1024,512]{2,1,0:T(8,128)(2,1)} fusion(bf16[2,1024,16]{1,2,0:T(8,128)(2,1)S(1)} %reshape.358, f32[16,512]{1,0:T(8,128)} %get-tuple-element.37, f32[2]{0:T(128)S(1)} %get-tuple-element.6, f32[16,512]{1,0:T(8,128)} %get-tuple-element.38, f32[2]{0:T(128)S(1)} %get-tuple-element.7, f32[16,512]{1,0:T(8,128)} %get-tuple-element.39, ...), kind=kOutput, calls=%fused_computation.4 | convolution fusion | flops 203374592 | bytes 3178744 | tf_op jit(solution)/shard_map/dot_general | solution.py:133
  (41 shorter events, 4.8 us)
Async XLA Ops:
  0.0 1.6 %copy-start = (bf16[2,1024,512]{2,1,0:T(8,128)(2,1)S(1)}, bf16[2,1024,512]{2,1,0:T(8,128)(2,1)}, u32[]{:S(2)}) copy-start(bf16[2,1024,512]{2,1,0:T(8,128)(2,1)} %param.5) | copy-start | bytes 6291460
  0.0 9.2 %copy-start.6 = (u32[256]{0:T(256)S(1)}, u32[256]{0:T(256)}, u32[]{:S(2)}) copy-start(u32[256]{0:T(256)} %constant.77) | copy-start | bytes 3076
  15.3 16.4 %copy-start.2 = (s32[256,8]{0,1:T(8,128)S(1)}, s32[256,8]{0,1:T(8,128)}, u32[]{:S(2)}) copy-start(s32[256,8]{0,1:T(8,128)} %param.8) | copy-start | bytes 24580
  15.3 17.7 %copy-start.3 = (s32[8]{0:T(128)S(1)}, s32[8]{0:T(128)}, u32[]{:S(2)}) copy-start(s32[8]{0:T(128)} %param.6) | copy-start | bytes 100
  17.9 46.0 %all-to-all-start = ((bf16[128,2,2112]{2,1,0:T(2,128)(2,1)}), bf16[128,2,2112]{2,1,0:T(2,128)(2,1)S(1)}, u32[]{:S(2)}, u32[]{:S(2)}) async-start(bf16[128,2,2112]{2,1,0:T(2,128)(2,1)} %reshape.399), calls=%async_computation | async-start | bytes 2228224 | tf_op jit(solution)/shard_map/all_to_all | solution.py:97
  31.7 5.4 %copy-start.5 = (bf16[2,31]{1,0:T(2,128)(2,1)S(1)}, bf16[2,31]{1,0:T(2,128)(2,1)}, u32[]{:S(2)}) copy-start(bf16[2,31]{1,0:T(2,128)(2,1)} %param.9) | copy-start | bytes 376
  37.1 2.9 %copy-start.1 = (s32[2,8,128,32]{3,2,1,0:T(8,128)S(1)}, s32[2,8,128,32]{3,2,1,0:T(8,128)}, u32[]{:S(2)}) copy-start(s32[2,8,128,32]{3,2,1,0:T(8,128)} %copy.74) | copy-start | bytes 786436
  77.9 16.8 %all-to-all-start.1 = ((bf16[128,1,128]{2,1,0:T(2,128)(2,1)}), bf16[128,1,128]{2,1,0:T(2,128)(2,1)S(1)}, u32[]{:S(2)}, u32[]{:S(2)}) async-start(bf16[128,1,128]{2,1,0:T(2,128)(2,1)} %copy.75), calls=%async_computation.1 | async-start | bytes 131072 | tf_op jit(solution)/shard_map/all_to_all | solution.py:117
  85.2 16.3 %copy-start.4 = (f32[2]{0:T(128)S(1)}, f32[2]{0:T(128)}, u32[]{:S(2)}) copy-start(f32[2]{0:T(128)} %get-tuple-element.24) | copy-start | bytes 28

commit v4 on v3

--- a/solution.py
+++ b/solution.py
@@ -34,7 +34,7 @@
     return (jnp.cos(angles), jnp.sin(angles))
 
 
-def multiply_kernel(incoming_ref, counts_ref, out_ref, acc_ref, *, local_bins, shot_dev, receiver_dev, groups):
+def multiply_kernel(incoming_ref, counts_ref, out_ref, acc_ref, recv_ref, sems, *, local_bins, shot_dev, receiver_dev, groups):
     near = local_bins * 2 * shot_dev * receiver_dev
     q_t = incoming_ref[:, 0:near].astype(jnp.float32).T
     width = shot_dev * groups
@@ -65,7 +65,35 @@
                 col_i = ((f * 2 + 1) * shot_dev + i) * receiver_dev + r
                 acc_ref[:, col_r : col_r + 1] = jnp.sum(real_sum, axis=1, keepdims=True)
                 acc_ref[:, col_i : col_i + 1] = jnp.sum(imag_sum, axis=1, keepdims=True)
-    out_ref[...] = (acc_ref[...] * KMAX ** (-0.5)).astype(out_ref.dtype)
+    acc_ref[...] = (acc_ref[...] * KMAX ** (-0.5)).astype(jnp.bfloat16).astype(jnp.float32)
+    me = lax.axis_index("shot")
+    half = lax.axis_index("freq")
+    recv_ref[pl.ds(me, 1), :] = acc_ref[pl.ds(me, 1), :]
+
+    def send(step, carry):
+        target = lax.rem(me + step, groups)
+        pltpu.make_async_remote_copy(
+            src_ref=acc_ref.at[pl.ds(target, 1)],
+            dst_ref=recv_ref.at[pl.ds(me, 1)],
+            send_sem=sems.at[0],
+            recv_sem=sems.at[1],
+            device_id=(target, half),
+            device_id_type=pl.DeviceIdType.MESH,
+        ).start()
+        return carry
+
+    lax.fori_loop(1, groups, send, 0)
+    every = pltpu.make_async_remote_copy(
+        src_ref=acc_ref.at[pl.ds(0, groups - 1)],
+        dst_ref=recv_ref.at[pl.ds(0, groups - 1)],
+        send_sem=sems.at[0],
+        recv_sem=sems.at[1],
+        device_id=(me, half),
+        device_id_type=pl.DeviceIdType.MESH,
+    )
+    every.wait_send()
+    every.wait_recv()
+    out_ref[...] = recv_ref[...]
 
 
 def shards(traces, frequency_bins, aperture, lengths, filters):
@@ -104,18 +132,22 @@
     kernel = functools.partial(
         multiply_kernel, local_bins=local_bins, shot_dev=shot_dev, receiver_dev=receiver_dev, groups=groups
     )
-    multiples_spectra = pl.pallas_call(
+    back = pl.pallas_call(
         kernel,
-        out_shape=jax.ShapeDtypeStruct((groups, rows * receiver_dev), jnp.bfloat16),
+        out_shape=jax.ShapeDtypeStruct((groups, rows * receiver_dev), jnp.float32),
         in_specs=[pl.BlockSpec(memory_space=pltpu.VMEM)] * 2,
         out_specs=pl.BlockSpec(memory_space=pltpu.VMEM),
-        scratch_shapes=[pltpu.VMEM((groups, rows * receiver_dev), jnp.float32)],
+        scratch_shapes=[
+            pltpu.VMEM((groups, rows * receiver_dev), jnp.float32),
+            pltpu.VMEM((groups, rows * receiver_dev), jnp.float32),
+            pltpu.SemaphoreType.DMA((2,)),
+        ],
+        compiler_params=pltpu.CompilerParams(has_side_effects=True),
         cost_estimate=pl.CostEstimate(
             flops=16 * groups * shots * rows * receiver_dev // 2, transcendentals=0, bytes_accessed=4 * 1024 * 1024
         ),
     )(incoming, counts)
-    back = lax.all_to_all(multiples_spectra.reshape(groups, rows * receiver_dev), "shot", 0, 0, tiled=True)
-    piece = lax.all_gather(back, "freq", axis=0, tiled=False)
+    piece = lax.all_gather(back.astype(jnp.bfloat16), "freq", axis=0, tiled=False)
     piece = piece.reshape(freq_dev, groups, local_bins, 2, shot_dev, receiver_dev)
     piece = piece.transpose(4, 1, 5, 0, 2, 3).reshape(shot_dev, receivers, NF * 2)
     wide = time_dev + 2 * half_taps

time: 107 us -> 104 us (0.972)
  Pallas kernels: 6.27 us -> 23 us
  waiting for transfers between devices: 18.8 us -> 8.39 us
  starting transfers between devices: 20.1 us -> 13.8 us
  blocking collectives: 11.6 us -> 9.85 us
  local copies, waits for them, and re-layouts: 23.9 us -> 22.4 us
    pallas_call x1, Pallas kernels: 6.27 us -> 23 us  [shards(): pl.pallas_call(kernel, out_shape=jax.ShapeDtypeStruct((groups, rows * rec...]
    all_to_all x1 -> x0, waiting for transfers between devices: 9.53 us -> none  [shards(): lax.all_to_all(multiples_spectra.reshape(groups, rows * receiver_dev), 's...]
    all_to_all x1 -> x0, starting transfers between devices: 6.33 us -> none  [shards(): lax.all_to_all(multiples_spectra.reshape(groups, rows * receiver_dev), 's...]
    all_gather x1, blocking collectives: 4.67 us -> 2.92 us  [shards(): lax.all_gather(back.astype(jnp.bfloat16), 'freq', axis=0, tiled=False)]
    all_to_all x2 -> x0, local copies, waits for them, and re-layouts: 1.44 us -> none  [shards(): lax.all_to_all(multiples_spectra.reshape(groups, rows * receiver_dev), 's...]
    unnamed x19 -> x17, local copies, waits for them, and re-layouts: 10.1 us -> 10.1 us
  transfers between devices with their start and end apart: 2 -> 1, of which waited for: 2 -> 1; matrix products, arithmetic and copies ran while one was open for 22% -> 23% of each run, Pallas kernels for 0% -> 0%
where the time goes in v4:
time: 104 us
  Pallas kernels  23 us (22%)
  local copies, waits for them, and re-layouts  22.4 us (22%)
  other arithmetic  20.1 us (19%)
  starting transfers between devices  13.8 us (13%)
  blocking collectives  9.85 us (9%)
  waiting for transfers between devices  8.39 us (8%)
  matrix products  5.2 us (5%)
  between operations  1.05 us (1%)
    pallas_call x1, Pallas kernels, shards(): pl.pallas_call(kernel, out_shape=jax.ShapeDtypeStruct((groups, rows * rec...  23 us
    reduce_sum x1, other arithmetic, shards(): jnp.sum((codes[..., None] == jnp.arange(shots, dtype=jnp.int32)).astype(j...  14.7 us
    all_to_all x1, starting transfers between devices, shards(): incoming = lax.all_to_all(outgoing, 'shot', 0, 0, tiled=True)  13.8 us
    unnamed x17, local copies, waits for them, and re-layouts  10.1 us
    all_to_all x1, waiting for transfers between devices, shards(): incoming = lax.all_to_all(outgoing, 'shot', 0, 0, tiled=True)  8.39 us
    unnamed x1, blocking collectives  6.93 us
    dot_general x1, matrix products, shards(): lax.dot_general(piece.astype(jnp.float32), shaped, (((2,), (1,)), ((0,),...  4.56 us
    all_gather x1, blocking collectives, shards(): lax.all_gather(back.astype(jnp.bfloat16), 'freq', axis=0, tiled=False)  2.92 us
  transfers between devices with their start and end apart: 1, of which 1 were waited for; matrix products, arithmetic and copies ran while one was open for 23% of the time, Pallas kernels for 0%

profile of v4, /device:TPU:1, one launch (start us, length us, event | category | flops | bytes accessed | tf_op | source)
XLA Modules:
  0.0 103.8 jit_solution(3152877778438380356)
XLA Ops:
  0.0 1.0 fusion.142
  1.0 0.6 copy-done
  1.6 0.6 fusion
  2.2 6.9 %all-reduce.2 = bf16[8,2,2,1024]{3,0,2,1:T(8,128)(2,1)S(1)} all-reduce(f32[8,2,2,1024]{3,0,2,1:T(8,128)S(1)} %fusion), channel_id=3, replica_groups=mesh['shot'=128,'freq'=2] {'freq'}, use_global_device_ids=true, to_apply=%region_0.1.clone | all-reduce | flops 32768 | bytes 196608
  11.5 0.6 reshape.351
  13.2 2.1 %reduce.62 = bf16[128,4224]{1,0:T(8,128)(2,1)} reduce(bf16[128,1,4224]{2,0,1:T(8,128)(2,1)S(1)} %maximum_bitcast_fusion, bf16[]{:T(256)} %broadcast.375), dimensions={1}, to_apply=%copy.55.reduce_sub_computation | reduce | bytes 2162690 | tf_op jit(solution)/shard_map/all_to_all | solution.py:125
  15.3 2.6 %reshape.396 = bf16[128,2,2112]{2,1,0:T(2,128)(2,1)} reshape(bf16[128,4224]{1,0:T(8,128)(2,1)} %reduce.62) | data formatting | bytes 2162688
  17.9 13.8 %all-to-all-start = ((bf16[128,2,2112]{2,1,0:T(2,128)(2,1)}), bf16[128,2,2112]{2,1,0:T(2,128)(2,1)S(1)}, u32[]{:S(2)}, u32[]{:S(2)}) async-start(bf16[128,2,2112]{2,1,0:T(2,128)(2,1)} %reshape.396), calls=%async_computation | async-start | bytes 2228224 | tf_op jit(solution)/shard_map/all_to_all | solution.py:125
  31.7 1.2 %fusion.4 = s32[256,8,32]{0,2,1:T(8,128)S(1)} fusion(s32[256,8,32]{0,2,1:T(8,128)} %param.7, s32[256,8]{0,1:T(8,128)S(1)} %copy-done.2), kind=kLoop, calls=%fused_computation.14 | loop fusion | flops 1507328 | bytes 532480 | tf_op jit(solution)/shard_map/jit(_where)/select_n | solution.py:127
  32.9 1.3 %copy.56 = s32[256,8,32]{2,1,0:T(8,128)} copy(s32[256,8,32]{0,2,1:T(8,128)S(1)} %fusion.4) | data formatting | bytes 524288 | tf_op jit(solution)/shard_map/jit(_where)/select_n | solution.py:127
  34.3 2.6 %copy.57 = s32[2,8,128,32]{3,2,1,0:T(8,128)} copy(s32[2,8,128,32]{3,1,0,2:T(8,128)} %bitcast.30) | data formatting | bytes 524288 | tf_op jit(solution)/shard_map/transpose | solution.py:128
  37.1 0.9 slice_reduce_fusion.29
  38.0 1.1 %slice_reduce_fusion.30 = (f32[2]{0:T(128)S(1)}, f32[2]{0:T(128)S(1)}, f32[2]{0:T(128)S(1)}, f32[2]{0:T(128)S(1)}, f32[2]{0:T(128)}, /*index=5*/f32[2]{0:T(128)}...) fusion(f32[2,31]{1,0:T(2,128)S(1)} %convert_element_type.64), kind=kLoop, calls=%fused_computation.208 | loop fusion | bytes 304 | tf_op jit(solution)/shard_map/slice | solution.py:162
  39.1 0.8 fusion.150
  39.9 1.0 fusion.149
  40.9 14.7 %convert_reduce_fusion.counts_ref = f32[2,8,128,256]{3,2,1,0:T(8,128)} fusion(s32[2,8,128,32]{3,2,1,0:T(8,128)S(1)} %copy-done.1), kind=kLoop, calls=%fused_computation | loop fusion | flops 49807360 | bytes 2359296 | tf_op jit(solution)/shard_map/reduce_sum | solution.py:129
  55.6 8.4 %all-to-all-done = bf16[128,2,2112]{2,1,0:T(2,128)(2,1)S(1)} async-done(((bf16[128,2,2112]{2,1,0:T(2,128)(2,1)}), bf16[128,2,2112]{2,1,0:T(2,128)(2,1)S(1)}, u32[]{:S(2)}, u32[]{:S(2)}) %all-to-all-start) | async-done | bytes 1081376 | tf_op jit(solution)/shard_map/all_to_all | solution.py:125
  63.9 3.6 %reshape.397 = bf16[128,1,4224]{2,1,0:T(2,128)(2,1)} reshape(bf16[128,2,2112]{2,1,0:T(2,128)(2,1)S(1)} %all-to-all-done) | data formatting | bytes 2162688
  67.5 2.7 %copy.67 = bf16[128,1,4224]{2,0,1:T(8,128)(2,1)} copy(bf16[128,1,4224]{2,1,0:T(2,128)(2,1)} %reshape.397) | data formatting | bytes 2162688
  70.2 23.0 %shard_map.55 = f32[128,128]{1,0:T(8,128)} custom-call(bf16[128,4224]{1,0:T(8,128)(2,1)} %bitcast.29, f32[2,8,128,256]{3,2,1,0:T(8,128)} %convert_reduce_fusion.counts_ref), custom_call_target="tpu_custom_call" | custom-call | flops 33554432 | bytes 4194304 | tf_op jit(solution)/shard_map/pallas_call | solution.py:135
  93.2 0.8 convert_element_type.63
  94.1 2.9 %all-gather = bf16[256,128]{1,0:T(8,128)(2,1)S(1)} all-gather(bf16[128,128]{1,0:T(8,128)(2,1)S(1)} %convert_element_type.63), channel_id=2, replica_groups=mesh['shot'=128,'freq'=2] {'freq'}, dimensions={0}, use_global_device_ids=true | all-gather | bytes 98304 | tf_op jit(solution)/shard_map/all_gather | solution.py:150
  97.6 1.5 %reshape.355 = bf16[2,1024,16]{1,2,0:T(8,128)(2,1)S(1)} reshape(bf16[2,128,8,2,4,2]{2,1,5,4,3,0:T(8,128)(2,1)S(1)} %copy.59) | data formatting | bytes 131072 | tf_op jit(solution)/shard_map/reshape | solution.py:152
  99.1 4.6 %convolution_convert_fusion = bf16[2,1024,512]{2,1,0:T(8,128)(2,1)} fusion(bf16[2,1024,16]{1,2,0:T(8,128)(2,1)S(1)} %reshape.355, f32[16,512]{1,0:T(8,128)} %get-tuple-element.37, f32[2]{0:T(128)S(1)} %get-tuple-element.6, f32[16,512]{1,0:T(8,128)} %get-tuple-element.38, f32[2]{0:T(128)S(1)} %get-tuple-element.7, f32[16,512]{1,0:T(8,128)} %get-tuple-element.39, ...), kind=kOutput, calls=%fused_computation.4 | convolution fusion | flops 203374592 | bytes 3178744 | tf_op jit(solution)/shard_map/dot_general | solution.py:165
  (36 shorter events, 3.5 us)
Async XLA Ops:
  0.0 1.6 %copy-start = (bf16[2,1024,512]{2,1,0:T(8,128)(2,1)S(1)}, bf16[2,1024,512]{2,1,0:T(8,128)(2,1)}, u32[]{:S(2)}) copy-start(bf16[2,1024,512]{2,1,0:T(8,128)(2,1)} %param.5) | copy-start | bytes 6291460
  0.0 9.2 %copy-start.5 = (u32[256]{0:T(256)S(1)}, u32[256]{0:T(256)}, u32[]{:S(2)}) copy-start(u32[256]{0:T(256)} %constant.77) | copy-start | bytes 3076
  15.3 16.4 %copy-start.2 = (s32[256,8]{0,1:T(8,128)S(1)}, s32[256,8]{0,1:T(8,128)}, u32[]{:S(2)}) copy-start(s32[256,8]{0,1:T(8,128)} %param.8) | copy-start | bytes 24580
  17.9 46.0 %all-to-all-start = ((bf16[128,2,2112]{2,1,0:T(2,128)(2,1)}), bf16[128,2,2112]{2,1,0:T(2,128)(2,1)S(1)}, u32[]{:S(2)}, u32[]{:S(2)}) async-start(bf16[128,2,2112]{2,1,0:T(2,128)(2,1)} %reshape.396), calls=%async_computation | async-start | bytes 2228224 | tf_op jit(solution)/shard_map/all_to_all | solution.py:125
  31.7 5.1 %copy-start.3 = (s32[8]{0:T(128)S(1)}, s32[8]{0:T(128)}, u32[]{:S(2)}) copy-start(s32[8]{0:T(128)} %param.6) | copy-start | bytes 100
  31.7 5.4 %copy-start.4 = (bf16[2,31]{1,0:T(2,128)(2,1)S(1)}, bf16[2,31]{1,0:T(2,128)(2,1)}, u32[]{:S(2)}) copy-start(bf16[2,31]{1,0:T(2,128)(2,1)} %param.9) | copy-start | bytes 376
  37.1 3.8 %copy-start.1 = (s32[2,8,128,32]{3,2,1,0:T(8,128)S(1)}, s32[2,8,128,32]{3,2,1,0:T(8,128)}, u32[]{:S(2)}) copy-start(s32[2,8,128,32]{3,2,1,0:T(8,128)} %copy.57) | copy-start | bytes 786436

commit v5 on v4

--- a/solution.py
+++ b/solution.py
@@ -34,55 +34,65 @@
     return (jnp.cos(angles), jnp.sin(angles))
 
 
-def multiply_kernel(incoming_ref, counts_ref, out_ref, acc_ref, recv_ref, sems, *, local_bins, shot_dev, receiver_dev, groups):
+def multiply_kernel(
+    incoming_ref, counts_ref, out_ref, qt_ref, acc_ref, recv_ref, sems, *, local_bins, shot_dev, receiver_dev, groups
+):
     near = local_bins * 2 * shot_dev * receiver_dev
-    q_t = incoming_ref[:, 0:near].astype(jnp.float32).T
     width = shot_dev * groups
-
-    def q_row(f, c, i, r):
-        row = ((f * 2 + c) * shot_dev + i) * receiver_dev + r
-        return q_t[row : row + 1, :]
-
-    for i in range(shot_dev):
-        for r in range(receiver_dev):
-            weights = [counts_ref[i, r, :, h * groups : (h + 1) * groups] for h in range(shot_dev)]
-            for f in range(local_bins):
-                real_sum = None
-                imag_sum = None
-                for h in range(shot_dev):
-                    base_r = near + ((f * 2 + 0) * shot_dev + i) * width + h * groups
-                    base_i = near + ((f * 2 + 1) * shot_dev + i) * width + h * groups
-                    pr = incoming_ref[:, base_r : base_r + groups].astype(jnp.float32)
-                    pi = incoming_ref[:, base_i : base_i + groups].astype(jnp.float32)
-                    qr = q_row(f, 0, h, r)
-                    qi = q_row(f, 1, h, r)
-                    w = weights[h]
-                    real_term = w * (pr * qr - pi * qi)
-                    imag_term = w * (pr * qi + pi * qr)
-                    real_sum = real_term if real_sum is None else real_sum + real_term
-                    imag_sum = imag_term if imag_sum is None else imag_sum + imag_term
-                col_r = ((f * 2 + 0) * shot_dev + i) * receiver_dev + r
-                col_i = ((f * 2 + 1) * shot_dev + i) * receiver_dev + r
-                acc_ref[:, col_r : col_r + 1] = jnp.sum(real_sum, axis=1, keepdims=True)
-                acc_ref[:, col_i : col_i + 1] = jnp.sum(imag_sum, axis=1, keepdims=True)
-    acc_ref[...] = (acc_ref[...] * KMAX ** (-0.5)).astype(jnp.bfloat16).astype(jnp.float32)
+    qt_ref[...] = incoming_ref[:, 0:near].astype(jnp.float32).T
     me = lax.axis_index("shot")
     half = lax.axis_index("freq")
-    recv_ref[pl.ds(me, 1), :] = acc_ref[pl.ds(me, 1), :]
+    block = 16
 
-    def send(step, carry):
-        target = lax.rem(me + step, groups)
-        pltpu.make_async_remote_copy(
-            src_ref=acc_ref.at[pl.ds(target, 1)],
-            dst_ref=recv_ref.at[pl.ds(me, 1)],
-            send_sem=sems.at[0],
-            recv_sem=sems.at[1],
-            device_id=(target, half),
-            device_id_type=pl.DeviceIdType.MESH,
-        ).start()
+    def chunk(step, carry):
+        top = pl.multiple_of(step * block, block)
+        rows = pl.ds(top, block)
+        for i in range(shot_dev):
+            for r in range(receiver_dev):
+                weights = [counts_ref[i, r, rows, h * groups : (h + 1) * groups] for h in range(shot_dev)]
+                for f in range(local_bins):
+                    real_sum = None
+                    imag_sum = None
+                    for h in range(shot_dev):
+                        base_r = near + ((f * 2 + 0) * shot_dev + i) * width + h * groups
+                        base_i = near + ((f * 2 + 1) * shot_dev + i) * width + h * groups
+                        pr = incoming_ref[rows, base_r : base_r + groups].astype(jnp.float32)
+                        pi = incoming_ref[rows, base_i : base_i + groups].astype(jnp.float32)
+                        row_r = ((f * 2 + 0) * shot_dev + h) * receiver_dev + r
+                        row_i = ((f * 2 + 1) * shot_dev + h) * receiver_dev + r
+                        qr = qt_ref[row_r : row_r + 1, :]
+                        qi = qt_ref[row_i : row_i + 1, :]
+                        w = weights[h]
+                        real_term = w * (pr * qr - pi * qi)
+                        imag_term = w * (pr * qi + pi * qr)
+                        real_sum = real_term if real_sum is None else real_sum + real_term
+                        imag_sum = imag_term if imag_sum is None else imag_sum + imag_term
+                    col_r = ((f * 2 + 0) * shot_dev + i) * receiver_dev + r
+                    col_i = ((f * 2 + 1) * shot_dev + i) * receiver_dev + r
+                    acc_ref[rows, col_r : col_r + 1] = jnp.sum(real_sum, axis=1, keepdims=True)
+                    acc_ref[rows, col_i : col_i + 1] = jnp.sum(imag_sum, axis=1, keepdims=True)
+        acc_ref[rows, :] = (acc_ref[rows, :] * KMAX ** (-0.5)).astype(jnp.bfloat16).astype(jnp.float32)
+        for t in range(block):
+            target = top + t
+
+            @pl.when(target != me)
+            def _():
+                pltpu.make_async_remote_copy(
+                    src_ref=acc_ref.at[pl.ds(target, 1)],
+                    dst_ref=recv_ref.at[pl.ds(me, 1)],
+                    send_sem=sems.at[0],
+                    recv_sem=sems.at[1],
+                    device_id=(target, half),
+                    device_id_type=pl.DeviceIdType.MESH,
+                ).start()
+
+            @pl.when(target == me)
+            def _():
+                recv_ref[pl.ds(me, 1), :] = acc_ref[pl.ds(me, 1), :]
+
         return carry
 
-    lax.fori_loop(1, groups, send, 0)
+    lax.fori_loop(0, groups // block, chunk, 0)
     every = pltpu.make_async_remote_copy(
         src_ref=acc_ref.at[pl.ds(0, groups - 1)],
         dst_ref=recv_ref.at[pl.ds(0, groups - 1)],
@@ -138,6 +148,7 @@
         in_specs=[pl.BlockSpec(memory_space=pltpu.VMEM)] * 2,
         out_specs=pl.BlockSpec(memory_space=pltpu.VMEM),
         scratch_shapes=[
+            pltpu.VMEM((rows * receiver_dev, groups), jnp.float32),
             pltpu.VMEM((groups, rows * receiver_dev), jnp.float32),
             pltpu.VMEM((groups, rows * receiver_dev), jnp.float32),
             pltpu.SemaphoreType.DMA((2,)),

time: 104 us -> 101 us (0.971); the launches traced: 104 us -> 99.7 us
  Pallas kernels: 23 us -> 19.2 us
    pallas_call x1, Pallas kernels: 23 us -> 19.2 us  [shards(): pl.pallas_call(kernel, out_shape=jax.ShapeDtypeStruct((groups, rows * rec...]
  transfers between devices with their start and end apart: 1 -> 1, of which waited for: 1 -> 1; matrix products, arithmetic and copies ran while one was open for 23% -> 24% of each run, Pallas kernels for 0% -> 0%
where the time goes in v5:
time: 101 us; the launch traced here: 99.7 us
  local copies, waits for them, and re-layouts  22.4 us (22%)
  other arithmetic  20.1 us (20%)
  Pallas kernels  19.2 us (19%)
  starting transfers between devices  13.8 us (14%)
  blocking collectives  9.66 us (10%)
  waiting for transfers between devices  8.39 us (8%)
  matrix products  5.19 us (5%)
    pallas_call x1, Pallas kernels, shards(): pl.pallas_call(kernel, out_shape=jax.ShapeDtypeStruct((groups, rows * rec...  19.2 us
    reduce_sum x1, other arithmetic, shards(): jnp.sum((codes[..., None] == jnp.arange(shots, dtype=jnp.int32)).astype(j...  14.7 us
    all_to_all x1, starting transfers between devices, shards(): incoming = lax.all_to_all(outgoing, 'shot', 0, 0, tiled=True)  13.8 us
    unnamed x17, local copies, waits for them, and re-layouts  10.1 us
    all_to_all x1, waiting for transfers between devices, shards(): incoming = lax.all_to_all(outgoing, 'shot', 0, 0, tiled=True)  8.39 us
    unnamed x1, blocking collectives  6.93 us
    dot_general x1, matrix products, shards(): lax.dot_general(piece.astype(jnp.float32), shaped, (((2,), (1,)), ((0,),...  4.55 us
    all_gather x1, blocking collectives, shards(): lax.all_gather(back.astype(jnp.bfloat16), 'freq', axis=0, tiled=False)  2.72 us
  transfers between devices with their start and end apart: 1, of which 1 were waited for; matrix products, arithmetic and copies ran while one was open for 24% of the time, Pallas kernels for 0%

profile of v5, /device:TPU:1, one launch (start us, length us, event | category | flops | bytes accessed | tf_op | source)
XLA Modules:
  0.0 99.7 jit_solution(7371077692225632174)
XLA Ops:
  0.0 1.0 fusion.142
  1.0 0.6 copy-done
  1.6 0.6 fusion
  2.2 6.9 %all-reduce.2 = bf16[8,2,2,1024]{3,0,2,1:T(8,128)(2,1)S(1)} all-reduce(f32[8,2,2,1024]{3,0,2,1:T(8,128)S(1)} %fusion), channel_id=3, replica_groups=mesh['shot'=128,'freq'=2] {'freq'}, use_global_device_ids=true, to_apply=%region_0.1.clone | all-reduce | flops 32768 | bytes 196608
  11.5 0.6 reshape.351
  13.2 2.1 %reduce.62 = bf16[128,4224]{1,0:T(8,128)(2,1)} reduce(bf16[128,1,4224]{2,0,1:T(8,128)(2,1)S(1)} %maximum_bitcast_fusion, bf16[]{:T(256)} %broadcast.375), dimensions={1}, to_apply=%copy.55.reduce_sub_computation | reduce | bytes 2162690 | tf_op jit(solution)/shard_map/all_to_all | solution.py:135
  15.3 2.6 %reshape.396 = bf16[128,2,2112]{2,1,0:T(2,128)(2,1)} reshape(bf16[128,4224]{1,0:T(8,128)(2,1)} %reduce.62) | data formatting | bytes 2162688
  17.9 13.8 %all-to-all-start = ((bf16[128,2,2112]{2,1,0:T(2,128)(2,1)}), bf16[128,2,2112]{2,1,0:T(2,128)(2,1)S(1)}, u32[]{:S(2)}, u32[]{:S(2)}) async-start(bf16[128,2,2112]{2,1,0:T(2,128)(2,1)} %reshape.396), calls=%async_computation | async-start | bytes 2228224 | tf_op jit(solution)/shard_map/all_to_all | solution.py:135
  31.7 1.2 %fusion.4 = s32[256,8,32]{0,2,1:T(8,128)S(1)} fusion(s32[256,8,32]{0,2,1:T(8,128)} %param.7, s32[256,8]{0,1:T(8,128)S(1)} %copy-done.2), kind=kLoop, calls=%fused_computation.14 | loop fusion | flops 1507328 | bytes 532480 | tf_op jit(solution)/shard_map/jit(_where)/select_n | solution.py:137
  32.9 1.3 %copy.56 = s32[256,8,32]{2,1,0:T(8,128)} copy(s32[256,8,32]{0,2,1:T(8,128)S(1)} %fusion.4) | data formatting | bytes 524288 | tf_op jit(solution)/shard_map/jit(_where)/select_n | solution.py:137
  34.3 2.6 %copy.57 = s32[2,8,128,32]{3,2,1,0:T(8,128)} copy(s32[2,8,128,32]{3,1,0,2:T(8,128)} %bitcast.30) | data formatting | bytes 524288 | tf_op jit(solution)/shard_map/transpose | solution.py:138
  37.1 0.9 slice_reduce_fusion.29
  38.0 1.1 %slice_reduce_fusion.30 = (f32[2]{0:T(128)S(1)}, f32[2]{0:T(128)S(1)}, f32[2]{0:T(128)S(1)}, f32[2]{0:T(128)S(1)}, f32[2]{0:T(128)}, /*index=5*/f32[2]{0:T(128)}...) fusion(f32[2,31]{1,0:T(2,128)S(1)} %convert_element_type.64), kind=kLoop, calls=%fused_computation.208 | loop fusion | bytes 304 | tf_op jit(solution)/shard_map/slice | solution.py:173
  39.1 0.8 fusion.150
  39.9 1.0 %fusion.149 = (f32[16,512]{1,0:T(8,128)}, f32[16,512]{1,0:T(8,128)}, f32[16,512]{1,0:T(8,128)}, f32[16,512]{1,0:T(8,128)}, f32[16,512]{1,0:T(8,128)}, /*index=5*...) fusion(f32[16,542]{1,0:T(8,128)S(1)} %broadcast_select_fusion), kind=kLoop, calls=%fused_computation.211 | loop fusion | bytes 1245184 | tf_op jit(solution)/shard_map/slice | solution.py:173
  40.9 14.7 %convert_reduce_fusion.counts_ref = f32[2,8,128,256]{3,2,1,0:T(8,128)} fusion(s32[2,8,128,32]{3,2,1,0:T(8,128)S(1)} %copy-done.1), kind=kLoop, calls=%fused_computation | loop fusion | flops 49807360 | bytes 2359296 | tf_op jit(solution)/shard_map/reduce_sum | solution.py:139
  55.6 8.4 %all-to-all-done = bf16[128,2,2112]{2,1,0:T(2,128)(2,1)S(1)} async-done(((bf16[128,2,2112]{2,1,0:T(2,128)(2,1)}), bf16[128,2,2112]{2,1,0:T(2,128)(2,1)S(1)}, u32[]{:S(2)}, u32[]{:S(2)}) %all-to-all-start) | async-done | bytes 1081376 | tf_op jit(solution)/shard_map/all_to_all | solution.py:135
  63.9 3.6 %reshape.397 = bf16[128,1,4224]{2,1,0:T(2,128)(2,1)} reshape(bf16[128,2,2112]{2,1,0:T(2,128)(2,1)S(1)} %all-to-all-done) | data formatting | bytes 2162688
  67.5 2.7 %copy.67 = bf16[128,1,4224]{2,0,1:T(8,128)(2,1)} copy(bf16[128,1,4224]{2,1,0:T(2,128)(2,1)} %reshape.397) | data formatting | bytes 2162688
  70.2 19.2 %shard_map.55 = f32[128,128]{1,0:T(8,128)} custom-call(bf16[128,4224]{1,0:T(8,128)(2,1)} %bitcast.29, f32[2,8,128,256]{3,2,1,0:T(8,128)} %convert_reduce_fusion.counts_ref), custom_call_target="tpu_custom_call" | custom-call | flops 33554432 | bytes 4194304 | tf_op jit(solution)/shard_map/pallas_call | solution.py:145
  89.5 0.8 convert_element_type.63
  90.3 2.7 %all-gather = bf16[256,128]{1,0:T(8,128)(2,1)S(1)} all-gather(bf16[128,128]{1,0:T(8,128)(2,1)S(1)} %convert_element_type.63), channel_id=2, replica_groups=mesh['shot'=128,'freq'=2] {'freq'}, dimensions={0}, use_global_device_ids=true | all-gather | bytes 98304 | tf_op jit(solution)/shard_map/all_gather | solution.py:161
  93.7 1.5 %reshape.355 = bf16[2,1024,16]{1,2,0:T(8,128)(2,1)S(1)} reshape(bf16[2,128,8,2,4,2]{2,1,5,4,3,0:T(8,128)(2,1)S(1)} %copy.59) | data formatting | bytes 131072 | tf_op jit(solution)/shard_map/reshape | solution.py:163
  95.1 4.6 %convolution_convert_fusion = bf16[2,1024,512]{2,1,0:T(8,128)(2,1)} fusion(bf16[2,1024,16]{1,2,0:T(8,128)(2,1)S(1)} %reshape.355, f32[16,512]{1,0:T(8,128)} %get-tuple-element.37, f32[2]{0:T(128)S(1)} %get-tuple-element.6, f32[16,512]{1,0:T(8,128)} %get-tuple-element.38, f32[2]{0:T(128)S(1)} %get-tuple-element.7, f32[16,512]{1,0:T(8,128)} %get-tuple-element.39, ...), kind=kOutput, calls=%fused_computation.4 | convolution fusion | flops 203374592 | bytes 3178744 | tf_op jit(solution)/shard_map/dot_general | solution.py:176
  (36 shorter events, 3.5 us)
Async XLA Ops:
  0.0 1.6 %copy-start = (bf16[2,1024,512]{2,1,0:T(8,128)(2,1)S(1)}, bf16[2,1024,512]{2,1,0:T(8,128)(2,1)}, u32[]{:S(2)}) copy-start(bf16[2,1024,512]{2,1,0:T(8,128)(2,1)} %param.5) | copy-start | bytes 6291460
  0.0 9.2 %copy-start.5 = (u32[256]{0:T(256)S(1)}, u32[256]{0:T(256)}, u32[]{:S(2)}) copy-start(u32[256]{0:T(256)} %constant.77) | copy-start | bytes 3076
  15.3 16.4 %copy-start.2 = (s32[256,8]{0,1:T(8,128)S(1)}, s32[256,8]{0,1:T(8,128)}, u32[]{:S(2)}) copy-start(s32[256,8]{0,1:T(8,128)} %param.8) | copy-start | bytes 24580
  17.9 46.0 %all-to-all-start = ((bf16[128,2,2112]{2,1,0:T(2,128)(2,1)}), bf16[128,2,2112]{2,1,0:T(2,128)(2,1)S(1)}, u32[]{:S(2)}, u32[]{:S(2)}) async-start(bf16[128,2,2112]{2,1,0:T(2,128)(2,1)} %reshape.396), calls=%async_computation | async-start | bytes 2228224 | tf_op jit(solution)/shard_map/all_to_all | solution.py:135
  31.7 5.1 %copy-start.3 = (s32[8]{0:T(128)S(1)}, s32[8]{0:T(128)}, u32[]{:S(2)}) copy-start(s32[8]{0:T(128)} %param.6) | copy-start | bytes 100
  31.7 5.4 %copy-start.4 = (bf16[2,31]{1,0:T(2,128)(2,1)S(1)}, bf16[2,31]{1,0:T(2,128)(2,1)}, u32[]{:S(2)}) copy-start(bf16[2,31]{1,0:T(2,128)(2,1)} %param.9) | copy-start | bytes 376
  37.1 3.8 %copy-start.1 = (s32[2,8,128,32]{3,2,1,0:T(8,128)S(1)}, s32[2,8,128,32]{3,2,1,0:T(8,128)}, u32[]{:S(2)}) copy-start(s32[2,8,128,32]{3,2,1,0:T(8,128)} %copy.57) | copy-start | bytes 786436

commit v6 on v5

--- a/solution.py
+++ b/solution.py
@@ -173,11 +173,12 @@
         taps[:, tap, None, None] * wide_rows[None, :, 2 * half_taps - tap : 2 * half_taps - tap + time_dev]
         for tap in range(TAPS)
     )
+    leading = shaped.astype(jnp.bfloat16)
+    trailing = (shaped - leading.astype(jnp.float32)).astype(jnp.bfloat16)
     filtered = lax.dot_general(
-        piece.astype(jnp.float32),
-        shaped,
+        jnp.concatenate([piece, piece], axis=2),
+        jnp.concatenate([leading, trailing], axis=1),
         (((2,), (1,)), ((0,), (0,))),
-        precision=lax.Precision.HIGHEST,
         preferred_element_type=jnp.float32,
     )
     return filtered.astype(jnp.bfloat16)

time: 101 us -> 99 us (0.980)
  matrix products: 5.19 us -> 2.72 us
  local copies, waits for them, and re-layouts: 22.4 us -> 20.6 us
  waiting for transfers between devices: 8.39 us -> 9.43 us
    dot_general x1, matrix products: 4.55 us -> 2.08 us  [shards(): lax.dot_general(jnp.concatenate([piece, piece], axis=2), jnp.concatenate(...]
    slice x2, local copies, waits for them, and re-layouts: 1.79 us -> 0.39 us  [shards(): wide_rows[None, :, 2 * half_taps - tap:2 * half_taps - tap + time_dev]]
    all_to_all x1, waiting for transfers between devices: 8.39 us -> 9.43 us  [shards(): incoming = lax.all_to_all(outgoing, 'shot', 0, 0, tiled=True)]
    unnamed x17 -> x25, local copies, waits for them, and re-layouts: 10.1 us -> 10.2 us
  transfers between devices with their start and end apart: 1 -> 1, of which waited for: 1 -> 1; matrix products, arithmetic and copies ran while one was open for 24% -> 23% of each run, Pallas kernels for 0% -> 0%
where the time goes in v6:
time: 99 us; the launch traced here: 97.2 us
  other arithmetic  20.9 us (21%)
  local copies, waits for them, and re-layouts  20.6 us (21%)
  Pallas kernels  19.2 us (19%)
  starting transfers between devices  13.8 us (14%)
  blocking collectives  9.66 us (10%)
  waiting for transfers between devices  9.43 us (10%)
  matrix products  2.72 us (3%)
    pallas_call x1, Pallas kernels, shards(): pl.pallas_call(kernel, out_shape=jax.ShapeDtypeStruct((groups, rows * rec...  19.2 us
    reduce_sum x1, other arithmetic, shards(): jnp.sum((codes[..., None] == jnp.arange(shots, dtype=jnp.int32)).astype(j...  14.7 us
    all_to_all x1, starting transfers between devices, shards(): incoming = lax.all_to_all(outgoing, 'shot', 0, 0, tiled=True)  13.8 us
    unnamed x25, local copies, waits for them, and re-layouts  10.2 us
    all_to_all x1, waiting for transfers between devices, shards(): incoming = lax.all_to_all(outgoing, 'shot', 0, 0, tiled=True)  9.43 us
    unnamed x1, blocking collectives  6.93 us
    all_gather x1, blocking collectives, shards(): lax.all_gather(back.astype(jnp.bfloat16), 'freq', axis=0, tiled=False)  2.72 us
    transpose x1, local copies, waits for them, and re-layouts, shards(): codes.reshape(groups, shot_dev, receiver_dev, KMAX).transpose(1, 2, 0, 3)  2.58 us
  transfers between devices with their start and end apart: 1, of which 1 were waited for; matrix products, arithmetic and copies ran while one was open for 23% of the time, Pallas kernels for 0%

profile of v6, /device:TPU:1, one launch (start us, length us, event | category | flops | bytes accessed | tf_op | source)
XLA Modules:
  0.0 97.2 jit_solution(12850789849246741059)
XLA Ops:
  0.0 1.0 fusion.25
  1.0 0.6 copy-done
  1.6 0.6 fusion
  2.2 6.9 %all-reduce.2 = bf16[8,2,2,1024]{3,0,2,1:T(8,128)(2,1)S(1)} all-reduce(f32[8,2,2,1024]{3,0,2,1:T(8,128)S(1)} %fusion), channel_id=3, replica_groups=mesh['shot'=128,'freq'=2] {'freq'}, use_global_device_ids=true, to_apply=%region_0.1.clone | all-reduce | flops 32768 | bytes 196608
  9.2 0.6 dynamic-slice
  11.5 0.6 reshape.351
  12.6 0.6 broadcast.375
  13.2 2.1 %reduce.62 = bf16[128,4224]{1,0:T(8,128)(2,1)} reduce(bf16[128,1,4224]{2,0,1:T(8,128)(2,1)S(1)} %maximum_bitcast_fusion, bf16[]{:T(256)} %broadcast.375), dimensions={1}, to_apply=%copy.55.reduce_sub_computation | reduce | bytes 2162690 | tf_op jit(solution)/shard_map/all_to_all | solution.py:135
  15.3 2.6 %reshape.396 = bf16[128,2,2112]{2,1,0:T(2,128)(2,1)} reshape(bf16[128,4224]{1,0:T(8,128)(2,1)} %reduce.62) | data formatting | bytes 2162688
  17.9 13.8 %all-to-all-start = ((bf16[128,2,2112]{2,1,0:T(2,128)(2,1)}), bf16[128,2,2112]{2,1,0:T(2,128)(2,1)S(1)}, u32[]{:S(2)}, u32[]{:S(2)}) async-start(bf16[128,2,2112]{2,1,0:T(2,128)(2,1)} %reshape.396), calls=%async_computation | async-start | bytes 2228224 | tf_op jit(solution)/shard_map/all_to_all | solution.py:135
  31.9 0.9 slice_reduce_fusion.29
  32.9 1.2 %fusion.4 = s32[256,8,32]{0,2,1:T(8,128)S(1)} fusion(s32[256,8,32]{0,2,1:T(8,128)} %param.7, s32[256,8]{0,1:T(8,128)S(1)} %copy-done.2), kind=kLoop, calls=%fused_computation.14 | loop fusion | flops 1507328 | bytes 532480 | tf_op jit(solution)/shard_map/jit(_where)/select_n | solution.py:137
  34.1 0.6 fusion.29
  34.7 1.3 %copy.56 = s32[256,8,32]{2,1,0:T(8,128)} copy(s32[256,8,32]{0,2,1:T(8,128)S(1)} %fusion.4) | data formatting | bytes 524288 | tf_op jit(solution)/shard_map/jit(_where)/select_n | solution.py:137
  36.0 2.6 %copy.57 = s32[2,8,128,32]{3,2,1,0:T(8,128)} copy(s32[2,8,128,32]{3,1,0,2:T(8,128)} %bitcast.29) | data formatting | bytes 524288 | tf_op jit(solution)/shard_map/transpose | solution.py:138
  39.9 14.7 %convert_reduce_fusion.counts_ref = f32[2,8,128,256]{3,2,1,0:T(8,128)} fusion(s32[2,8,128,32]{3,2,1,0:T(8,128)S(1)} %copy-done.1), kind=kLoop, calls=%fused_computation | loop fusion | flops 49807360 | bytes 2359296 | tf_op jit(solution)/shard_map/reduce_sum | solution.py:139
  54.5 9.4 %all-to-all-done = bf16[128,2,2112]{2,1,0:T(2,128)(2,1)S(1)} async-done(((bf16[128,2,2112]{2,1,0:T(2,128)(2,1)}), bf16[128,2,2112]{2,1,0:T(2,128)(2,1)S(1)}, u32[]{:S(2)}, u32[]{:S(2)}) %all-to-all-start) | async-done | bytes 1081376 | tf_op jit(solution)/shard_map/all_to_all | solution.py:135
  64.0 3.6 %reshape.397 = bf16[128,1,4224]{2,1,0:T(2,128)(2,1)} reshape(bf16[128,2,2112]{2,1,0:T(2,128)(2,1)S(1)} %all-to-all-done) | data formatting | bytes 2162688
  67.5 2.7 %copy.67 = bf16[128,1,4224]{2,0,1:T(8,128)(2,1)} copy(bf16[128,1,4224]{2,1,0:T(2,128)(2,1)} %reshape.397) | data formatting | bytes 2162688
  70.3 19.2 %shard_map.55 = f32[128,128]{1,0:T(8,128)} custom-call(bf16[128,4224]{1,0:T(8,128)(2,1)} %bitcast.28, f32[2,8,128,256]{3,2,1,0:T(8,128)} %convert_reduce_fusion.counts_ref), custom_call_target="tpu_custom_call" | custom-call | flops 33554432 | bytes 4194304 | tf_op jit(solution)/shard_map/pallas_call | solution.py:145
  89.5 0.8 convert_element_type.71
  90.3 2.7 %all-gather = bf16[256,128]{1,0:T(8,128)(2,1)S(1)} all-gather(bf16[128,128]{1,0:T(8,128)(2,1)S(1)} %convert_element_type.71), channel_id=2, replica_groups=mesh['shot'=128,'freq'=2] {'freq'}, dimensions={0}, use_global_device_ids=true | all-gather | bytes 98304 | tf_op jit(solution)/shard_map/all_gather | solution.py:161
  93.7 1.5 %reshape.355 = bf16[2,1024,16]{1,2,0:T(8,128)(2,1)S(1)} reshape(bf16[2,128,8,2,4,2]{2,1,5,4,3,0:T(8,128)(2,1)S(1)} %copy.59) | data formatting | bytes 131072 | tf_op jit(solution)/shard_map/reshape | solution.py:163
  95.2 2.1 %convolution_convert_fusion = bf16[2,1024,512]{2,1,0:T(8,128)(2,1)} fusion(bf16[2,1024,16]{1,2,0:T(8,128)(2,1)S(1)} %reshape.355, bf16[2,16,512]{2,1,0:T(8,128)(2,1)S(1)} %get-tuple-element.36, bf16[2,16,512]{2,1,0:T(8,128)(2,1)S(1)} %get-tuple-element.37), kind=kOutput, calls=%fused_computation.4 | convolution fusion | flops 68550656 | bytes 2228224 | tf_op jit(solution)/shard_map/dot_general | solution.py:178
  (45 shorter events, 3.5 us)
Async XLA Ops:
  0.0 1.6 %copy-start = (bf16[2,1024,512]{2,1,0:T(8,128)(2,1)S(1)}, bf16[2,1024,512]{2,1,0:T(8,128)(2,1)}, u32[]{:S(2)}) copy-start(bf16[2,1024,512]{2,1,0:T(8,128)(2,1)} %param.5) | copy-start | bytes 6291460
  0.0 9.2 %copy-start.9 = (u32[256]{0:T(256)S(1)}, u32[256]{0:T(256)}, u32[]{:S(2)}) copy-start(u32[256]{0:T(256)} %constant.77) | copy-start | bytes 3076
  15.3 16.4 %copy-start.3 = (s32[8]{0:T(128)S(1)}, s32[8]{0:T(128)}, u32[]{:S(2)}) copy-start(s32[8]{0:T(128)} %param.6) | copy-start | bytes 100
  15.3 16.6 %copy-start.8 = (bf16[2,31]{1,0:T(2,128)(2,1)S(1)}, bf16[2,31]{1,0:T(2,128)(2,1)}, u32[]{:S(2)}) copy-start(bf16[2,31]{1,0:T(2,128)(2,1)} %param.9) | copy-start | bytes 376
  15.3 17.6 %copy-start.2 = (s32[256,8]{0,1:T(8,128)S(1)}, s32[256,8]{0,1:T(8,128)}, u32[]{:S(2)}) copy-start(s32[256,8]{0,1:T(8,128)} %param.8) | copy-start | bytes 24580
  17.9 46.0 %all-to-all-start = ((bf16[128,2,2112]{2,1,0:T(2,128)(2,1)}), bf16[128,2,2112]{2,1,0:T(2,128)(2,1)S(1)}, u32[]{:S(2)}, u32[]{:S(2)}) async-start(bf16[128,2,2112]{2,1,0:T(2,128)(2,1)} %reshape.396), calls=%async_computation | async-start | bytes 2228224 | tf_op jit(solution)/shard_map/all_to_all | solution.py:135
  36.0 3.1 %copy-start.7 = (pred[542]{0:T(1024)(128)(4,1)S(1)}, pred[542]{0:T(1024)(128)(4,1)}, u32[]{:S(2)}) copy-start(pred[542]{0:T(1024)(128)(4,1)} %fusion.29) | copy-start | bytes 1630
  36.0 3.6 %copy-start.4 = (f32[2]{0:T(128)S(1)}, f32[2]{0:T(128)}, u32[]{:S(2)}) copy-start(f32[2]{0:T(128)} %get-tuple-element.33) | copy-start | bytes 28
  36.0 3.6 %copy-start.5 = (f32[2]{0:T(128)S(1)}, f32[2]{0:T(128)}, u32[]{:S(2)}) copy-start(f32[2]{0:T(128)} %get-tuple-element.34) | copy-start | bytes 28
  36.0 3.6 %copy-start.6 = (f32[2]{0:T(128)S(1)}, f32[2]{0:T(128)}, u32[]{:S(2)}) copy-start(f32[2]{0:T(128)} %get-tuple-element.35) | copy-start | bytes 28
  38.7 1.2 %copy-start.1 = (s32[2,8,128,32]{3,2,1,0:T(8,128)S(1)}, s32[2,8,128,32]{3,2,1,0:T(8,128)}, u32[]{:S(2)}) copy-start(s32[2,8,128,32]{3,2,1,0:T(8,128)} %copy.57) | copy-start | bytes 786436

commit v7 on v6

--- a/solution.py
+++ b/solution.py
@@ -37,9 +37,7 @@
 def multiply_kernel(
     incoming_ref, counts_ref, out_ref, qt_ref, acc_ref, recv_ref, sems, *, local_bins, shot_dev, receiver_dev, groups
 ):
-    near = local_bins * 2 * shot_dev * receiver_dev
-    width = shot_dev * groups
-    qt_ref[...] = incoming_ref[:, 0:near].astype(jnp.float32).T
+    qt_ref[...] = incoming_ref[0].astype(jnp.float32).T
     me = lax.axis_index("shot")
     half = lax.axis_index("freq")
     block = 16
@@ -54,10 +52,10 @@
                     real_sum = None
                     imag_sum = None
                     for h in range(shot_dev):
-                        base_r = near + ((f * 2 + 0) * shot_dev + i) * width + h * groups
-                        base_i = near + ((f * 2 + 1) * shot_dev + i) * width + h * groups
-                        pr = incoming_ref[rows, base_r : base_r + groups].astype(jnp.float32)
-                        pi = incoming_ref[rows, base_i : base_i + groups].astype(jnp.float32)
+                        slab_r = 1 + ((f * 2 + 0) * shot_dev + i) * shot_dev + h
+                        slab_i = 1 + ((f * 2 + 1) * shot_dev + i) * shot_dev + h
+                        pr = incoming_ref[slab_r, rows, :].astype(jnp.float32)
+                        pi = incoming_ref[slab_i, rows, :].astype(jnp.float32)
                         row_r = ((f * 2 + 0) * shot_dev + h) * receiver_dev + r
                         row_i = ((f * 2 + 1) * shot_dev + h) * receiver_dev + r
                         qr = qt_ref[row_r : row_r + 1, :]
@@ -131,8 +129,15 @@
     stations = jnp.concatenate(
         [spectra[:, :, :, 0 :: 2 * stride], spectra[:, :, :, stride :: 2 * stride]], axis=-1
     ).reshape(1, rows * shots)
-    outgoing = jnp.concatenate([near, jnp.broadcast_to(stations, (groups, rows * shots))], axis=1)
-    incoming = lax.all_to_all(outgoing, "shot", 0, 0, tiled=True)
+    lanes = 128
+    outgoing = jnp.concatenate(
+        [
+            near.reshape(groups, rows * receiver_dev // lanes, lanes).transpose(1, 0, 2),
+            jnp.broadcast_to(stations.reshape(rows * shots // lanes, 1, lanes), (rows * shots // lanes, groups, lanes)),
+        ],
+        axis=0,
+    )
+    incoming = lax.all_to_all(outgoing, "shot", 1, 1, tiled=True)
     used = jnp.arange(KMAX, dtype=jnp.int32)[None, None, :] < lengths[:, :, None]
     codes = jnp.where(used, (aperture % shot_dev) * groups + aperture // shot_dev, -1)
     codes = codes.reshape(groups, shot_dev, receiver_dev, KMAX).transpose(1, 2, 0, 3)

time: 99 us -> 94.5 us (0.955)
  local copies, waits for them, and re-layouts: 20.6 us -> 12.9 us
  waiting for transfers between devices: 9.43 us -> 13.3 us
    unnamed x25 -> x13, local copies, waits for them, and re-layouts: 10.2 us -> 1.33 us
    all_to_all x1, waiting for transfers between devices: 9.43 us -> 13.3 us  [shards(): incoming = lax.all_to_all(outgoing, 'shot', 1, 1, tiled=True)]
    all_to_all x2 -> x0, other arithmetic: 2.22 us -> none  [shards(): incoming = lax.all_to_all(outgoing, 'shot', 0, 0, tiled=True)]
    concatenate x0 -> x1, other arithmetic: none -> 1.68 us  [shards(): jnp.concatenate([near.reshape(groups, rows * receiver_dev // lanes, lanes...]
  transfers between devices with their start and end apart: 1 -> 1, of which waited for: 1 -> 1; matrix products, arithmetic and copies ran while one was open for 23% -> 25% of each run, Pallas kernels for 0% -> 0%
where the time goes in v7:
time: 94.5 us; the launch traced here: 92.8 us
  other arithmetic  20.5 us (22%)
  Pallas kernels  19 us (20%)
  starting transfers between devices  13.8 us (15%)
  waiting for transfers between devices  13.3 us (14%)
  local copies, waits for them, and re-layouts  12.9 us (14%)
  blocking collectives  9.66 us (10%)
  matrix products  2.72 us (3%)
    pallas_call x1, Pallas kernels, shards(): pl.pallas_call(kernel, out_shape=jax.ShapeDtypeStruct((groups, rows * rec...  19 us
    reduce_sum x1, other arithmetic, shards(): jnp.sum((codes[..., None] == jnp.arange(shots, dtype=jnp.int32)).astype(j...  14.7 us
    all_to_all x1, starting transfers between devices, shards(): incoming = lax.all_to_all(outgoing, 'shot', 1, 1, tiled=True)  13.8 us
    all_to_all x1, waiting for transfers between devices, shards(): incoming = lax.all_to_all(outgoing, 'shot', 1, 1, tiled=True)  13.3 us
    unnamed x1, blocking collectives  6.93 us
    all_gather x1, blocking collectives, shards(): lax.all_gather(back.astype(jnp.bfloat16), 'freq', axis=0, tiled=False)  2.73 us
    transpose x1, local copies, waits for them, and re-layouts, shards(): codes.reshape(groups, shot_dev, receiver_dev, KMAX).transpose(1, 2, 0, 3)  2.56 us
    select_n x1, local copies, waits for them, and re-layouts, shards(): jnp.where(used, aperture % shot_dev * groups + aperture // shot_dev, -1)  2.27 us
  transfers between devices with their start and end apart: 1, of which 1 were waited for; matrix products, arithmetic and copies ran while one was open for 25% of the time, Pallas kernels for 0%

profile of v7, /device:TPU:1, one launch (start us, length us, event | category | flops | bytes accessed | tf_op | source)
XLA Modules:
  0.0 92.8 jit_solution(12039992526644260355)
XLA Ops:
  0.0 1.0 %fusion.25 = (f32[8,1,512]{2,0,1:T(8,128)S(1)}, f32[8,1,512]{2,0,1:T(8,128)S(1)}) fusion(s32[512]{0:T(512)S(1)} %iota_add_fusion.1, s32[8]{0:T(128)} %param.6), kind=kLoop, calls=%fused_computation.55 | loop fusion | flops 61440 | bytes 34848 | tf_op jit(solution)/shard_map/cos | solution.py:34
  1.0 0.6 copy-done
  1.6 0.6 fusion
  2.2 6.9 %all-reduce.2 = bf16[8,2,2,1024]{3,0,2,1:T(8,128)(2,1)S(1)} all-reduce(f32[8,2,2,1024]{3,0,2,1:T(8,128)S(1)} %fusion), channel_id=3, replica_groups=mesh['shot'=128,'freq'=2] {'freq'}, use_global_device_ids=true, to_apply=%region_0.1.clone | all-reduce | flops 32768 | bytes 196608
  9.2 0.6 dynamic-slice
  10.5 0.5 slice.193
  11.0 0.5 slice.192
  11.5 0.6 reshape.345
  12.7 1.7 %pad_maximum_fusion = bf16[33,128,128]{2,0,1:T(8,128)(2,1)} fusion(bf16[32,128,128]{2,0,1:T(8,128)(2,1)S(1)} %broadcast_in_dim.15, bf16[1,128,128]{2,0,1:T(2,128)(2,1)S(1)} %copy.46), kind=kLoop, calls=%fused_computation.5 | loop fusion | flops 2162688 | bytes 2162688 | tf_op jit(solution)/shard_map/concatenate | solution.py:133
  14.3 13.8 %all-to-all-start = ((bf16[33,128,128]{2,0,1:T(8,128)(2,1)}), bf16[33,128,128]{2,0,1:T(8,128)(2,1)S(1)}, u32[]{:S(2)}, u32[]{:S(2)}) async-start(bf16[33,128,128]{2,0,1:T(8,128)(2,1)} %pad_maximum_fusion), calls=%async_computation | async-start | bytes 2621440 | tf_op jit(solution)/shard_map/all_to_all | solution.py:140
  28.3 0.4 slice_reduce_fusion.29
  28.7 1.9 %fusion.4 = s32[256,8,32]{0,2,1:T(8,128)} fusion(s32[256,8,32]{0,2,1:T(8,128)} %param.7, s32[256,8]{0,1:T(8,128)S(1)} %copy-done.2), kind=kLoop, calls=%fused_computation.13 | loop fusion | flops 1507328 | bytes 532480 | tf_op jit(solution)/shard_map/jit(_where)/select_n | solution.py:142
  30.7 2.3 %copy.47 = s32[256,8,32]{2,1,0:T(8,128)} copy(s32[256,8,32]{0,2,1:T(8,128)} %fusion.4) | data formatting | bytes 524288 | tf_op jit(solution)/shard_map/jit(_where)/select_n | solution.py:142
  32.9 2.6 %copy.48 = s32[2,8,128,32]{3,2,1,0:T(8,128)} copy(s32[2,8,128,32]{3,1,0,2:T(8,128)} %bitcast.21) | data formatting | bytes 524288 | tf_op jit(solution)/shard_map/transpose | solution.py:143
  35.6 0.5 slice_reduce_fusion.30
  36.8 14.7 %convert_reduce_fusion.counts_ref = f32[2,8,128,256]{3,2,1,0:T(8,128)} fusion(s32[2,8,128,32]{3,2,1,0:T(8,128)S(1)} %copy-done.1), kind=kLoop, calls=%fused_computation | loop fusion | flops 49807360 | bytes 2359296 | tf_op jit(solution)/shard_map/reduce_sum | solution.py:144
  51.4 13.3 %all-to-all-done = bf16[33,128,128]{2,0,1:T(8,128)(2,1)S(1)} async-done(((bf16[33,128,128]{2,0,1:T(8,128)(2,1)}), bf16[33,128,128]{2,0,1:T(8,128)(2,1)S(1)}, u32[]{:S(2)}, u32[]{:S(2)}) %all-to-all-start) | async-done | bytes 1081376 | tf_op jit(solution)/shard_map/all_to_all | solution.py:140
  64.7 1.2 %copy.49.incoming_ref = bf16[33,128,128]{2,1,0:T(8,128)(2,1)} copy(bf16[33,128,128]{2,0,1:T(8,128)(2,1)S(1)} %all-to-all-done) | data formatting | bytes 2162688 | tf_op jit(solution)/shard_map/all_to_all | solution.py:140
  66.0 19.0 %shard_map.55 = f32[128,128]{1,0:T(8,128)} custom-call(bf16[33,128,128]{2,1,0:T(8,128)(2,1)} %copy.49.incoming_ref, f32[2,8,128,256]{3,2,1,0:T(8,128)} %convert_reduce_fusion.counts_ref), custom_call_target="tpu_custom_call" | custom-call | flops 33554432 | bytes 4194304 | tf_op jit(solution)/shard_map/pallas_call | solution.py:150
  85.0 0.8 convert_element_type.71
  85.9 2.7 %all-gather = bf16[256,128]{1,0:T(8,128)(2,1)S(1)} all-gather(bf16[128,128]{1,0:T(8,128)(2,1)S(1)} %convert_element_type.71), channel_id=2, replica_groups=mesh['shot'=128,'freq'=2] {'freq'}, dimensions={0}, use_global_device_ids=true | all-gather | bytes 98304 | tf_op jit(solution)/shard_map/all_gather | solution.py:166
  88.7 0.5 copy.51
  89.2 1.5 %reshape.348 = bf16[2,1024,16]{1,2,0:T(8,128)(2,1)S(1)} reshape(bf16[2,128,8,2,4,2]{2,1,5,4,3,0:T(8,128)(2,1)S(1)} %copy.51) | data formatting | bytes 131072 | tf_op jit(solution)/shard_map/reshape | solution.py:168
  90.7 2.1 %convolution_convert_fusion = bf16[2,1024,512]{2,1,0:T(8,128)(2,1)} fusion(bf16[2,1024,16]{1,2,0:T(8,128)(2,1)S(1)} %reshape.348, bf16[2,16,512]{2,1,0:T(8,128)(2,1)S(1)} %get-tuple-element.36, bf16[2,16,512]{2,1,0:T(8,128)(2,1)S(1)} %get-tuple-element.37), kind=kOutput, calls=%fused_computation.4 | convolution fusion | flops 68550656 | bytes 2228224 | tf_op jit(solution)/shard_map/dot_general | solution.py:183
  (33 shorter events, 1.6 us)
Async XLA Ops:
  0.0 1.6 %copy-start = (bf16[2,1024,512]{2,1,0:T(8,128)(2,1)S(1)}, bf16[2,1024,512]{2,1,0:T(8,128)(2,1)}, u32[]{:S(2)}) copy-start(bf16[2,1024,512]{2,1,0:T(8,128)(2,1)} %param.5) | copy-start | bytes 6291460
  0.0 9.2 %copy-start.5 = (u32[256]{0:T(256)S(1)}, u32[256]{0:T(256)}, u32[]{:S(2)}) copy-start(u32[256]{0:T(256)} %constant.77) | copy-start | bytes 3076
  12.6 15.5 %copy-start.3 = (s32[8]{0:T(128)S(1)}, s32[8]{0:T(128)}, u32[]{:S(2)}) copy-start(s32[8]{0:T(128)} %param.6) | copy-start | bytes 100
  12.6 15.7 %copy-start.4 = (bf16[2,31]{1,0:T(2,128)(2,1)S(1)}, bf16[2,31]{1,0:T(2,128)(2,1)}, u32[]{:S(2)}) copy-start(bf16[2,31]{1,0:T(2,128)(2,1)} %param.9) | copy-start | bytes 376
  12.7 16.1 %copy-start.2 = (s32[256,8]{0,1:T(8,128)S(1)}, s32[256,8]{0,1:T(8,128)}, u32[]{:S(2)}) copy-start(s32[256,8]{0,1:T(8,128)} %param.8) | copy-start | bytes 24580
  14.3 50.4 %all-to-all-start = ((bf16[33,128,128]{2,0,1:T(8,128)(2,1)}), bf16[33,128,128]{2,0,1:T(8,128)(2,1)S(1)}, u32[]{:S(2)}, u32[]{:S(2)}) async-start(bf16[33,128,128]{2,0,1:T(8,128)(2,1)} %pad_maximum_fusion), calls=%async_computation | async-start | bytes 2621440 | tf_op jit(solution)/shard_map/all_to_all | solution.py:140
  35.6 1.2 %copy-start.1 = (s32[2,8,128,32]{3,2,1,0:T(8,128)S(1)}, s32[2,8,128,32]{3,2,1,0:T(8,128)}, u32[]{:S(2)}) copy-start(s32[2,8,128,32]{3,2,1,0:T(8,128)} %copy.48) | copy-start | bytes 786436

commit v8 on v7

--- a/solution.py
+++ b/solution.py
@@ -42,8 +42,10 @@
     half = lax.axis_index("freq")
     block = 16
 
+    steps = groups // block
+
     def chunk(step, carry):
-        top = pl.multiple_of(step * block, block)
+        top = pl.multiple_of(lax.rem(step + me, steps) * block, block)
         rows = pl.ds(top, block)
         for i in range(shot_dev):
             for r in range(receiver_dev):
@@ -90,7 +92,7 @@
 
         return carry
 
-    lax.fori_loop(0, groups // block, chunk, 0)
+    lax.fori_loop(0, steps, chunk, 0)
     every = pltpu.make_async_remote_copy(
         src_ref=acc_ref.at[pl.ds(0, groups - 1)],
         dst_ref=recv_ref.at[pl.ds(0, groups - 1)],
@@ -121,9 +123,12 @@
     term = lax.dot_general(
         basis_rows, flat_traces, (((1,), (1,)), ((), ())), preferred_element_type=jnp.float32
     )
-    spectra = lax.psum_scatter(
-        term.reshape(NF, 2, shot_dev, receivers), "freq", scatter_dimension=0, tiled=True
-    ).astype(jnp.bfloat16)
+    term = term.reshape(NF, 2, shot_dev, receivers)
+    core = lax.axis_index("freq")
+    mine = lax.dynamic_slice_in_dim(term, core * local_bins, local_bins, axis=0)
+    theirs = lax.dynamic_slice_in_dim(term, (1 - core) * local_bins, local_bins, axis=0)
+    theirs = lax.ppermute(theirs, "freq", [(0, 1), (1, 0)])
+    spectra = (mine + theirs).astype(jnp.bfloat16)
     rows = local_bins * 2 * shot_dev
     near = spectra.reshape(rows, groups, receiver_dev).transpose(1, 0, 2).reshape(groups, rows * receiver_dev)
     stations = jnp.concatenate(

time: 94.5 us -> 92.2 us (0.976); the launches traced: 92.8 us -> 91.9 us
  blocking collectives: 9.66 us -> 2.72 us
  starting transfers between devices: 13.8 us -> 17.1 us
  waiting for transfers between devices: 13.3 us -> 16 us
  Pallas kernels: 19 us -> 21.3 us
    unnamed x1 -> x0, blocking collectives: 6.93 us -> none
    ppermute x0 -> x1, starting transfers between devices: none -> 3.33 us  [shards(): theirs = lax.ppermute(theirs, 'freq', [(0, 1), (1, 0)])]
    all_to_all x1, waiting for transfers between devices: 13.3 us -> 16 us  [shards(): incoming = lax.all_to_all(outgoing, 'shot', 1, 1, tiled=True)]
    pallas_call x1, Pallas kernels: 19 us -> 21.3 us  [shards(): pl.pallas_call(kernel, out_shape=jax.ShapeDtypeStruct((groups, rows * rec...]
    select_n x1, other arithmetic: 1.93 us -> 0.98 us  [shards(): jnp.where(used, aperture % shot_dev * groups + aperture // shot_dev, -1)]
  transfers between devices with their start and end apart: 1 -> 2, of which waited for: 1 -> 1; matrix products, arithmetic and copies ran while one was open for 25% -> 24% of each run, Pallas kernels for 0% -> 0%
where the time goes in v8:
time: 92.2 us; the launch traced here: 91.9 us
  Pallas kernels  21.3 us (23%)
  other arithmetic  19.6 us (21%)
  starting transfers between devices  17.1 us (19%)
  waiting for transfers between devices  16 us (17%)
  local copies, waits for them, and re-layouts  12.2 us (13%)
  matrix products  2.72 us (3%)
  blocking collectives  2.72 us (3%)
    pallas_call x1, Pallas kernels, shards(): pl.pallas_call(kernel, out_shape=jax.ShapeDtypeStruct((groups, rows * rec...  21.3 us
    all_to_all x1, waiting for transfers between devices, shards(): incoming = lax.all_to_all(outgoing, 'shot', 1, 1, tiled=True)  16 us
    reduce_sum x1, other arithmetic, shards(): jnp.sum((codes[..., None] == jnp.arange(shots, dtype=jnp.int32)).astype(j...  14.7 us
    all_to_all x1, starting transfers between devices, shards(): incoming = lax.all_to_all(outgoing, 'shot', 1, 1, tiled=True)  13.8 us
    ppermute x1, starting transfers between devices, shards(): theirs = lax.ppermute(theirs, 'freq', [(0, 1), (1, 0)])  3.33 us
    all_gather x1, blocking collectives, shards(): lax.all_gather(back.astype(jnp.bfloat16), 'freq', axis=0, tiled=False)  2.72 us
    transpose x1, local copies, waits for them, and re-layouts, shards(): codes.reshape(groups, shot_dev, receiver_dev, KMAX).transpose(1, 2, 0, 3)  2.56 us
    select_n x1, local copies, waits for them, and re-layouts, shards(): jnp.where(used, aperture % shot_dev * groups + aperture // shot_dev, -1)  2.27 us
  transfers between devices with their start and end apart: 2, of which 1 were waited for; matrix products, arithmetic and copies ran while one was open for 24% of the time, Pallas kernels for 0%

profile of v8, /device:TPU:1, one launch (start us, length us, event | category | flops | bytes accessed | tf_op | source)
XLA Modules:
  0.0 91.9 jit_solution(17487749333313126518)
XLA Ops:
  0.1 1.0 %fusion.25 = (f32[8,1,512]{2,0,1:T(8,128)S(1)}, f32[8,1,512]{2,0,1:T(8,128)S(1)}) fusion(s32[512]{0:T(512)S(1)} %iota_add_fusion.1, s32[8]{0:T(128)} %param.6), kind=kLoop, calls=%fused_computation.55 | loop fusion | flops 61440 | bytes 34848 | tf_op jit(solution)/shard_map/cos | solution.py:34
  1.0 0.6 copy-done
  1.6 0.6 fusion
  2.3 3.3 %collective-permute-start = (f32[4,2,2,1024]{3,0,2,1:T(4,128)S(1)}, f32[4,2,2,1024]{3,0,2,1:T(4,128)S(1)}, u32[]{:S(2)}, u32[]{:S(2)}) collective-permute-start(f32[4,2,2,1024]{3,0,2,1:T(4,128)S(1)} %constant_dynamic-slice_fusion), channel_id=1, source_target_pairs={{0,1},{1,0},{2,3},{3,2},{4,5},{5,4},{6,7},{7,6},{8,9},{9,8},{10,11... | collective-permute-start | bytes 196616 | tf_op jit(solution)/shard_map/ppermute | solution.py:130
  5.8 1.0 %fusion.4 = s32[256,8,32]{0,2,1:T(8,128)} fusion(s32[256,8,32]{0,2,1:T(8,128)S(1)} %copy-done.2, s32[256,8]{0,1:T(8,128)S(1)} %copy-done.3), kind=kLoop, calls=%fused_computation.13 | loop fusion | flops 1507328 | bytes 532480 | tf_op jit(solution)/shard_map/jit(_where)/select_n | solution.py:147
  6.8 0.4 slice_reduce_fusion.29
  7.2 0.5 slice.193
  7.7 0.5 slice.192
  8.3 0.6 reshape.345
  9.4 1.7 %pad_maximum_fusion = bf16[33,128,128]{2,0,1:T(8,128)(2,1)} fusion(bf16[32,128,128]{2,0,1:T(8,128)(2,1)S(1)} %broadcast_in_dim.15, bf16[1,128,128]{2,0,1:T(2,128)(2,1)S(1)} %copy.46), kind=kLoop, calls=%fused_computation.5 | loop fusion | flops 2162688 | bytes 2162688 | tf_op jit(solution)/shard_map/concatenate | solution.py:138
  11.1 13.8 %all-to-all-start = ((bf16[33,128,128]{2,0,1:T(8,128)(2,1)}), bf16[33,128,128]{2,0,1:T(8,128)(2,1)S(1)}, u32[]{:S(2)}, u32[]{:S(2)}) async-start(bf16[33,128,128]{2,0,1:T(8,128)(2,1)} %pad_maximum_fusion), calls=%async_computation | async-start | bytes 2621440 | tf_op jit(solution)/shard_map/all_to_all | solution.py:145
  24.9 2.3 %copy.47 = s32[256,8,32]{2,1,0:T(8,128)} copy(s32[256,8,32]{0,2,1:T(8,128)} %fusion.4) | data formatting | bytes 524288 | tf_op jit(solution)/shard_map/jit(_where)/select_n | solution.py:147
  27.1 2.6 %copy.48 = s32[2,8,128,32]{3,2,1,0:T(8,128)} copy(s32[2,8,128,32]{3,1,0,2:T(8,128)} %bitcast.20) | data formatting | bytes 524288 | tf_op jit(solution)/shard_map/transpose | solution.py:148
  29.8 0.5 slice_reduce_fusion.30
  30.6 0.2 subtract_convert_fusion
  31.0 14.7 %convert_reduce_fusion.counts_ref = f32[2,8,128,256]{3,2,1,0:T(8,128)} fusion(s32[2,8,128,32]{3,2,1,0:T(8,128)S(1)} %copy-done.1), kind=kLoop, calls=%fused_computation | loop fusion | flops 49807360 | bytes 2359296 | tf_op jit(solution)/shard_map/reduce_sum | solution.py:149
  45.6 16.0 %all-to-all-done = bf16[33,128,128]{2,0,1:T(8,128)(2,1)S(1)} async-done(((bf16[33,128,128]{2,0,1:T(8,128)(2,1)}), bf16[33,128,128]{2,0,1:T(8,128)(2,1)S(1)}, u32[]{:S(2)}, u32[]{:S(2)}) %all-to-all-start) | async-done | bytes 1081376 | tf_op jit(solution)/shard_map/all_to_all | solution.py:145
  61.6 1.2 %copy.49.incoming_ref = bf16[33,128,128]{2,1,0:T(8,128)(2,1)} copy(bf16[33,128,128]{2,0,1:T(8,128)(2,1)S(1)} %all-to-all-done) | data formatting | bytes 2162688 | tf_op jit(solution)/shard_map/all_to_all | solution.py:145
  62.8 21.3 %shard_map.55 = f32[128,128]{1,0:T(8,128)} custom-call(bf16[33,128,128]{2,1,0:T(8,128)(2,1)} %copy.49.incoming_ref, f32[2,8,128,256]{3,2,1,0:T(8,128)} %convert_reduce_fusion.counts_ref), custom_call_target="tpu_custom_call" | custom-call | flops 33554432 | bytes 4194304 | tf_op jit(solution)/shard_map/pallas_call | solution.py:155
  84.1 0.8 convert_element_type.71
  85.0 2.7 %all-gather = bf16[256,128]{1,0:T(8,128)(2,1)S(1)} all-gather(bf16[128,128]{1,0:T(8,128)(2,1)S(1)} %convert_element_type.71), channel_id=2, replica_groups=mesh['shot'=128,'freq'=2] {'freq'}, dimensions={0}, use_global_device_ids=true | all-gather | bytes 98304 | tf_op jit(solution)/shard_map/all_gather | solution.py:171
  87.8 0.5 copy.51
  88.3 1.5 %reshape.348 = bf16[2,1024,16]{1,2,0:T(8,128)(2,1)S(1)} reshape(bf16[2,128,8,2,4,2]{2,1,5,4,3,0:T(8,128)(2,1)S(1)} %copy.51) | data formatting | bytes 131072 | tf_op jit(solution)/shard_map/reshape | solution.py:173
  89.8 2.1 %convolution_convert_fusion = bf16[2,1024,512]{2,1,0:T(8,128)(2,1)} fusion(bf16[2,1024,16]{1,2,0:T(8,128)(2,1)S(1)} %reshape.348, bf16[2,16,512]{2,1,0:T(8,128)(2,1)S(1)} %get-tuple-element.36, bf16[2,16,512]{2,1,0:T(8,128)(2,1)S(1)} %get-tuple-element.37), kind=kOutput, calls=%fused_computation.4 | convolution fusion | flops 68550656 | bytes 2228224 | tf_op jit(solution)/shard_map/dot_general | solution.py:188
  (34 shorter events, 1.4 us)
Async XLA Ops:
  0.0 1.6 %copy-start = (bf16[2,1024,512]{2,1,0:T(8,128)(2,1)S(1)}, bf16[2,1024,512]{2,1,0:T(8,128)(2,1)}, u32[]{:S(2)}) copy-start(bf16[2,1024,512]{2,1,0:T(8,128)(2,1)} %param.5) | copy-start | bytes 6291460
  0.0 5.6 %copy-start.4 = (s32[8]{0:T(128)S(1)}, s32[8]{0:T(128)}, u32[]{:S(2)}) copy-start(s32[8]{0:T(128)} %param.6) | copy-start | bytes 100
  0.0 5.8 %copy-start.5 = (bf16[2,31]{1,0:T(2,128)(2,1)S(1)}, bf16[2,31]{1,0:T(2,128)(2,1)}, u32[]{:S(2)}) copy-start(bf16[2,31]{1,0:T(2,128)(2,1)} %param.9) | copy-start | bytes 376
  0.0 5.8 %copy-start.2 = (s32[256,8,32]{0,2,1:T(8,128)S(1)}, s32[256,8,32]{0,2,1:T(8,128)}, u32[]{:S(2)}) copy-start(s32[256,8,32]{0,2,1:T(8,128)} %param.7) | copy-start | bytes 786436
  0.0 5.8 %copy-start.3 = (s32[256,8]{0,1:T(8,128)S(1)}, s32[256,8]{0,1:T(8,128)}, u32[]{:S(2)}) copy-start(s32[256,8]{0,1:T(8,128)} %param.8) | copy-start | bytes 24580
  2.3 4.9 %collective-permute-start = (f32[4,2,2,1024]{3,0,2,1:T(4,128)S(1)}, f32[4,2,2,1024]{3,0,2,1:T(4,128)S(1)}, u32[]{:S(2)}, u32[]{:S(2)}) collective-permute-start(f32[4,2,2,1024]{3,0,2,1:T(4,128)S(1)} %constant_dynamic-slice_fusion), channel_id=1, source_target_pairs={{0,1},{1,0},{2,3},{3,2},{4,5},{5,4},{6,7},{7,6},{8,9},{9,8},{10,11... | collective-permute-start | bytes 196616 | tf_op jit(solution)/shard_map/ppermute | solution.py:130
  11.1 50.5 %all-to-all-start = ((bf16[33,128,128]{2,0,1:T(8,128)(2,1)}), bf16[33,128,128]{2,0,1:T(8,128)(2,1)S(1)}, u32[]{:S(2)}, u32[]{:S(2)}) async-start(bf16[33,128,128]{2,0,1:T(8,128)(2,1)} %pad_maximum_fusion), calls=%async_computation | async-start | bytes 2621440 | tf_op jit(solution)/shard_map/all_to_all | solution.py:145
  29.7 1.2 %copy-start.1 = (s32[2,8,128,32]{3,2,1,0:T(8,128)S(1)}, s32[2,8,128,32]{3,2,1,0:T(8,128)}, u32[]{:S(2)}) copy-start(s32[2,8,128,32]{3,2,1,0:T(8,128)} %copy.48) | copy-start | bytes 786436

commit v9 on v8

--- a/solution.py
+++ b/solution.py
@@ -103,7 +103,7 @@
     )
     every.wait_send()
     every.wait_recv()
-    out_ref[...] = recv_ref[...]
+    out_ref[...] = recv_ref[...].astype(out_ref.dtype)
 
 
 def shards(traces, frequency_bins, aperture, lengths, filters):
@@ -154,7 +154,7 @@
     )
     back = pl.pallas_call(
         kernel,
-        out_shape=jax.ShapeDtypeStruct((groups, rows * receiver_dev), jnp.float32),
+        out_shape=jax.ShapeDtypeStruct((groups, rows * receiver_dev), jnp.bfloat16),
         in_specs=[pl.BlockSpec(memory_space=pltpu.VMEM)] * 2,
         out_specs=pl.BlockSpec(memory_space=pltpu.VMEM),
         scratch_shapes=[
@@ -168,7 +168,7 @@
             flops=16 * groups * shots * rows * receiver_dev // 2, transcendentals=0, bytes_accessed=4 * 1024 * 1024
         ),
     )(incoming, counts)
-    piece = lax.all_gather(back.astype(jnp.bfloat16), "freq", axis=0, tiled=False)
+    piece = lax.all_gather(back, "freq", axis=0, tiled=False)
     piece = piece.reshape(freq_dev, groups, local_bins, 2, shot_dev, receiver_dev)
     piece = piece.transpose(4, 1, 5, 0, 2, 3).reshape(shot_dev, receivers, NF * 2)
     wide = time_dev + 2 * half_taps

time: 92.2 us -> 91.6 us (level)
  no operation moved by 1% of the time
where the time goes in v9:
time: 91.6 us; the launch traced here: 91.2 us
  Pallas kernels  21.3 us (23%)
  other arithmetic  18.8 us (21%)
  starting transfers between devices  17.1 us (19%)
  waiting for transfers between devices  16 us (17%)
  local copies, waits for them, and re-layouts  12.2 us (13%)
  blocking collectives  2.94 us (3%)
  matrix products  2.72 us (3%)
    pallas_call x1, Pallas kernels, shards(): pl.pallas_call(kernel, out_shape=jax.ShapeDtypeStruct((groups, rows * rec...  21.3 us
    all_to_all x1, waiting for transfers between devices, shards(): incoming = lax.all_to_all(outgoing, 'shot', 1, 1, tiled=True)  16 us
    reduce_sum x1, other arithmetic, shards(): jnp.sum((codes[..., None] == jnp.arange(shots, dtype=jnp.int32)).astype(j...  14.7 us
    all_to_all x1, starting transfers between devices, shards(): incoming = lax.all_to_all(outgoing, 'shot', 1, 1, tiled=True)  13.8 us
    ppermute x1, starting transfers between devices, shards(): theirs = lax.ppermute(theirs, 'freq', [(0, 1), (1, 0)])  3.33 us
    all_gather x1, blocking collectives, shards(): piece = lax.all_gather(back, 'freq', axis=0, tiled=False)  2.94 us
    transpose x1, local copies, waits for them, and re-layouts, shards(): codes.reshape(groups, shot_dev, receiver_dev, KMAX).transpose(1, 2, 0, 3)  2.56 us
    select_n x1, local copies, waits for them, and re-layouts, shards(): jnp.where(used, aperture % shot_dev * groups + aperture // shot_dev, -1)  2.27 us
  transfers between devices with their start and end apart: 2, of which 1 were waited for; matrix products, arithmetic and copies ran while one was open for 24% of the time, Pallas kernels for 0%

profile of v9, /device:TPU:1, one launch (start us, length us, event | category | flops | bytes accessed | tf_op | source)
XLA Modules:
  0.0 91.2 jit_solution(15480916710786436201)
XLA Ops:
  0.1 1.0 %fusion.25 = (f32[8,1,512]{2,0,1:T(8,128)S(1)}, f32[8,1,512]{2,0,1:T(8,128)S(1)}) fusion(s32[512]{0:T(512)S(1)} %iota_add_fusion.1, s32[8]{0:T(128)} %param.6), kind=kLoop, calls=%fused_computation.55 | loop fusion | flops 61440 | bytes 34848 | tf_op jit(solution)/shard_map/cos | solution.py:34
  1.0 0.6 copy-done
  1.6 0.6 fusion
  2.3 3.3 %collective-permute-start = (f32[4,2,2,1024]{3,0,2,1:T(4,128)S(1)}, f32[4,2,2,1024]{3,0,2,1:T(4,128)S(1)}, u32[]{:S(2)}, u32[]{:S(2)}) collective-permute-start(f32[4,2,2,1024]{3,0,2,1:T(4,128)S(1)} %constant_dynamic-slice_fusion), channel_id=1, source_target_pairs={{0,1},{1,0},{2,3},{3,2},{4,5},{5,4},{6,7},{7,6},{8,9},{9,8},{10,11... | collective-permute-start | bytes 196616 | tf_op jit(solution)/shard_map/ppermute | solution.py:130
  5.8 1.0 %fusion.4 = s32[256,8,32]{0,2,1:T(8,128)} fusion(s32[256,8,32]{0,2,1:T(8,128)S(1)} %copy-done.2, s32[256,8]{0,1:T(8,128)S(1)} %copy-done.3), kind=kLoop, calls=%fused_computation.13 | loop fusion | flops 1507328 | bytes 532480 | tf_op jit(solution)/shard_map/jit(_where)/select_n | solution.py:147
  6.8 0.4 slice_reduce_fusion.29
  7.2 0.5 slice.193
  7.7 0.5 slice.192
  8.3 0.6 reshape.345
  9.4 1.7 %pad_maximum_fusion = bf16[33,128,128]{2,0,1:T(8,128)(2,1)} fusion(bf16[32,128,128]{2,0,1:T(8,128)(2,1)S(1)} %broadcast_in_dim.15, bf16[1,128,128]{2,0,1:T(2,128)(2,1)S(1)} %copy.46), kind=kLoop, calls=%fused_computation.5 | loop fusion | flops 2162688 | bytes 2162688 | tf_op jit(solution)/shard_map/concatenate | solution.py:138
  11.1 13.8 %all-to-all-start = ((bf16[33,128,128]{2,0,1:T(8,128)(2,1)}), bf16[33,128,128]{2,0,1:T(8,128)(2,1)S(1)}, u32[]{:S(2)}, u32[]{:S(2)}) async-start(bf16[33,128,128]{2,0,1:T(8,128)(2,1)} %pad_maximum_fusion), calls=%async_computation | async-start | bytes 2621440 | tf_op jit(solution)/shard_map/all_to_all | solution.py:145
  24.9 2.3 %copy.47 = s32[256,8,32]{2,1,0:T(8,128)} copy(s32[256,8,32]{0,2,1:T(8,128)} %fusion.4) | data formatting | bytes 524288 | tf_op jit(solution)/shard_map/jit(_where)/select_n | solution.py:147
  27.1 2.6 %copy.48 = s32[2,8,128,32]{3,2,1,0:T(8,128)} copy(s32[2,8,128,32]{3,1,0,2:T(8,128)} %bitcast.20) | data formatting | bytes 524288 | tf_op jit(solution)/shard_map/transpose | solution.py:148
  29.8 0.5 slice_reduce_fusion.30
  30.4 0.2 fusion.33
  30.6 0.2 subtract_convert_fusion
  31.0 14.7 %convert_reduce_fusion.counts_ref = f32[2,8,128,256]{3,2,1,0:T(8,128)} fusion(s32[2,8,128,32]{3,2,1,0:T(8,128)S(1)} %copy-done.1), kind=kLoop, calls=%fused_computation | loop fusion | flops 49807360 | bytes 2359296 | tf_op jit(solution)/shard_map/reduce_sum | solution.py:149
  45.6 16.0 %all-to-all-done = bf16[33,128,128]{2,0,1:T(8,128)(2,1)S(1)} async-done(((bf16[33,128,128]{2,0,1:T(8,128)(2,1)}), bf16[33,128,128]{2,0,1:T(8,128)(2,1)S(1)}, u32[]{:S(2)}, u32[]{:S(2)}) %all-to-all-start) | async-done | bytes 1081376 | tf_op jit(solution)/shard_map/all_to_all | solution.py:145
  61.6 1.2 %copy.49.incoming_ref = bf16[33,128,128]{2,1,0:T(8,128)(2,1)} copy(bf16[33,128,128]{2,0,1:T(8,128)(2,1)S(1)} %all-to-all-done) | data formatting | bytes 2162688 | tf_op jit(solution)/shard_map/all_to_all | solution.py:145
  62.8 21.3 %shard_map.55 = bf16[128,128]{1,0:T(8,128)(2,1)} custom-call(bf16[33,128,128]{2,1,0:T(8,128)(2,1)} %copy.49.incoming_ref, f32[2,8,128,256]{3,2,1,0:T(8,128)} %convert_reduce_fusion.counts_ref), custom_call_target="tpu_custom_call" | custom-call | flops 33554432 | bytes 4194304 | tf_op jit(solution)/shard_map/pallas_call | solution.py:155
  84.1 2.9 %all-gather = bf16[256,128]{1,0:T(8,128)(2,1)S(1)} all-gather(bf16[128,128]{1,0:T(8,128)(2,1)} %shard_map.55), channel_id=2, replica_groups=mesh['shot'=128,'freq'=2] {'freq'}, dimensions={0}, use_global_device_ids=true | all-gather | bytes 98304 | tf_op jit(solution)/shard_map/all_gather | solution.py:171
  87.2 0.5 copy.51
  87.7 1.5 %reshape.348 = bf16[2,1024,16]{1,2,0:T(8,128)(2,1)S(1)} reshape(bf16[2,128,8,2,4,2]{2,1,5,4,3,0:T(8,128)(2,1)S(1)} %copy.51) | data formatting | bytes 131072 | tf_op jit(solution)/shard_map/reshape | solution.py:173
  89.2 2.1 %convolution_convert_fusion = bf16[2,1024,512]{2,1,0:T(8,128)(2,1)} fusion(bf16[2,1024,16]{1,2,0:T(8,128)(2,1)S(1)} %reshape.348, bf16[2,16,512]{2,1,0:T(8,128)(2,1)S(1)} %get-tuple-element.36, bf16[2,16,512]{2,1,0:T(8,128)(2,1)S(1)} %get-tuple-element.37), kind=kOutput, calls=%fused_computation.4 | convolution fusion | flops 68550656 | bytes 2228224 | tf_op jit(solution)/shard_map/dot_general | solution.py:188
  (33 shorter events, 1.2 us)
Async XLA Ops:
  0.0 1.6 %copy-start = (bf16[2,1024,512]{2,1,0:T(8,128)(2,1)S(1)}, bf16[2,1024,512]{2,1,0:T(8,128)(2,1)}, u32[]{:S(2)}) copy-start(bf16[2,1024,512]{2,1,0:T(8,128)(2,1)} %param.5) | copy-start | bytes 6291460
  0.0 5.6 %copy-start.4 = (s32[8]{0:T(128)S(1)}, s32[8]{0:T(128)}, u32[]{:S(2)}) copy-start(s32[8]{0:T(128)} %param.6) | copy-start | bytes 100
  0.0 5.8 %copy-start.5 = (bf16[2,31]{1,0:T(2,128)(2,1)S(1)}, bf16[2,31]{1,0:T(2,128)(2,1)}, u32[]{:S(2)}) copy-start(bf16[2,31]{1,0:T(2,128)(2,1)} %param.9) | copy-start | bytes 376
  0.0 5.8 %copy-start.2 = (s32[256,8,32]{0,2,1:T(8,128)S(1)}, s32[256,8,32]{0,2,1:T(8,128)}, u32[]{:S(2)}) copy-start(s32[256,8,32]{0,2,1:T(8,128)} %param.7) | copy-start | bytes 786436
  0.0 5.8 %copy-start.3 = (s32[256,8]{0,1:T(8,128)S(1)}, s32[256,8]{0,1:T(8,128)}, u32[]{:S(2)}) copy-start(s32[256,8]{0,1:T(8,128)} %param.8) | copy-start | bytes 24580
  2.3 4.9 %collective-permute-start = (f32[4,2,2,1024]{3,0,2,1:T(4,128)S(1)}, f32[4,2,2,1024]{3,0,2,1:T(4,128)S(1)}, u32[]{:S(2)}, u32[]{:S(2)}) collective-permute-start(f32[4,2,2,1024]{3,0,2,1:T(4,128)S(1)} %constant_dynamic-slice_fusion), channel_id=1, source_target_pairs={{0,1},{1,0},{2,3},{3,2},{4,5},{5,4},{6,7},{7,6},{8,9},{9,8},{10,11... | collective-permute-start | bytes 196616 | tf_op jit(solution)/shard_map/ppermute | solution.py:130
  11.1 50.5 %all-to-all-start = ((bf16[33,128,128]{2,0,1:T(8,128)(2,1)}), bf16[33,128,128]{2,0,1:T(8,128)(2,1)S(1)}, u32[]{:S(2)}, u32[]{:S(2)}) async-start(bf16[33,128,128]{2,0,1:T(8,128)(2,1)} %pad_maximum_fusion), calls=%async_computation | async-start | bytes 2621440 | tf_op jit(solution)/shard_map/all_to_all | solution.py:145
  29.7 1.2 %copy-start.1 = (s32[2,8,128,32]{3,2,1,0:T(8,128)S(1)}, s32[2,8,128,32]{3,2,1,0:T(8,128)}, u32[]{:S(2)}) copy-start(s32[2,8,128,32]{3,2,1,0:T(8,128)} %copy.48) | copy-start | bytes 786436

commit v10 on v9

--- a/solution.py
+++ b/solution.py
@@ -44,8 +44,17 @@
 
     steps = groups // block
 
-    def chunk(step, carry):
-        top = pl.multiple_of(lax.rem(step + me, steps) * block, block)
+    def remote_send(target):
+        pltpu.make_async_remote_copy(
+            src_ref=acc_ref.at[pl.ds(target, 1)],
+            dst_ref=recv_ref.at[pl.ds(me, 1)],
+            send_sem=sems.at[0],
+            recv_sem=sems.at[1],
+            device_id=(target, half),
+            device_id_type=pl.DeviceIdType.MESH,
+        ).start()
+
+    def compute(top):
         rows = pl.ds(top, block)
         for i in range(shot_dev):
             for r in range(receiver_dev):
@@ -72,27 +81,27 @@
                     acc_ref[rows, col_r : col_r + 1] = jnp.sum(real_sum, axis=1, keepdims=True)
                     acc_ref[rows, col_i : col_i + 1] = jnp.sum(imag_sum, axis=1, keepdims=True)
         acc_ref[rows, :] = (acc_ref[rows, :] * KMAX ** (-0.5)).astype(jnp.bfloat16).astype(jnp.float32)
+
+    own_block = me // block
+    own_top = pl.multiple_of(own_block * block, block)
+    compute(own_top)
+    for t in range(block):
+        target = own_top + lax.rem(me + t, block)
+
+        @pl.when(target != me)
+        def _():
+            remote_send(target)
+
+    recv_ref[pl.ds(me, 1), :] = acc_ref[pl.ds(me, 1), :]
+
+    def chunk(step, carry):
+        top = pl.multiple_of(lax.rem(own_block + step, steps) * block, block)
+        compute(top)
         for t in range(block):
-            target = top + t
-
-            @pl.when(target != me)
-            def _():
-                pltpu.make_async_remote_copy(
-                    src_ref=acc_ref.at[pl.ds(target, 1)],
-                    dst_ref=recv_ref.at[pl.ds(me, 1)],
-                    send_sem=sems.at[0],
-                    recv_sem=sems.at[1],
-                    device_id=(target, half),
-                    device_id_type=pl.DeviceIdType.MESH,
-                ).start()
-
-            @pl.when(target == me)
-            def _():
-                recv_ref[pl.ds(me, 1), :] = acc_ref[pl.ds(me, 1), :]
-
+            remote_send(top + lax.rem(me + t, block))
         return carry
 
-    lax.fori_loop(0, steps, chunk, 0)
+    lax.fori_loop(1, steps, chunk, 0)
     every = pltpu.make_async_remote_copy(
         src_ref=acc_ref.at[pl.ds(0, groups - 1)],
         dst_ref=recv_ref.at[pl.ds(0, groups - 1)],

time: 91.6 us -> 90.8 us (level)
  no operation moved by 1% of the time
where the time goes in v10:
time: 90.8 us; the launch traced here: 90.5 us
  Pallas kernels  20.5 us (23%)
  other arithmetic  18.8 us (21%)
  starting transfers between devices  17.1 us (19%)
  waiting for transfers between devices  16 us (18%)
  local copies, waits for them, and re-layouts  12.2 us (13%)
  blocking collectives  2.95 us (3%)
  matrix products  2.71 us (3%)
    pallas_call x1, Pallas kernels, shards(): pl.pallas_call(kernel, out_shape=jax.ShapeDtypeStruct((groups, rows * rec...  20.5 us
    all_to_all x1, waiting for transfers between devices, shards(): incoming = lax.all_to_all(outgoing, 'shot', 1, 1, tiled=True)  16 us
    reduce_sum x1, other arithmetic, shards(): jnp.sum((codes[..., None] == jnp.arange(shots, dtype=jnp.int32)).astype(j...  14.7 us
    all_to_all x1, starting transfers between devices, shards(): incoming = lax.all_to_all(outgoing, 'shot', 1, 1, tiled=True)  13.8 us
    ppermute x1, starting transfers between devices, shards(): theirs = lax.ppermute(theirs, 'freq', [(0, 1), (1, 0)])  3.33 us
    all_gather x1, blocking collectives, shards(): piece = lax.all_gather(back, 'freq', axis=0, tiled=False)  2.95 us
    transpose x1, local copies, waits for them, and re-layouts, shards(): codes.reshape(groups, shot_dev, receiver_dev, KMAX).transpose(1, 2, 0, 3)  2.56 us
    select_n x1, local copies, waits for them, and re-layouts, shards(): jnp.where(used, aperture % shot_dev * groups + aperture // shot_dev, -1)  2.27 us
  transfers between devices with their start and end apart: 2, of which 1 were waited for; matrix products, arithmetic and copies ran while one was open for 24% of the time, Pallas kernels for 0%

profile of v10, /device:TPU:1, one launch (start us, length us, event | category | flops | bytes accessed | tf_op | source)
XLA Modules:
  0.0 90.5 jit_solution(2200613235692016676)
XLA Ops:
  0.1 1.0 %fusion.25 = (f32[8,1,512]{2,0,1:T(8,128)S(1)}, f32[8,1,512]{2,0,1:T(8,128)S(1)}) fusion(s32[512]{0:T(512)S(1)} %iota_add_fusion.1, s32[8]{0:T(128)} %param.6), kind=kLoop, calls=%fused_computation.55 | loop fusion | flops 61440 | bytes 34848 | tf_op jit(solution)/shard_map/cos | solution.py:34
  1.0 0.6 copy-done
  1.6 0.6 fusion
  2.3 3.3 %collective-permute-start = (f32[4,2,2,1024]{3,0,2,1:T(4,128)S(1)}, f32[4,2,2,1024]{3,0,2,1:T(4,128)S(1)}, u32[]{:S(2)}, u32[]{:S(2)}) collective-permute-start(f32[4,2,2,1024]{3,0,2,1:T(4,128)S(1)} %constant_dynamic-slice_fusion), channel_id=1, source_target_pairs={{0,1},{1,0},{2,3},{3,2},{4,5},{5,4},{6,7},{7,6},{8,9},{9,8},{10,11... | collective-permute-start | bytes 196616 | tf_op jit(solution)/shard_map/ppermute | solution.py:139
  5.8 1.0 %fusion.4 = s32[256,8,32]{0,2,1:T(8,128)} fusion(s32[256,8,32]{0,2,1:T(8,128)S(1)} %copy-done.2, s32[256,8]{0,1:T(8,128)S(1)} %copy-done.3), kind=kLoop, calls=%fused_computation.13 | loop fusion | flops 1507328 | bytes 532480 | tf_op jit(solution)/shard_map/jit(_where)/select_n | solution.py:156
  6.8 0.4 slice_reduce_fusion.29
  7.2 0.5 slice.193
  7.7 0.5 slice.192
  8.3 0.6 reshape.345
  9.4 1.7 %pad_maximum_fusion = bf16[33,128,128]{2,0,1:T(8,128)(2,1)} fusion(bf16[32,128,128]{2,0,1:T(8,128)(2,1)S(1)} %broadcast_in_dim.15, bf16[1,128,128]{2,0,1:T(2,128)(2,1)S(1)} %copy.46), kind=kLoop, calls=%fused_computation.5 | loop fusion | flops 2162688 | bytes 2162688 | tf_op jit(solution)/shard_map/concatenate | solution.py:147
  11.1 13.8 %all-to-all-start = ((bf16[33,128,128]{2,0,1:T(8,128)(2,1)}), bf16[33,128,128]{2,0,1:T(8,128)(2,1)S(1)}, u32[]{:S(2)}, u32[]{:S(2)}) async-start(bf16[33,128,128]{2,0,1:T(8,128)(2,1)} %pad_maximum_fusion), calls=%async_computation | async-start | bytes 2621440 | tf_op jit(solution)/shard_map/all_to_all | solution.py:154
  24.9 2.3 %copy.47 = s32[256,8,32]{2,1,0:T(8,128)} copy(s32[256,8,32]{0,2,1:T(8,128)} %fusion.4) | data formatting | bytes 524288 | tf_op jit(solution)/shard_map/jit(_where)/select_n | solution.py:156
  27.1 2.6 %copy.48 = s32[2,8,128,32]{3,2,1,0:T(8,128)} copy(s32[2,8,128,32]{3,1,0,2:T(8,128)} %bitcast.20) | data formatting | bytes 524288 | tf_op jit(solution)/shard_map/transpose | solution.py:157
  29.8 0.5 slice_reduce_fusion.30
  30.4 0.2 fusion.33
  30.6 0.2 subtract_convert_fusion
  31.0 14.7 %convert_reduce_fusion.counts_ref = f32[2,8,128,256]{3,2,1,0:T(8,128)} fusion(s32[2,8,128,32]{3,2,1,0:T(8,128)S(1)} %copy-done.1), kind=kLoop, calls=%fused_computation | loop fusion | flops 49807360 | bytes 2359296 | tf_op jit(solution)/shard_map/reduce_sum | solution.py:158
  45.6 16.0 %all-to-all-done = bf16[33,128,128]{2,0,1:T(8,128)(2,1)S(1)} async-done(((bf16[33,128,128]{2,0,1:T(8,128)(2,1)}), bf16[33,128,128]{2,0,1:T(8,128)(2,1)S(1)}, u32[]{:S(2)}, u32[]{:S(2)}) %all-to-all-start) | async-done | bytes 1081376 | tf_op jit(solution)/shard_map/all_to_all | solution.py:154
  61.6 1.2 %copy.49.incoming_ref = bf16[33,128,128]{2,1,0:T(8,128)(2,1)} copy(bf16[33,128,128]{2,0,1:T(8,128)(2,1)S(1)} %all-to-all-done) | data formatting | bytes 2162688 | tf_op jit(solution)/shard_map/all_to_all | solution.py:154
  62.8 20.5 %shard_map.55 = bf16[128,128]{1,0:T(8,128)(2,1)} custom-call(bf16[33,128,128]{2,1,0:T(8,128)(2,1)} %copy.49.incoming_ref, f32[2,8,128,256]{3,2,1,0:T(8,128)} %convert_reduce_fusion.counts_ref), custom_call_target="tpu_custom_call" | custom-call | flops 33554432 | bytes 4194304 | tf_op jit(solution)/shard_map/pallas_call | solution.py:164
  83.4 2.9 %all-gather = bf16[256,128]{1,0:T(8,128)(2,1)S(1)} all-gather(bf16[128,128]{1,0:T(8,128)(2,1)} %shard_map.55), channel_id=2, replica_groups=mesh['shot'=128,'freq'=2] {'freq'}, dimensions={0}, use_global_device_ids=true | all-gather | bytes 98304 | tf_op jit(solution)/shard_map/all_gather | solution.py:180
  86.5 0.5 copy.51
  86.9 1.5 %reshape.348 = bf16[2,1024,16]{1,2,0:T(8,128)(2,1)S(1)} reshape(bf16[2,128,8,2,4,2]{2,1,5,4,3,0:T(8,128)(2,1)S(1)} %copy.51) | data formatting | bytes 131072 | tf_op jit(solution)/shard_map/reshape | solution.py:182
  88.4 2.1 %convolution_convert_fusion = bf16[2,1024,512]{2,1,0:T(8,128)(2,1)} fusion(bf16[2,1024,16]{1,2,0:T(8,128)(2,1)S(1)} %reshape.348, bf16[2,16,512]{2,1,0:T(8,128)(2,1)S(1)} %get-tuple-element.36, bf16[2,16,512]{2,1,0:T(8,128)(2,1)S(1)} %get-tuple-element.37), kind=kOutput, calls=%fused_computation.4 | convolution fusion | flops 68550656 | bytes 2228224 | tf_op jit(solution)/shard_map/dot_general | solution.py:197
  (33 shorter events, 1.2 us)
Async XLA Ops:
  0.0 1.6 %copy-start = (bf16[2,1024,512]{2,1,0:T(8,128)(2,1)S(1)}, bf16[2,1024,512]{2,1,0:T(8,128)(2,1)}, u32[]{:S(2)}) copy-start(bf16[2,1024,512]{2,1,0:T(8,128)(2,1)} %param.5) | copy-start | bytes 6291460
  0.0 5.6 %copy-start.4 = (s32[8]{0:T(128)S(1)}, s32[8]{0:T(128)}, u32[]{:S(2)}) copy-start(s32[8]{0:T(128)} %param.6) | copy-start | bytes 100
  0.0 5.8 %copy-start.5 = (bf16[2,31]{1,0:T(2,128)(2,1)S(1)}, bf16[2,31]{1,0:T(2,128)(2,1)}, u32[]{:S(2)}) copy-start(bf16[2,31]{1,0:T(2,128)(2,1)} %param.9) | copy-start | bytes 376
  0.0 5.8 %copy-start.2 = (s32[256,8,32]{0,2,1:T(8,128)S(1)}, s32[256,8,32]{0,2,1:T(8,128)}, u32[]{:S(2)}) copy-start(s32[256,8,32]{0,2,1:T(8,128)} %param.7) | copy-start | bytes 786436
  0.0 5.8 %copy-start.3 = (s32[256,8]{0,1:T(8,128)S(1)}, s32[256,8]{0,1:T(8,128)}, u32[]{:S(2)}) copy-start(s32[256,8]{0,1:T(8,128)} %param.8) | copy-start | bytes 24580
  2.3 4.9 %collective-permute-start = (f32[4,2,2,1024]{3,0,2,1:T(4,128)S(1)}, f32[4,2,2,1024]{3,0,2,1:T(4,128)S(1)}, u32[]{:S(2)}, u32[]{:S(2)}) collective-permute-start(f32[4,2,2,1024]{3,0,2,1:T(4,128)S(1)} %constant_dynamic-slice_fusion), channel_id=1, source_target_pairs={{0,1},{1,0},{2,3},{3,2},{4,5},{5,4},{6,7},{7,6},{8,9},{9,8},{10,11... | collective-permute-start | bytes 196616 | tf_op jit(solution)/shard_map/ppermute | solution.py:139
  11.1 50.5 %all-to-all-start = ((bf16[33,128,128]{2,0,1:T(8,128)(2,1)}), bf16[33,128,128]{2,0,1:T(8,128)(2,1)S(1)}, u32[]{:S(2)}, u32[]{:S(2)}) async-start(bf16[33,128,128]{2,0,1:T(8,128)(2,1)} %pad_maximum_fusion), calls=%async_computation | async-start | bytes 2621440 | tf_op jit(solution)/shard_map/all_to_all | solution.py:154
  29.7 1.2 %copy-start.1 = (s32[2,8,128,32]{3,2,1,0:T(8,128)S(1)}, s32[2,8,128,32]{3,2,1,0:T(8,128)}, u32[]{:S(2)}) copy-start(s32[2,8,128,32]{3,2,1,0:T(8,128)} %copy.48) | copy-start | bytes 786436

commit v11 on v10

--- a/solution.py
+++ b/solution.py
@@ -151,6 +151,7 @@
         ],
         axis=0,
     )
+    outgoing, aperture, lengths = lax.optimization_barrier((outgoing, aperture, lengths))
     incoming = lax.all_to_all(outgoing, "shot", 1, 1, tiled=True)
     used = jnp.arange(KMAX, dtype=jnp.int32)[None, None, :] < lengths[:, :, None]
     codes = jnp.where(used, (aperture % shot_dev) * groups + aperture // shot_dev, -1)

time: 90.8 us -> 90.2 us (level)
  local copies, waits for them, and re-layouts: 12.2 us -> 11.2 us
    transpose x1, local copies, waits for them, and re-layouts: 2.56 us -> 1.56 us  [shards(): codes.reshape(groups, shot_dev, receiver_dev, KMAX).transpose(1, 2, 0, 3)]
  transfers between devices with their start and end apart: 2 -> 2, of which waited for: 1 -> 2; matrix products, arithmetic and copies ran while one was open for 24% -> 24% of each run, Pallas kernels for 0% -> 0%
where the time goes in v11:
time: 90.2 us; the launch traced here: 89.9 us
  Pallas kernels  21 us (23%)
  other arithmetic  18.7 us (21%)
  starting transfers between devices  17.1 us (19%)
  waiting for transfers between devices  16 us (18%)
  local copies, waits for them, and re-layouts  11.2 us (12%)
  blocking collectives  2.95 us (3%)
  matrix products  2.72 us (3%)
    pallas_call x1, Pallas kernels, shards(): pl.pallas_call(kernel, out_shape=jax.ShapeDtypeStruct((groups, rows * rec...  21 us
    all_to_all x1, waiting for transfers between devices, shards(): incoming = lax.all_to_all(outgoing, 'shot', 1, 1, tiled=True)  15.4 us
    reduce_sum x1, other arithmetic, shards(): jnp.sum((codes[..., None] == jnp.arange(shots, dtype=jnp.int32)).astype(j...  14.7 us
    all_to_all x1, starting transfers between devices, shards(): incoming = lax.all_to_all(outgoing, 'shot', 1, 1, tiled=True)  13.8 us
    ppermute x1, starting transfers between devices, shards(): theirs = lax.ppermute(theirs, 'freq', [(0, 1), (1, 0)])  3.33 us
    all_gather x1, blocking collectives, shards(): piece = lax.all_gather(back, 'freq', axis=0, tiled=False)  2.95 us
    select_n x1, local copies, waits for them, and re-layouts, shards(): jnp.where(used, aperture % shot_dev * groups + aperture // shot_dev, -1)  2.27 us
    dot_general x1, matrix products, shards(): lax.dot_general(jnp.concatenate([piece, piece], axis=2), jnp.concatenate(...  2.08 us
  transfers between devices with their start and end apart: 2, of which 2 were waited for; matrix products, arithmetic and copies ran while one was open for 24% of the time, Pallas kernels for 0%

profile of v11, /device:TPU:1, one launch (start us, length us, event | category | flops | bytes accessed | tf_op | source)
XLA Modules:
  0.0 89.9 jit_solution(17337207221911539952)
XLA Ops:
  0.0 1.0 %fusion.25 = (f32[8,1,512]{2,0,1:T(8,128)S(1)}, f32[8,1,512]{2,0,1:T(8,128)S(1)}) fusion(s32[512]{0:T(512)S(1)} %iota_add_fusion.1, s32[8]{0:T(128)} %param.6), kind=kLoop, calls=%fused_computation.55 | loop fusion | flops 61440 | bytes 34848 | tf_op jit(solution)/shard_map/cos | solution.py:34
  1.0 0.6 copy-done
  1.6 0.6 fusion
  2.3 3.3 %collective-permute-start = (f32[4,2,2,1024]{3,0,2,1:T(4,128)S(1)}, f32[4,2,2,1024]{3,0,2,1:T(4,128)S(1)}, u32[]{:S(2)}, u32[]{:S(2)}) collective-permute-start(f32[4,2,2,1024]{3,0,2,1:T(4,128)S(1)} %constant_dynamic-slice_fusion), channel_id=1, source_target_pairs={{0,1},{1,0},{2,3},{3,2},{4,5},{5,4},{6,7},{7,6},{8,9},{9,8},{10,11... | collective-permute-start | bytes 196616 | tf_op jit(solution)/shard_map/ppermute | solution.py:139
  5.9 0.6 collective-permute-done
  6.5 0.5 slice.193
  7.0 0.5 slice.192
  7.6 0.6 reshape.345
  8.7 1.7 %pad_maximum_fusion = bf16[33,128,128]{2,0,1:T(8,128)(2,1)} fusion(bf16[32,128,128]{2,0,1:T(8,128)(2,1)S(1)} %broadcast_in_dim.15, bf16[1,128,128]{2,0,1:T(2,128)(2,1)S(1)} %copy.46), kind=kLoop, calls=%fused_computation.5 | loop fusion | flops 2162688 | bytes 2162688 | tf_op jit(solution)/shard_map/concatenate | solution.py:147
  10.4 13.8 %all-to-all-start = ((bf16[33,128,128]{2,0,1:T(8,128)(2,1)}), bf16[33,128,128]{2,0,1:T(8,128)(2,1)S(1)}, u32[]{:S(2)}, u32[]{:S(2)}) async-start(bf16[33,128,128]{2,0,1:T(8,128)(2,1)} %pad_maximum_fusion), calls=%async_computation | async-start | bytes 2621440 | tf_op jit(solution)/shard_map/all_to_all | solution.py:155
  24.2 0.4 slice_reduce_fusion.29
  24.5 0.5 slice_reduce_fusion.30
  25.4 0.2 subtract_convert_fusion
  25.7 1.0 %fusion.4 = s32[256,8,32]{0,2,1:T(8,128)} fusion(s32[256,8,32]{0,2,1:T(8,128)S(1)} %copy-done.1, s32[256,8]{0,1:T(8,128)S(1)} %copy-done.2), kind=kLoop, calls=%fused_computation.13 | loop fusion | flops 1507328 | bytes 532480 | tf_op jit(solution)/shard_map/jit(_where)/select_n | solution.py:157
  26.7 2.3 %copy.47 = s32[256,8,32]{2,1,0:T(8,128)} copy(s32[256,8,32]{0,2,1:T(8,128)} %fusion.4) | data formatting | bytes 524288 | tf_op jit(solution)/shard_map/jit(_where)/select_n | solution.py:157
  28.9 1.6 %copy.48 = s32[2,8,128,32]{3,2,1,0:T(8,128)S(1)} copy(s32[2,8,128,32]{3,1,0,2:T(8,128)} %bitcast.20) | data formatting | bytes 524288 | tf_op jit(solution)/shard_map/transpose | solution.py:158
  30.5 14.7 %convert_reduce_fusion.counts_ref = f32[2,8,128,256]{3,2,1,0:T(8,128)} fusion(s32[2,8,128,32]{3,2,1,0:T(8,128)S(1)} %copy.48), kind=kLoop, calls=%fused_computation | loop fusion | flops 49807360 | bytes 2359296 | tf_op jit(solution)/shard_map/reduce_sum | solution.py:159
  45.2 15.4 %all-to-all-done = bf16[33,128,128]{2,0,1:T(8,128)(2,1)S(1)} async-done(((bf16[33,128,128]{2,0,1:T(8,128)(2,1)}), bf16[33,128,128]{2,0,1:T(8,128)(2,1)S(1)}, u32[]{:S(2)}, u32[]{:S(2)}) %all-to-all-start) | async-done | bytes 1081376 | tf_op jit(solution)/shard_map/all_to_all | solution.py:155
  60.6 1.2 %copy.49.incoming_ref = bf16[33,128,128]{2,1,0:T(8,128)(2,1)} copy(bf16[33,128,128]{2,0,1:T(8,128)(2,1)S(1)} %all-to-all-done) | data formatting | bytes 2162688 | tf_op jit(solution)/shard_map/all_to_all | solution.py:155
  61.8 21.0 %shard_map.55 = bf16[128,128]{1,0:T(8,128)(2,1)} custom-call(bf16[33,128,128]{2,1,0:T(8,128)(2,1)} %copy.49.incoming_ref, f32[2,8,128,256]{3,2,1,0:T(8,128)} %convert_reduce_fusion.counts_ref), custom_call_target="tpu_custom_call" | custom-call | flops 33554432 | bytes 4194304 | tf_op jit(solution)/shard_map/pallas_call | solution.py:165
  82.8 2.9 %all-gather = bf16[256,128]{1,0:T(8,128)(2,1)S(1)} all-gather(bf16[128,128]{1,0:T(8,128)(2,1)} %shard_map.55), channel_id=2, replica_groups=mesh['shot'=128,'freq'=2] {'freq'}, dimensions={0}, use_global_device_ids=true | all-gather | bytes 98304 | tf_op jit(solution)/shard_map/all_gather | solution.py:181
  85.9 0.5 copy.51
  86.4 1.5 %reshape.348 = bf16[2,1024,16]{1,2,0:T(8,128)(2,1)S(1)} reshape(bf16[2,128,8,2,4,2]{2,1,5,4,3,0:T(8,128)(2,1)S(1)} %copy.51) | data formatting | bytes 131072 | tf_op jit(solution)/shard_map/reshape | solution.py:183
  87.8 2.1 %convolution_convert_fusion = bf16[2,1024,512]{2,1,0:T(8,128)(2,1)} fusion(bf16[2,1024,16]{1,2,0:T(8,128)(2,1)S(1)} %reshape.348, bf16[2,16,512]{2,1,0:T(8,128)(2,1)S(1)} %get-tuple-element.42, bf16[2,16,512]{2,1,0:T(8,128)(2,1)S(1)} %get-tuple-element.43), kind=kOutput, calls=%fused_computation.4 | convolution fusion | flops 68550656 | bytes 2228224 | tf_op jit(solution)/shard_map/dot_general | solution.py:198
  (31 shorter events, 1.4 us)
Async XLA Ops:
  0.0 1.6 %copy-start = (bf16[2,1024,512]{2,1,0:T(8,128)(2,1)S(1)}, bf16[2,1024,512]{2,1,0:T(8,128)(2,1)}, u32[]{:S(2)}) copy-start(bf16[2,1024,512]{2,1,0:T(8,128)(2,1)} %param.5) | copy-start | bytes 6291460
  0.0 5.6 %copy-start.3 = (s32[8]{0:T(128)S(1)}, s32[8]{0:T(128)}, u32[]{:S(2)}) copy-start(s32[8]{0:T(128)} %param.6) | copy-start | bytes 100
  0.0 5.9 %copy-start.4 = (bf16[2,31]{1,0:T(2,128)(2,1)S(1)}, bf16[2,31]{1,0:T(2,128)(2,1)}, u32[]{:S(2)}) copy-start(bf16[2,31]{1,0:T(2,128)(2,1)} %param.9) | copy-start | bytes 376
  2.3 4.2 %collective-permute-start = (f32[4,2,2,1024]{3,0,2,1:T(4,128)S(1)}, f32[4,2,2,1024]{3,0,2,1:T(4,128)S(1)}, u32[]{:S(2)}, u32[]{:S(2)}) collective-permute-start(f32[4,2,2,1024]{3,0,2,1:T(4,128)S(1)} %constant_dynamic-slice_fusion), channel_id=1, source_target_pairs={{0,1},{1,0},{2,3},{3,2},{4,5},{5,4},{6,7},{7,6},{8,9},{9,8},{10,11... | collective-permute-start | bytes 196616 | tf_op jit(solution)/shard_map/ppermute | solution.py:139
  10.4 50.2 %all-to-all-start = ((bf16[33,128,128]{2,0,1:T(8,128)(2,1)}), bf16[33,128,128]{2,0,1:T(8,128)(2,1)S(1)}, u32[]{:S(2)}, u32[]{:S(2)}) async-start(bf16[33,128,128]{2,0,1:T(8,128)(2,1)} %pad_maximum_fusion), calls=%async_computation | async-start | bytes 2621440 | tf_op jit(solution)/shard_map/all_to_all | solution.py:155
  24.2 1.5 %copy-start.1 = (s32[256,8,32]{0,2,1:T(8,128)S(1)}, s32[256,8,32]{0,2,1:T(8,128)}, u32[]{:S(2)}) copy-start(s32[256,8,32]{0,2,1:T(8,128)} %param.7) | copy-start | bytes 786436
  24.2 1.5 %copy-start.2 = (s32[256,8]{0,1:T(8,128)S(1)}, s32[256,8]{0,1:T(8,128)}, u32[]{:S(2)}) copy-start(s32[256,8]{0,1:T(8,128)} %param.8) | copy-start | bytes 24580

commit v12 on v11

--- a/solution.py
+++ b/solution.py
@@ -40,7 +40,7 @@
     qt_ref[...] = incoming_ref[0].astype(jnp.float32).T
     me = lax.axis_index("shot")
     half = lax.axis_index("freq")
-    block = 16
+    block = 32
 
     steps = groups // block
 

time: 90.2 us -> 91 us (level)
  transfers between devices with their start and end apart: 2 -> 2, of which waited for: 2 -> 2; matrix products, arithmetic and copies ran while one was open for 24% -> 23% of each run, Pallas kernels for 0% -> 0%
where the time goes in v12:
time: 91 us; the launch traced here: 90.7 us
  Pallas kernels  21.8 us (24%)
  other arithmetic  18.7 us (21%)
  starting transfers between devices  17.1 us (19%)
  waiting for transfers between devices  16 us (18%)
  local copies, waits for them, and re-layouts  11.2 us (12%)
  blocking collectives  2.94 us (3%)
  matrix products  2.72 us (3%)
    pallas_call x1, Pallas kernels, shards(): pl.pallas_call(kernel, out_shape=jax.ShapeDtypeStruct((groups, rows * rec...  21.8 us
    all_to_all x1, waiting for transfers between devices, shards(): incoming = lax.all_to_all(outgoing, 'shot', 1, 1, tiled=True)  15.4 us
    reduce_sum x1, other arithmetic, shards(): jnp.sum((codes[..., None] == jnp.arange(shots, dtype=jnp.int32)).astype(j...  14.7 us
    all_to_all x1, starting transfers between devices, shards(): incoming = lax.all_to_all(outgoing, 'shot', 1, 1, tiled=True)  13.8 us
    ppermute x1, starting transfers between devices, shards(): theirs = lax.ppermute(theirs, 'freq', [(0, 1), (1, 0)])  3.33 us
    all_gather x1, blocking collectives, shards(): piece = lax.all_gather(back, 'freq', axis=0, tiled=False)  2.94 us
    select_n x1, local copies, waits for them, and re-layouts, shards(): jnp.where(used, aperture % shot_dev * groups + aperture // shot_dev, -1)  2.27 us
    dot_general x1, matrix products, shards(): lax.dot_general(jnp.concatenate([piece, piece], axis=2), jnp.concatenate(...  2.08 us
  transfers between devices with their start and end apart: 2, of which 2 were waited for; matrix products, arithmetic and copies ran while one was open for 23% of the time, Pallas kernels for 0%

profile of v12, /device:TPU:1, one launch (start us, length us, event | category | flops | bytes accessed | tf_op | source)
XLA Modules:
  0.0 90.7 jit_solution(3118450033936189563)
XLA Ops:
  0.0 1.0 %fusion.25 = (f32[8,1,512]{2,0,1:T(8,128)S(1)}, f32[8,1,512]{2,0,1:T(8,128)S(1)}) fusion(s32[512]{0:T(512)S(1)} %iota_add_fusion.1, s32[8]{0:T(128)} %param.6), kind=kLoop, calls=%fused_computation.55 | loop fusion | flops 61440 | bytes 34848 | tf_op jit(solution)/shard_map/cos | solution.py:34
  1.0 0.6 copy-done
  1.6 0.6 fusion
  2.3 3.3 %collective-permute-start = (f32[4,2,2,1024]{3,0,2,1:T(4,128)S(1)}, f32[4,2,2,1024]{3,0,2,1:T(4,128)S(1)}, u32[]{:S(2)}, u32[]{:S(2)}) collective-permute-start(f32[4,2,2,1024]{3,0,2,1:T(4,128)S(1)} %constant_dynamic-slice_fusion), channel_id=1, source_target_pairs={{0,1},{1,0},{2,3},{3,2},{4,5},{5,4},{6,7},{7,6},{8,9},{9,8},{10,11... | collective-permute-start | bytes 196616 | tf_op jit(solution)/shard_map/ppermute | solution.py:139
  5.9 0.6 collective-permute-done
  6.5 0.5 slice.193
  7.0 0.5 slice.192
  7.6 0.6 reshape.345
  8.7 1.7 %pad_maximum_fusion = bf16[33,128,128]{2,0,1:T(8,128)(2,1)} fusion(bf16[32,128,128]{2,0,1:T(8,128)(2,1)S(1)} %broadcast_in_dim.15, bf16[1,128,128]{2,0,1:T(2,128)(2,1)S(1)} %copy.46), kind=kLoop, calls=%fused_computation.5 | loop fusion | flops 2162688 | bytes 2162688 | tf_op jit(solution)/shard_map/concatenate | solution.py:147
  10.4 13.8 %all-to-all-start = ((bf16[33,128,128]{2,0,1:T(8,128)(2,1)}), bf16[33,128,128]{2,0,1:T(8,128)(2,1)S(1)}, u32[]{:S(2)}, u32[]{:S(2)}) async-start(bf16[33,128,128]{2,0,1:T(8,128)(2,1)} %pad_maximum_fusion), calls=%async_computation | async-start | bytes 2621440 | tf_op jit(solution)/shard_map/all_to_all | solution.py:155
  24.2 0.4 slice_reduce_fusion.29
  24.5 0.5 slice_reduce_fusion.30
  25.4 0.2 subtract_convert_fusion
  25.7 1.0 %fusion.4 = s32[256,8,32]{0,2,1:T(8,128)} fusion(s32[256,8,32]{0,2,1:T(8,128)S(1)} %copy-done.1, s32[256,8]{0,1:T(8,128)S(1)} %copy-done.2), kind=kLoop, calls=%fused_computation.13 | loop fusion | flops 1507328 | bytes 532480 | tf_op jit(solution)/shard_map/jit(_where)/select_n | solution.py:157
  26.7 2.3 %copy.47 = s32[256,8,32]{2,1,0:T(8,128)} copy(s32[256,8,32]{0,2,1:T(8,128)} %fusion.4) | data formatting | bytes 524288 | tf_op jit(solution)/shard_map/jit(_where)/select_n | solution.py:157
  28.9 1.6 %copy.48 = s32[2,8,128,32]{3,2,1,0:T(8,128)S(1)} copy(s32[2,8,128,32]{3,1,0,2:T(8,128)} %bitcast.20) | data formatting | bytes 524288 | tf_op jit(solution)/shard_map/transpose | solution.py:158
  30.5 14.7 %convert_reduce_fusion.counts_ref = f32[2,8,128,256]{3,2,1,0:T(8,128)} fusion(s32[2,8,128,32]{3,2,1,0:T(8,128)S(1)} %copy.48), kind=kLoop, calls=%fused_computation | loop fusion | flops 49807360 | bytes 2359296 | tf_op jit(solution)/shard_map/reduce_sum | solution.py:159
  45.2 15.4 %all-to-all-done = bf16[33,128,128]{2,0,1:T(8,128)(2,1)S(1)} async-done(((bf16[33,128,128]{2,0,1:T(8,128)(2,1)}), bf16[33,128,128]{2,0,1:T(8,128)(2,1)S(1)}, u32[]{:S(2)}, u32[]{:S(2)}) %all-to-all-start) | async-done | bytes 1081376 | tf_op jit(solution)/shard_map/all_to_all | solution.py:155
  60.6 1.2 %copy.49.incoming_ref = bf16[33,128,128]{2,1,0:T(8,128)(2,1)} copy(bf16[33,128,128]{2,0,1:T(8,128)(2,1)S(1)} %all-to-all-done) | data formatting | bytes 2162688 | tf_op jit(solution)/shard_map/all_to_all | solution.py:155
  61.8 21.8 %shard_map.55 = bf16[128,128]{1,0:T(8,128)(2,1)} custom-call(bf16[33,128,128]{2,1,0:T(8,128)(2,1)} %copy.49.incoming_ref, f32[2,8,128,256]{3,2,1,0:T(8,128)} %convert_reduce_fusion.counts_ref), custom_call_target="tpu_custom_call" | custom-call | flops 33554432 | bytes 4194304 | tf_op jit(solution)/shard_map/pallas_call | solution.py:165
  83.6 2.9 %all-gather = bf16[256,128]{1,0:T(8,128)(2,1)S(1)} all-gather(bf16[128,128]{1,0:T(8,128)(2,1)} %shard_map.55), channel_id=2, replica_groups=mesh['shot'=128,'freq'=2] {'freq'}, dimensions={0}, use_global_device_ids=true | all-gather | bytes 98304 | tf_op jit(solution)/shard_map/all_gather | solution.py:181
  86.7 0.5 copy.51
  87.2 1.5 %reshape.348 = bf16[2,1024,16]{1,2,0:T(8,128)(2,1)S(1)} reshape(bf16[2,128,8,2,4,2]{2,1,5,4,3,0:T(8,128)(2,1)S(1)} %copy.51) | data formatting | bytes 131072 | tf_op jit(solution)/shard_map/reshape | solution.py:183
  88.7 2.1 %convolution_convert_fusion = bf16[2,1024,512]{2,1,0:T(8,128)(2,1)} fusion(bf16[2,1024,16]{1,2,0:T(8,128)(2,1)S(1)} %reshape.348, bf16[2,16,512]{2,1,0:T(8,128)(2,1)S(1)} %get-tuple-element.42, bf16[2,16,512]{2,1,0:T(8,128)(2,1)S(1)} %get-tuple-element.43), kind=kOutput, calls=%fused_computation.4 | convolution fusion | flops 68550656 | bytes 2228224 | tf_op jit(solution)/shard_map/dot_general | solution.py:198
  (31 shorter events, 1.4 us)
Async XLA Ops:
  0.0 1.6 %copy-start = (bf16[2,1024,512]{2,1,0:T(8,128)(2,1)S(1)}, bf16[2,1024,512]{2,1,0:T(8,128)(2,1)}, u32[]{:S(2)}) copy-start(bf16[2,1024,512]{2,1,0:T(8,128)(2,1)} %param.5) | copy-start | bytes 6291460
  0.0 5.6 %copy-start.3 = (s32[8]{0:T(128)S(1)}, s32[8]{0:T(128)}, u32[]{:S(2)}) copy-start(s32[8]{0:T(128)} %param.6) | copy-start | bytes 100
  0.0 5.9 %copy-start.4 = (bf16[2,31]{1,0:T(2,128)(2,1)S(1)}, bf16[2,31]{1,0:T(2,128)(2,1)}, u32[]{:S(2)}) copy-start(bf16[2,31]{1,0:T(2,128)(2,1)} %param.9) | copy-start | bytes 376
  2.3 4.2 %collective-permute-start = (f32[4,2,2,1024]{3,0,2,1:T(4,128)S(1)}, f32[4,2,2,1024]{3,0,2,1:T(4,128)S(1)}, u32[]{:S(2)}, u32[]{:S(2)}) collective-permute-start(f32[4,2,2,1024]{3,0,2,1:T(4,128)S(1)} %constant_dynamic-slice_fusion), channel_id=1, source_target_pairs={{0,1},{1,0},{2,3},{3,2},{4,5},{5,4},{6,7},{7,6},{8,9},{9,8},{10,11... | collective-permute-start | bytes 196616 | tf_op jit(solution)/shard_map/ppermute | solution.py:139
  10.4 50.2 %all-to-all-start = ((bf16[33,128,128]{2,0,1:T(8,128)(2,1)}), bf16[33,128,128]{2,0,1:T(8,128)(2,1)S(1)}, u32[]{:S(2)}, u32[]{:S(2)}) async-start(bf16[33,128,128]{2,0,1:T(8,128)(2,1)} %pad_maximum_fusion), calls=%async_computation | async-start | bytes 2621440 | tf_op jit(solution)/shard_map/all_to_all | solution.py:155
  24.2 1.5 %copy-start.1 = (s32[256,8,32]{0,2,1:T(8,128)S(1)}, s32[256,8,32]{0,2,1:T(8,128)}, u32[]{:S(2)}) copy-start(s32[256,8,32]{0,2,1:T(8,128)} %param.7) | copy-start | bytes 786436
  24.2 1.5 %copy-start.2 = (s32[256,8]{0,1:T(8,128)S(1)}, s32[256,8]{0,1:T(8,128)}, u32[]{:S(2)}) copy-start(s32[256,8]{0,1:T(8,128)} %param.8) | copy-start | bytes 24580

commit v13 on v12

--- a/solution.py
+++ b/solution.py
@@ -40,7 +40,7 @@
     qt_ref[...] = incoming_ref[0].astype(jnp.float32).T
     me = lax.axis_index("shot")
     half = lax.axis_index("freq")
-    block = 32
+    block = 8
 
     steps = groups // block
 

time: 91 us -> 90.1 us (level)
  transfers between devices with their start and end apart: 2 -> 2, of which waited for: 2 -> 2; matrix products, arithmetic and copies ran while one was open for 23% -> 24% of each run, Pallas kernels for 0% -> 0%
where the time goes in v13:
time: 90.1 us; the launch traced here: 89.8 us
  Pallas kernels  20.9 us (23%)
  other arithmetic  18.7 us (21%)
  starting transfers between devices  17.1 us (19%)
  waiting for transfers between devices  16 us (18%)
  local copies, waits for them, and re-layouts  11.2 us (12%)
  blocking collectives  2.94 us (3%)
  matrix products  2.71 us (3%)
    pallas_call x1, Pallas kernels, shards(): pl.pallas_call(kernel, out_shape=jax.ShapeDtypeStruct((groups, rows * rec...  20.9 us
    all_to_all x1, waiting for transfers between devices, shards(): incoming = lax.all_to_all(outgoing, 'shot', 1, 1, tiled=True)  15.4 us
    reduce_sum x1, other arithmetic, shards(): jnp.sum((codes[..., None] == jnp.arange(shots, dtype=jnp.int32)).astype(j...  14.7 us
    all_to_all x1, starting transfers between devices, shards(): incoming = lax.all_to_all(outgoing, 'shot', 1, 1, tiled=True)  13.8 us
    ppermute x1, starting transfers between devices, shards(): theirs = lax.ppermute(theirs, 'freq', [(0, 1), (1, 0)])  3.33 us
    all_gather x1, blocking collectives, shards(): piece = lax.all_gather(back, 'freq', axis=0, tiled=False)  2.94 us
    select_n x1, local copies, waits for them, and re-layouts, shards(): jnp.where(used, aperture % shot_dev * groups + aperture // shot_dev, -1)  2.27 us
    dot_general x1, matrix products, shards(): lax.dot_general(jnp.concatenate([piece, piece], axis=2), jnp.concatenate(...  2.07 us
  transfers between devices with their start and end apart: 2, of which 2 were waited for; matrix products, arithmetic and copies ran while one was open for 24% of the time, Pallas kernels for 0%

profile of v13, /device:TPU:1, one launch (start us, length us, event | category | flops | bytes accessed | tf_op | source)
XLA Modules:
  0.0 89.8 jit_solution(3098816894698344820)
XLA Ops:
  0.0 1.0 %fusion.25 = (f32[8,1,512]{2,0,1:T(8,128)S(1)}, f32[8,1,512]{2,0,1:T(8,128)S(1)}) fusion(s32[512]{0:T(512)S(1)} %iota_add_fusion.1, s32[8]{0:T(128)} %param.6), kind=kLoop, calls=%fused_computation.55 | loop fusion | flops 61440 | bytes 34848 | tf_op jit(solution)/shard_map/cos | solution.py:34
  1.0 0.6 copy-done
  1.6 0.6 fusion
  2.3 3.3 %collective-permute-start = (f32[4,2,2,1024]{3,0,2,1:T(4,128)S(1)}, f32[4,2,2,1024]{3,0,2,1:T(4,128)S(1)}, u32[]{:S(2)}, u32[]{:S(2)}) collective-permute-start(f32[4,2,2,1024]{3,0,2,1:T(4,128)S(1)} %constant_dynamic-slice_fusion), channel_id=1, source_target_pairs={{0,1},{1,0},{2,3},{3,2},{4,5},{5,4},{6,7},{7,6},{8,9},{9,8},{10,11... | collective-permute-start | bytes 196616 | tf_op jit(solution)/shard_map/ppermute | solution.py:139
  5.9 0.6 collective-permute-done
  6.5 0.5 slice.193
  7.0 0.5 slice.192
  7.6 0.6 reshape.345
  8.7 1.7 %pad_maximum_fusion = bf16[33,128,128]{2,0,1:T(8,128)(2,1)} fusion(bf16[32,128,128]{2,0,1:T(8,128)(2,1)S(1)} %broadcast_in_dim.15, bf16[1,128,128]{2,0,1:T(2,128)(2,1)S(1)} %copy.46), kind=kLoop, calls=%fused_computation.5 | loop fusion | flops 2162688 | bytes 2162688 | tf_op jit(solution)/shard_map/concatenate | solution.py:147
  10.4 13.8 %all-to-all-start = ((bf16[33,128,128]{2,0,1:T(8,128)(2,1)}), bf16[33,128,128]{2,0,1:T(8,128)(2,1)S(1)}, u32[]{:S(2)}, u32[]{:S(2)}) async-start(bf16[33,128,128]{2,0,1:T(8,128)(2,1)} %pad_maximum_fusion), calls=%async_computation | async-start | bytes 2621440 | tf_op jit(solution)/shard_map/all_to_all | solution.py:155
  24.2 0.4 slice_reduce_fusion.29
  24.5 0.5 slice_reduce_fusion.30
  25.4 0.2 subtract_convert_fusion
  25.7 1.0 %fusion.4 = s32[256,8,32]{0,2,1:T(8,128)} fusion(s32[256,8,32]{0,2,1:T(8,128)S(1)} %copy-done.1, s32[256,8]{0,1:T(8,128)S(1)} %copy-done.2), kind=kLoop, calls=%fused_computation.13 | loop fusion | flops 1507328 | bytes 532480 | tf_op jit(solution)/shard_map/jit(_where)/select_n | solution.py:157
  26.7 2.3 %copy.47 = s32[256,8,32]{2,1,0:T(8,128)} copy(s32[256,8,32]{0,2,1:T(8,128)} %fusion.4) | data formatting | bytes 524288 | tf_op jit(solution)/shard_map/jit(_where)/select_n | solution.py:157
  28.9 1.6 %copy.48 = s32[2,8,128,32]{3,2,1,0:T(8,128)S(1)} copy(s32[2,8,128,32]{3,1,0,2:T(8,128)} %bitcast.20) | data formatting | bytes 524288 | tf_op jit(solution)/shard_map/transpose | solution.py:158
  30.5 14.7 %convert_reduce_fusion.counts_ref = f32[2,8,128,256]{3,2,1,0:T(8,128)} fusion(s32[2,8,128,32]{3,2,1,0:T(8,128)S(1)} %copy.48), kind=kLoop, calls=%fused_computation | loop fusion | flops 49807360 | bytes 2359296 | tf_op jit(solution)/shard_map/reduce_sum | solution.py:159
  45.2 15.4 %all-to-all-done = bf16[33,128,128]{2,0,1:T(8,128)(2,1)S(1)} async-done(((bf16[33,128,128]{2,0,1:T(8,128)(2,1)}), bf16[33,128,128]{2,0,1:T(8,128)(2,1)S(1)}, u32[]{:S(2)}, u32[]{:S(2)}) %all-to-all-start) | async-done | bytes 1081376 | tf_op jit(solution)/shard_map/all_to_all | solution.py:155
  60.6 1.2 %copy.49.incoming_ref = bf16[33,128,128]{2,1,0:T(8,128)(2,1)} copy(bf16[33,128,128]{2,0,1:T(8,128)(2,1)S(1)} %all-to-all-done) | data formatting | bytes 2162688 | tf_op jit(solution)/shard_map/all_to_all | solution.py:155
  61.8 20.9 %shard_map.55 = bf16[128,128]{1,0:T(8,128)(2,1)} custom-call(bf16[33,128,128]{2,1,0:T(8,128)(2,1)} %copy.49.incoming_ref, f32[2,8,128,256]{3,2,1,0:T(8,128)} %convert_reduce_fusion.counts_ref), custom_call_target="tpu_custom_call" | custom-call | flops 33554432 | bytes 4194304 | tf_op jit(solution)/shard_map/pallas_call | solution.py:165
  82.7 2.9 %all-gather = bf16[256,128]{1,0:T(8,128)(2,1)S(1)} all-gather(bf16[128,128]{1,0:T(8,128)(2,1)} %shard_map.55), channel_id=2, replica_groups=mesh['shot'=128,'freq'=2] {'freq'}, dimensions={0}, use_global_device_ids=true | all-gather | bytes 98304 | tf_op jit(solution)/shard_map/all_gather | solution.py:181
  85.8 0.5 copy.51
  86.3 1.5 %reshape.348 = bf16[2,1024,16]{1,2,0:T(8,128)(2,1)S(1)} reshape(bf16[2,128,8,2,4,2]{2,1,5,4,3,0:T(8,128)(2,1)S(1)} %copy.51) | data formatting | bytes 131072 | tf_op jit(solution)/shard_map/reshape | solution.py:183
  87.8 2.1 %convolution_convert_fusion = bf16[2,1024,512]{2,1,0:T(8,128)(2,1)} fusion(bf16[2,1024,16]{1,2,0:T(8,128)(2,1)S(1)} %reshape.348, bf16[2,16,512]{2,1,0:T(8,128)(2,1)S(1)} %get-tuple-element.42, bf16[2,16,512]{2,1,0:T(8,128)(2,1)S(1)} %get-tuple-element.43), kind=kOutput, calls=%fused_computation.4 | convolution fusion | flops 68550656 | bytes 2228224 | tf_op jit(solution)/shard_map/dot_general | solution.py:198
  (31 shorter events, 1.4 us)
Async XLA Ops:
  0.0 1.6 %copy-start = (bf16[2,1024,512]{2,1,0:T(8,128)(2,1)S(1)}, bf16[2,1024,512]{2,1,0:T(8,128)(2,1)}, u32[]{:S(2)}) copy-start(bf16[2,1024,512]{2,1,0:T(8,128)(2,1)} %param.5) | copy-start | bytes 6291460
  0.0 5.6 %copy-start.3 = (s32[8]{0:T(128)S(1)}, s32[8]{0:T(128)}, u32[]{:S(2)}) copy-start(s32[8]{0:T(128)} %param.6) | copy-start | bytes 100
  0.0 5.9 %copy-start.4 = (bf16[2,31]{1,0:T(2,128)(2,1)S(1)}, bf16[2,31]{1,0:T(2,128)(2,1)}, u32[]{:S(2)}) copy-start(bf16[2,31]{1,0:T(2,128)(2,1)} %param.9) | copy-start | bytes 376
  2.3 4.2 %collective-permute-start = (f32[4,2,2,1024]{3,0,2,1:T(4,128)S(1)}, f32[4,2,2,1024]{3,0,2,1:T(4,128)S(1)}, u32[]{:S(2)}, u32[]{:S(2)}) collective-permute-start(f32[4,2,2,1024]{3,0,2,1:T(4,128)S(1)} %constant_dynamic-slice_fusion), channel_id=1, source_target_pairs={{0,1},{1,0},{2,3},{3,2},{4,5},{5,4},{6,7},{7,6},{8,9},{9,8},{10,11... | collective-permute-start | bytes 196616 | tf_op jit(solution)/shard_map/ppermute | solution.py:139
  10.4 50.2 %all-to-all-start = ((bf16[33,128,128]{2,0,1:T(8,128)(2,1)}), bf16[33,128,128]{2,0,1:T(8,128)(2,1)S(1)}, u32[]{:S(2)}, u32[]{:S(2)}) async-start(bf16[33,128,128]{2,0,1:T(8,128)(2,1)} %pad_maximum_fusion), calls=%async_computation | async-start | bytes 2621440 | tf_op jit(solution)/shard_map/all_to_all | solution.py:155
  24.2 1.5 %copy-start.1 = (s32[256,8,32]{0,2,1:T(8,128)S(1)}, s32[256,8,32]{0,2,1:T(8,128)}, u32[]{:S(2)}) copy-start(s32[256,8,32]{0,2,1:T(8,128)} %param.7) | copy-start | bytes 786436
  24.2 1.5 %copy-start.2 = (s32[256,8]{0,1:T(8,128)S(1)}, s32[256,8]{0,1:T(8,128)}, u32[]{:S(2)}) copy-start(s32[256,8]{0,1:T(8,128)} %param.8) | copy-start | bytes 24580

commit v14 on v13

--- a/solution.py
+++ b/solution.py
@@ -178,7 +178,8 @@
             flops=16 * groups * shots * rows * receiver_dev // 2, transcendentals=0, bytes_accessed=4 * 1024 * 1024
         ),
     )(incoming, counts)
-    piece = lax.all_gather(back, "freq", axis=0, tiled=False)
+    other = lax.ppermute(back, "freq", [(0, 1), (1, 0)])
+    piece = jnp.where(core == 0, jnp.stack([back, other]), jnp.stack([other, back]))
     piece = piece.reshape(freq_dev, groups, local_bins, 2, shot_dev, receiver_dev)
     piece = piece.transpose(4, 1, 5, 0, 2, 3).reshape(shot_dev, receivers, NF * 2)
     wide = time_dev + 2 * half_taps

time: 90.1 us -> 91.6 us (1.017)
  local copies, waits for them, and re-layouts: 11.2 us -> 14.8 us
  blocking collectives: 2.94 us -> 0 us
  waiting for transfers between devices: 16 us -> 13.5 us
  other arithmetic: 18.7 us -> 20.3 us
  starting transfers between devices: 17.1 us -> 18.4 us
    all_gather x1 -> x0, blocking collectives: 2.94 us -> none  [shards(): piece = lax.all_gather(back, 'freq', axis=0, tiled=False)]
    all_to_all x1, waiting for transfers between devices: 15.4 us -> 13.5 us  [shards(): incoming = lax.all_to_all(outgoing, 'shot', 1, 1, tiled=True)]
    slice x2, local copies, waits for them, and re-layouts: 0.39 us -> 1.87 us  [shards(): wide_rows[None, :, 2 * half_taps - tap:2 * half_taps - tap + time_dev]]
    ppermute x0 -> x1, starting transfers between devices: none -> 1.31 us  [shards(): other = lax.ppermute(back, 'freq', [(0, 1), (1, 0)])]
    slice x2, local copies, waits for them, and re-layouts: 0.84 us -> 2 us  [shards(): taps[:, tap, None, None]]
  transfers between devices with their start and end apart: 2 -> 3, of which waited for: 2 -> 1; matrix products, arithmetic and copies ran while one was open for 24% -> 29% of each run, Pallas kernels for 0% -> 0%
where the time goes in v14:
time: 91.6 us; the launch traced here: 91.2 us
  Pallas kernels  20.6 us (22%)
  other arithmetic  20.3 us (22%)
  starting transfers between devices  18.4 us (20%)
  local copies, waits for them, and re-layouts  14.8 us (16%)
  waiting for transfers between devices  13.5 us (15%)
  matrix products  2.72 us (3%)
    pallas_call x1, Pallas kernels, shards(): pl.pallas_call(kernel, out_shape=jax.ShapeDtypeStruct((groups, rows * rec...  20.6 us
    reduce_sum x1, other arithmetic, shards(): jnp.sum((codes[..., None] == jnp.arange(shots, dtype=jnp.int32)).astype(j...  14.7 us
    all_to_all x1, starting transfers between devices, shards(): incoming = lax.all_to_all(outgoing, 'shot', 1, 1, tiled=True)  13.8 us
    all_to_all x1, waiting for transfers between devices, shards(): incoming = lax.all_to_all(outgoing, 'shot', 1, 1, tiled=True)  13.5 us
    ppermute x1, starting transfers between devices, shards(): theirs = lax.ppermute(theirs, 'freq', [(0, 1), (1, 0)])  3.33 us
    select_n x1, local copies, waits for them, and re-layouts, shards(): jnp.where(used, aperture % shot_dev * groups + aperture // shot_dev, -1)  2.27 us
    dot_general x1, matrix products, shards(): lax.dot_general(jnp.concatenate([piece, piece], axis=2), jnp.concatenate(...  2.08 us
    slice x2, local copies, waits for them, and re-layouts, shards(): taps[:, tap, None, None]  2 us
  transfers between devices with their start and end apart: 3, of which 1 were waited for; matrix products, arithmetic and copies ran while one was open for 29% of the time, Pallas kernels for 0%

profile of v14, /device:TPU:1, one launch (start us, length us, event | category | flops | bytes accessed | tf_op | source)
XLA Modules:
  0.0 91.2 jit_solution(6184310772609829910)
XLA Ops:
  0.0 1.0 %fusion.26 = (f32[8,1,512]{2,0,1:T(8,128)S(1)}, f32[8,1,512]{2,0,1:T(8,128)S(1)}) fusion(s32[512]{0:T(512)S(1)} %iota_add_fusion.1, s32[8]{0:T(128)} %param.6), kind=kLoop, calls=%fused_computation.57 | loop fusion | flops 61440 | bytes 34848 | tf_op jit(solution)/shard_map/cos | solution.py:34
  1.0 0.6 copy-done
  1.6 0.6 fusion
  2.3 3.3 %collective-permute-start = (f32[4,2,2,1024]{3,0,2,1:T(4,128)S(1)}, f32[4,2,2,1024]{3,0,2,1:T(4,128)S(1)}, u32[]{:S(2)}, u32[]{:S(2)}) collective-permute-start(f32[4,2,2,1024]{3,0,2,1:T(4,128)S(1)} %constant_dynamic-slice_fusion), channel_id=1, source_target_pairs={{0,1},{1,0},{2,3},{3,2},{4,5},{5,4},{6,7},{7,6},{8,9},{9,8},{10,11... | collective-permute-start | bytes 196616 | tf_op jit(solution)/shard_map/ppermute | solution.py:139
  5.8 0.9 %slice_reduce_fusion.29 = (f32[2]{0:T(128)}, f32[2]{0:T(128)}, f32[2]{0:T(128)}, f32[2]{0:T(128)}, f32[2]{0:T(128)}, /*index=5*/f32[2]{0:T(128)}, f32[2]{0:T(128...) fusion(f32[2,31]{1,0:T(2,128)S(1)} %convert_element_type.68), kind=kLoop, calls=%fused_computation.93 | loop fusion | bytes 192 | tf_op jit(solution)/shard_map/slice | solution.py:194
  7.9 0.6 reshape.351
  9.0 1.7 %pad_maximum_fusion = bf16[33,128,128]{2,0,1:T(8,128)(2,1)} fusion(bf16[32,128,128]{2,0,1:T(8,128)(2,1)S(1)} %broadcast_in_dim.15, bf16[1,128,128]{2,0,1:T(2,128)(2,1)S(1)} %copy.50), kind=kLoop, calls=%fused_computation.5 | loop fusion | flops 2162688 | bytes 2162688 | tf_op jit(solution)/shard_map/concatenate | solution.py:147
  10.6 13.8 %all-to-all-start = ((bf16[33,128,128]{2,0,1:T(8,128)(2,1)}), bf16[33,128,128]{2,0,1:T(8,128)(2,1)S(1)}, u32[]{:S(2)}, u32[]{:S(2)}) async-start(bf16[33,128,128]{2,0,1:T(8,128)(2,1)} %pad_maximum_fusion), calls=%async_computation | async-start | bytes 2621440 | tf_op jit(solution)/shard_map/all_to_all | solution.py:155
  24.5 1.1 %slice_reduce_fusion.30 = (f32[2]{0:T(128)S(1)}, f32[2]{0:T(128)}, f32[2]{0:T(128)}, f32[2]{0:T(128)}, f32[2]{0:T(128)}, /*index=5*/f32[2]{0:T(128)}, f32[2]{0:T...) fusion(f32[2,31]{1,0:T(2,128)S(1)} %convert_element_type.68), kind=kLoop, calls=%fused_computation.94 | loop fusion | bytes 304 | tf_op jit(solution)/shard_map/slice | solution.py:194
  25.6 0.9 fusion.35
  26.4 1.0 %fusion.34 = (f32[16,512]{1,0:T(8,128)}, f32[16,512]{1,0:T(8,128)}, f32[16,512]{1,0:T(8,128)}, f32[16,512]{1,0:T(8,128)}, f32[16,512]{1,0:T(8,128)}, /*index=5*/...) fusion(f32[16,542]{1,0:T(8,128)S(1)} %broadcast_select_fusion), kind=kLoop, calls=%fused_computation.99 | loop fusion | bytes 1245184 | tf_op jit(solution)/shard_map/slice | solution.py:194
  27.5 1.7 %fusion.4 = s32[256,8,32]{0,2,1:T(8,128)} fusion(s32[256,8,32]{0,2,1:T(8,128)S(1)} %copy-done.1, s32[256,8]{0,1:T(8,128)} %param.8), kind=kLoop, calls=%fused_computation.13 | loop fusion | flops 1507328 | bytes 532480 | tf_op jit(solution)/shard_map/jit(_where)/select_n | solution.py:157
  29.1 2.3 %copy.51 = s32[256,8,32]{2,1,0:T(8,128)} copy(s32[256,8,32]{0,2,1:T(8,128)} %fusion.4) | data formatting | bytes 524288 | tf_op jit(solution)/shard_map/jit(_where)/select_n | solution.py:157
  31.4 1.6 %copy.52 = s32[2,8,128,32]{3,2,1,0:T(8,128)S(1)} copy(s32[2,8,128,32]{3,1,0,2:T(8,128)} %bitcast.21) | data formatting | bytes 524288 | tf_op jit(solution)/shard_map/transpose | solution.py:158
  33.0 14.7 %convert_reduce_fusion.counts_ref = f32[2,8,128,256]{3,2,1,0:T(8,128)} fusion(s32[2,8,128,32]{3,2,1,0:T(8,128)S(1)} %copy.52), kind=kLoop, calls=%fused_computation | loop fusion | flops 49807360 | bytes 2359296 | tf_op jit(solution)/shard_map/reduce_sum | solution.py:159
  47.6 13.5 %all-to-all-done = bf16[33,128,128]{2,0,1:T(8,128)(2,1)S(1)} async-done(((bf16[33,128,128]{2,0,1:T(8,128)(2,1)}), bf16[33,128,128]{2,0,1:T(8,128)(2,1)S(1)}, u32[]{:S(2)}, u32[]{:S(2)}) %all-to-all-start) | async-done | bytes 1081376 | tf_op jit(solution)/shard_map/all_to_all | solution.py:155
  61.2 1.2 %copy.53.incoming_ref = bf16[33,128,128]{2,1,0:T(8,128)(2,1)} copy(bf16[33,128,128]{2,0,1:T(8,128)(2,1)S(1)} %all-to-all-done) | data formatting | bytes 2162688 | tf_op jit(solution)/shard_map/all_to_all | solution.py:155
  62.8 20.6 %shard_map.55 = bf16[128,128]{1,0:T(8,128)(2,1)} custom-call(bf16[33,128,128]{2,1,0:T(8,128)(2,1)} %copy.53.incoming_ref, f32[2,8,128,256]{3,2,1,0:T(8,128)} %convert_reduce_fusion.counts_ref), custom_call_target="tpu_custom_call" | custom-call | flops 33554432 | bytes 4194304 | tf_op jit(solution)/shard_map/pallas_call | solution.py:165
  83.4 1.3 %collective-permute-start.1 = (bf16[128,128]{1,0:T(8,128)(2,1)}, bf16[128,128]{1,0:T(8,128)(2,1)S(1)}, u32[]{:S(2)}, u32[]{:S(2)}) collective-permute-start(bf16[128,128]{1,0:T(8,128)(2,1)} %shard_map.55), channel_id=1, source_target_pairs={{0,1},{1,0},{2,3},{3,2},{4,5},{5,4},{6,7},{7,6},{8,9},{9,8},{10,11... | collective-permute-start | bytes 98312 | tf_op jit(solution)/shard_map/ppermute | solution.py:181
  85.1 1.0 %subtract_convert_fusion = (bf16[2,16,512]{2,1,0:T(8,128)(2,1)S(1)}, bf16[2,16,512]{2,1,0:T(8,128)(2,1)S(1)}) fusion(f32[16,512]{1,0:T(8,128)S(1)} %copy-done.12, f32[2]{0:T(128)S(1)} %copy-done.30, f32[16,512]{1,0:T(8,128)S(1)} %copy-done.13, f32[2]{0:T(128)S(1)} %copy-done.31, f32[16,512]{1,0:T(8,128)S(1)} %copy-done.14, f32[2]{0:T(128)S(1)} %copy-done.32, ...), kind=kLoop, calls=%fused_computation.28 | loop fusion | flops 1064960 | bytes 1081592 | tf_op jit(solution)/shard_map/convert_element_type | solution.py:198
  86.2 0.9 copy.54
  87.2 0.5 copy.56
  87.7 1.5 %reshape.353 = bf16[2,1024,16]{1,2,0:T(8,128)(2,1)S(1)} reshape(bf16[2,128,8,2,4,2]{2,1,5,4,3,0:T(8,128)(2,1)S(1)} %copy.56) | data formatting | bytes 131072 | tf_op jit(solution)/shard_map/reshape | solution.py:184
  89.2 2.1 %convolution_convert_fusion = bf16[2,1024,512]{2,1,0:T(8,128)(2,1)} fusion(bf16[2,1024,16]{1,2,0:T(8,128)(2,1)S(1)} %reshape.353, bf16[2,16,512]{2,1,0:T(8,128)(2,1)S(1)} %get-tuple-element.42, bf16[2,16,512]{2,1,0:T(8,128)(2,1)S(1)} %get-tuple-element.43), kind=kOutput, calls=%fused_computation.4 | convolution fusion | flops 68550656 | bytes 2228224 | tf_op jit(solution)/shard_map/dot_general | solution.py:199
  (111 shorter events, 2.1 us)
Async XLA Ops:
  2.3 4.5 %collective-permute-start = (f32[4,2,2,1024]{3,0,2,1:T(4,128)S(1)}, f32[4,2,2,1024]{3,0,2,1:T(4,128)S(1)}, u32[]{:S(2)}, u32[]{:S(2)}) collective-permute-start(f32[4,2,2,1024]{3,0,2,1:T(4,128)S(1)} %constant_dynamic-slice_fusion), channel_id=1, source_target_pairs={{0,1},{1,0},{2,3},{3,2},{4,5},{5,4},{6,7},{7,6},{8,9},{9,8},{10,11... | collective-permute-start | bytes 196616 | tf_op jit(solution)/shard_map/ppermute | solution.py:139
  10.6 50.5 %all-to-all-start = ((bf16[33,128,128]{2,0,1:T(8,128)(2,1)}), bf16[33,128,128]{2,0,1:T(8,128)(2,1)S(1)}, u32[]{:S(2)}, u32[]{:S(2)}) async-start(bf16[33,128,128]{2,0,1:T(8,128)(2,1)} %pad_maximum_fusion), calls=%async_computation | async-start | bytes 2621440 | tf_op jit(solution)/shard_map/all_to_all | solution.py:155
  62.4 22.3 %copy-start.6 = (f32[16,512]{1,0:T(8,128)S(1)}, f32[16,512]{1,0:T(8,128)}, u32[]{:S(2)}) copy-start(f32[16,512]{1,0:T(8,128)} %get-tuple-element.70) | copy-start | bytes 98308
  62.4 22.3 %copy-start.7 = (f32[16,512]{1,0:T(8,128)S(1)}, f32[16,512]{1,0:T(8,128)}, u32[]{:S(2)}) copy-start(f32[16,512]{1,0:T(8,128)} %get-tuple-element.71) | copy-start | bytes 98308
  62.4 22.3 %copy-start.8 = (f32[16,512]{1,0:T(8,128)S(1)}, f32[16,512]{1,0:T(8,128)}, u32[]{:S(2)}) copy-start(f32[16,512]{1,0:T(8,128)} %get-tuple-element.72) | copy-start | bytes 98308
  62.5 22.3 %copy-start.9 = (f32[16,512]{1,0:T(8,128)S(1)}, f32[16,512]{1,0:T(8,128)}, u32[]{:S(2)}) copy-start(f32[16,512]{1,0:T(8,128)} %get-tuple-element.73) | copy-start | bytes 98308
  62.5 22.3 %copy-start.10 = (f32[16,512]{1,0:T(8,128)S(1)}, f32[16,512]{1,0:T(8,128)}, u32[]{:S(2)}) copy-start(f32[16,512]{1,0:T(8,128)} %get-tuple-element.74) | copy-start | bytes 98308
  62.5 22.3 %copy-start.11 = (f32[16,512]{1,0:T(8,128)S(1)}, f32[16,512]{1,0:T(8,128)}, u32[]{:S(2)}) copy-start(f32[16,512]{1,0:T(8,128)} %get-tuple-element.44) | copy-start | bytes 98308
  62.5 22.3 %copy-start.12 = (f32[16,512]{1,0:T(8,128)S(1)}, f32[16,512]{1,0:T(8,128)}, u32[]{:S(2)}) copy-start(f32[16,512]{1,0:T(8,128)} %get-tuple-element.45) | copy-start | bytes 98308
  62.5 22.3 %copy-start.13 = (f32[16,512]{1,0:T(8,128)S(1)}, f32[16,512]{1,0:T(8,128)}, u32[]{:S(2)}) copy-start(f32[16,512]{1,0:T(8,128)} %get-tuple-element.46) | copy-start | bytes 98308
  62.5 22.3 %copy-start.14 = (f32[16,512]{1,0:T(8,128)S(1)}, f32[16,512]{1,0:T(8,128)}, u32[]{:S(2)}) copy-start(f32[16,512]{1,0:T(8,128)} %get-tuple-element.47) | copy-start | bytes 98308
  62.5 22.3 %copy-start.15 = (f32[16,512]{1,0:T(8,128)S(1)}, f32[16,512]{1,0:T(8,128)}, u32[]{:S(2)}) copy-start(f32[16,512]{1,0:T(8,128)} %get-tuple-element.48) | copy-start | bytes 98308
  62.5 22.3 %copy-start.16 = (f32[16,512]{1,0:T(8,128)S(1)}, f32[16,512]{1,0:T(8,128)}, u32[]{:S(2)}) copy-start(f32[16,512]{1,0:T(8,128)} %get-tuple-element.49) | copy-start | bytes 98308
  62.5 22.3 %copy-start.17 = (f32[16,512]{1,0:T(8,128)S(1)}, f32[16,512]{1,0:T(8,128)}, u32[]{:S(2)}) copy-start(f32[16,512]{1,0:T(8,128)} %get-tuple-element.50) | copy-start | bytes 98308
  62.5 22.3 %copy-start.18 = (f32[16,512]{1,0:T(8,128)S(1)}, f32[16,512]{1,0:T(8,128)}, u32[]{:S(2)}) copy-start(f32[16,512]{1,0:T(8,128)} %get-tuple-element.51) | copy-start | bytes 98308
  62.6 22.3 %copy-start.19 = (f32[16,512]{1,0:T(8,128)S(1)}, f32[16,512]{1,0:T(8,128)}, u32[]{:S(2)}) copy-start(f32[16,512]{1,0:T(8,128)} %get-tuple-element.52) | copy-start | bytes 98308
  62.6 22.3 %copy-start.20 = (f32[16,512]{1,0:T(8,128)S(1)}, f32[16,512]{1,0:T(8,128)}, u32[]{:S(2)}) copy-start(f32[16,512]{1,0:T(8,128)} %get-tuple-element.53) | copy-start | bytes 98308
  62.6 22.3 %copy-start.21 = (f32[16,512]{1,0:T(8,128)S(1)}, f32[16,512]{1,0:T(8,128)}, u32[]{:S(2)}) copy-start(f32[16,512]{1,0:T(8,128)} %get-tuple-element.54) | copy-start | bytes 98308
  62.6 22.3 %copy-start.22 = (f32[16,512]{1,0:T(8,128)S(1)}, f32[16,512]{1,0:T(8,128)}, u32[]{:S(2)}) copy-start(f32[16,512]{1,0:T(8,128)} %get-tuple-element.55) | copy-start | bytes 98308
  62.6 22.3 %copy-start.23 = (f32[16,512]{1,0:T(8,128)S(1)}, f32[16,512]{1,0:T(8,128)}, u32[]{:S(2)}) copy-start(f32[16,512]{1,0:T(8,128)} %get-tuple-element.56) | copy-start | bytes 98308
  62.6 22.3 %copy-start.24 = (f32[16,512]{1,0:T(8,128)S(1)}, f32[16,512]{1,0:T(8,128)}, u32[]{:S(2)}) copy-start(f32[16,512]{1,0:T(8,128)} %get-tuple-element.57) | copy-start | bytes 98308
  62.6 22.3 %copy-start.25 = (f32[16,512]{1,0:T(8,128)S(1)}, f32[16,512]{1,0:T(8,128)}, u32[]{:S(2)}) copy-start(f32[16,512]{1,0:T(8,128)} %get-tuple-element.58) | copy-start | bytes 98308
  62.6 22.3 %copy-start.26 = (f32[16,512]{1,0:T(8,128)S(1)}, f32[16,512]{1,0:T(8,128)}, u32[]{:S(2)}) copy-start(f32[16,512]{1,0:T(8,128)} %get-tuple-element.59) | copy-start | bytes 98308
  83.4 3.6 %collective-permute-start.1 = (bf16[128,128]{1,0:T(8,128)(2,1)}, bf16[128,128]{1,0:T(8,128)(2,1)S(1)}, u32[]{:S(2)}, u32[]{:S(2)}) collective-permute-start(bf16[128,128]{1,0:T(8,128)(2,1)} %shard_map.55), channel_id=1, source_target_pairs={{0,1},{1,0},{2,3},{3,2},{4,5},{5,4},{6,7},{7,6},{8,9},{9,8},{10,11... | collective-permute-start | bytes 98312 | tf_op jit(solution)/shard_map/ppermute | solution.py:181
  (23 other events, 440.3 us)

commit v15 on v13

--- a/solution.py
+++ b/solution.py
@@ -58,7 +58,9 @@
         rows = pl.ds(top, block)
         for i in range(shot_dev):
             for r in range(receiver_dev):
-                weights = [counts_ref[i, r, rows, h * groups : (h + 1) * groups] for h in range(shot_dev)]
+                weights = [
+                    counts_ref[i, r, rows, h * groups : (h + 1) * groups].astype(jnp.float32) for h in range(shot_dev)
+                ]
                 for f in range(local_bins):
                     real_sum = None
                     imag_sum = None
@@ -158,7 +160,7 @@
     codes = codes.reshape(groups, shot_dev, receiver_dev, KMAX).transpose(1, 2, 0, 3)
     counts = jnp.sum(
         (codes[..., None] == jnp.arange(shots, dtype=jnp.int32)).astype(jnp.float32), axis=3
-    )
+    ).astype(jnp.bfloat16)
     kernel = functools.partial(
         multiply_kernel, local_bins=local_bins, shot_dev=shot_dev, receiver_dev=receiver_dev, groups=groups
     )

time: 90.1 us -> 89.8 us (level)
  transfers between devices with their start and end apart: 2 -> 2, of which waited for: 2 -> 2; matrix products, arithmetic and copies ran while one was open for 24% -> 23% of each run, Pallas kernels for 0% -> 0%
where the time goes in v15:
time: 89.8 us; the launch traced here: 89.5 us
  Pallas kernels  20.6 us (23%)
  other arithmetic  18.5 us (21%)
  starting transfers between devices  17.1 us (19%)
  waiting for transfers between devices  16.2 us (18%)
  local copies, waits for them, and re-layouts  11.2 us (12%)
  blocking collectives  2.94 us (3%)
  matrix products  2.72 us (3%)
    pallas_call x1, Pallas kernels, shards(): pl.pallas_call(kernel, out_shape=jax.ShapeDtypeStruct((groups, rows * rec...  20.6 us
    all_to_all x1, waiting for transfers between devices, shards(): incoming = lax.all_to_all(outgoing, 'shot', 1, 1, tiled=True)  15.6 us
    reduce_sum x1, other arithmetic, shards(): jnp.sum((codes[..., None] == jnp.arange(shots, dtype=jnp.int32)).astype(j...  14.4 us
    all_to_all x1, starting transfers between devices, shards(): incoming = lax.all_to_all(outgoing, 'shot', 1, 1, tiled=True)  13.8 us
    ppermute x1, starting transfers between devices, shards(): theirs = lax.ppermute(theirs, 'freq', [(0, 1), (1, 0)])  3.33 us
    all_gather x1, blocking collectives, shards(): piece = lax.all_gather(back, 'freq', axis=0, tiled=False)  2.94 us
    select_n x1, local copies, waits for them, and re-layouts, shards(): jnp.where(used, aperture % shot_dev * groups + aperture // shot_dev, -1)  2.29 us
    dot_general x1, matrix products, shards(): lax.dot_general(jnp.concatenate([piece, piece], axis=2), jnp.concatenate(...  2.08 us
  transfers between devices with their start and end apart: 2, of which 2 were waited for; matrix products, arithmetic and copies ran while one was open for 23% of the time, Pallas kernels for 0%

profile of v15, /device:TPU:1, one launch (start us, length us, event | category | flops | bytes accessed | tf_op | source)
XLA Modules:
  0.0 89.5 jit_solution(18218772632885312754)
XLA Ops:
  0.0 1.0 %fusion.25 = (f32[8,1,512]{2,0,1:T(8,128)S(1)}, f32[8,1,512]{2,0,1:T(8,128)S(1)}) fusion(s32[512]{0:T(512)S(1)} %iota_add_fusion.1, s32[8]{0:T(128)} %param.6), kind=kLoop, calls=%fused_computation.55 | loop fusion | flops 61440 | bytes 34848 | tf_op jit(solution)/shard_map/cos | solution.py:34
  1.0 0.6 copy-done
  1.6 0.6 fusion
  2.3 3.3 %collective-permute-start = (f32[4,2,2,1024]{3,0,2,1:T(4,128)S(1)}, f32[4,2,2,1024]{3,0,2,1:T(4,128)S(1)}, u32[]{:S(2)}, u32[]{:S(2)}) collective-permute-start(f32[4,2,2,1024]{3,0,2,1:T(4,128)S(1)} %constant_dynamic-slice_fusion), channel_id=1, source_target_pairs={{0,1},{1,0},{2,3},{3,2},{4,5},{5,4},{6,7},{7,6},{8,9},{9,8},{10,11... | collective-permute-start | bytes 196616 | tf_op jit(solution)/shard_map/ppermute | solution.py:141
  5.9 0.6 collective-permute-done
  6.5 0.5 slice.193
  7.0 0.5 slice.192
  7.6 0.6 reshape.345
  8.7 1.7 %pad_maximum_fusion = bf16[33,128,128]{2,0,1:T(8,128)(2,1)} fusion(bf16[32,128,128]{2,0,1:T(8,128)(2,1)S(1)} %broadcast_in_dim.15, bf16[1,128,128]{2,0,1:T(2,128)(2,1)S(1)} %copy.46), kind=kLoop, calls=%fused_computation.5 | loop fusion | flops 2162688 | bytes 2162688 | tf_op jit(solution)/shard_map/concatenate | solution.py:149
  10.4 13.8 %all-to-all-start = ((bf16[33,128,128]{2,0,1:T(8,128)(2,1)}), bf16[33,128,128]{2,0,1:T(8,128)(2,1)S(1)}, u32[]{:S(2)}, u32[]{:S(2)}) async-start(bf16[33,128,128]{2,0,1:T(8,128)(2,1)} %pad_maximum_fusion), calls=%async_computation | async-start | bytes 2621440 | tf_op jit(solution)/shard_map/all_to_all | solution.py:157
  24.2 0.4 slice_reduce_fusion.29
  24.5 0.5 slice_reduce_fusion.30
  25.4 0.2 subtract_convert_fusion
  25.7 1.0 %fusion.4 = s32[256,8,32]{0,2,1:T(8,128)} fusion(s32[256,8,32]{0,2,1:T(8,128)S(1)} %copy-done.1, s32[256,8]{0,1:T(8,128)S(1)} %copy-done.2), kind=kLoop, calls=%fused_computation.13 | loop fusion | flops 1507328 | bytes 532480 | tf_op jit(solution)/shard_map/jit(_where)/select_n | solution.py:159
  26.7 2.3 %copy.47 = s32[256,8,32]{2,1,0:T(8,128)} copy(s32[256,8,32]{0,2,1:T(8,128)} %fusion.4) | data formatting | bytes 524288 | tf_op jit(solution)/shard_map/jit(_where)/select_n | solution.py:159
  29.0 1.6 %copy.48 = s32[2,8,128,32]{3,2,1,0:T(8,128)S(1)} copy(s32[2,8,128,32]{3,1,0,2:T(8,128)} %bitcast.20) | data formatting | bytes 524288 | tf_op jit(solution)/shard_map/transpose | solution.py:160
  30.5 14.4 %convert_reduce_fusion.counts_ref = bf16[2,8,128,256]{3,2,1,0:T(8,128)(2,1)} fusion(s32[2,8,128,32]{3,2,1,0:T(8,128)S(1)} %copy.48), kind=kLoop, calls=%fused_computation | loop fusion | flops 49807360 | bytes 1310720 | tf_op jit(solution)/shard_map/reduce_sum | solution.py:161
  45.0 15.6 %all-to-all-done = bf16[33,128,128]{2,0,1:T(8,128)(2,1)S(1)} async-done(((bf16[33,128,128]{2,0,1:T(8,128)(2,1)}), bf16[33,128,128]{2,0,1:T(8,128)(2,1)S(1)}, u32[]{:S(2)}, u32[]{:S(2)}) %all-to-all-start) | async-done | bytes 1081376 | tf_op jit(solution)/shard_map/all_to_all | solution.py:157
  60.6 1.2 %copy.49.incoming_ref = bf16[33,128,128]{2,1,0:T(8,128)(2,1)} copy(bf16[33,128,128]{2,0,1:T(8,128)(2,1)S(1)} %all-to-all-done) | data formatting | bytes 2162688 | tf_op jit(solution)/shard_map/all_to_all | solution.py:157
  61.8 20.6 %shard_map.55 = bf16[128,128]{1,0:T(8,128)(2,1)} custom-call(bf16[33,128,128]{2,1,0:T(8,128)(2,1)} %copy.49.incoming_ref, bf16[2,8,128,256]{3,2,1,0:T(8,128)(2,1)} %convert_reduce_fusion.counts_ref), custom_call_target="tpu_custom_call" | custom-call | flops 33554432 | bytes 4194304 | tf_op jit(solution)/shard_map/pallas_call | solution.py:167
  82.4 2.9 %all-gather = bf16[256,128]{1,0:T(8,128)(2,1)S(1)} all-gather(bf16[128,128]{1,0:T(8,128)(2,1)} %shard_map.55), channel_id=2, replica_groups=mesh['shot'=128,'freq'=2] {'freq'}, dimensions={0}, use_global_device_ids=true | all-gather | bytes 98304 | tf_op jit(solution)/shard_map/all_gather | solution.py:183
  85.5 0.5 copy.51
  86.0 1.5 %reshape.348 = bf16[2,1024,16]{1,2,0:T(8,128)(2,1)S(1)} reshape(bf16[2,128,8,2,4,2]{2,1,5,4,3,0:T(8,128)(2,1)S(1)} %copy.51) | data formatting | bytes 131072 | tf_op jit(solution)/shard_map/reshape | solution.py:185
  87.4 2.1 %convolution_convert_fusion = bf16[2,1024,512]{2,1,0:T(8,128)(2,1)} fusion(bf16[2,1024,16]{1,2,0:T(8,128)(2,1)S(1)} %reshape.348, bf16[2,16,512]{2,1,0:T(8,128)(2,1)S(1)} %get-tuple-element.42, bf16[2,16,512]{2,1,0:T(8,128)(2,1)S(1)} %get-tuple-element.43), kind=kOutput, calls=%fused_computation.4 | convolution fusion | flops 68550656 | bytes 2228224 | tf_op jit(solution)/shard_map/dot_general | solution.py:200
  (31 shorter events, 1.4 us)
Async XLA Ops:
  0.0 1.6 %copy-start = (bf16[2,1024,512]{2,1,0:T(8,128)(2,1)S(1)}, bf16[2,1024,512]{2,1,0:T(8,128)(2,1)}, u32[]{:S(2)}) copy-start(bf16[2,1024,512]{2,1,0:T(8,128)(2,1)} %param.5) | copy-start | bytes 6291460
  0.0 5.6 %copy-start.3 = (s32[8]{0:T(128)S(1)}, s32[8]{0:T(128)}, u32[]{:S(2)}) copy-start(s32[8]{0:T(128)} %param.6) | copy-start | bytes 100
  0.0 5.9 %copy-start.4 = (bf16[2,31]{1,0:T(2,128)(2,1)S(1)}, bf16[2,31]{1,0:T(2,128)(2,1)}, u32[]{:S(2)}) copy-start(bf16[2,31]{1,0:T(2,128)(2,1)} %param.9) | copy-start | bytes 376
  2.3 4.2 %collective-permute-start = (f32[4,2,2,1024]{3,0,2,1:T(4,128)S(1)}, f32[4,2,2,1024]{3,0,2,1:T(4,128)S(1)}, u32[]{:S(2)}, u32[]{:S(2)}) collective-permute-start(f32[4,2,2,1024]{3,0,2,1:T(4,128)S(1)} %constant_dynamic-slice_fusion), channel_id=1, source_target_pairs={{0,1},{1,0},{2,3},{3,2},{4,5},{5,4},{6,7},{7,6},{8,9},{9,8},{10,11... | collective-permute-start | bytes 196616 | tf_op jit(solution)/shard_map/ppermute | solution.py:141
  10.4 50.2 %all-to-all-start = ((bf16[33,128,128]{2,0,1:T(8,128)(2,1)}), bf16[33,128,128]{2,0,1:T(8,128)(2,1)S(1)}, u32[]{:S(2)}, u32[]{:S(2)}) async-start(bf16[33,128,128]{2,0,1:T(8,128)(2,1)} %pad_maximum_fusion), calls=%async_computation | async-start | bytes 2621440 | tf_op jit(solution)/shard_map/all_to_all | solution.py:157
  24.2 1.5 %copy-start.1 = (s32[256,8,32]{0,2,1:T(8,128)S(1)}, s32[256,8,32]{0,2,1:T(8,128)}, u32[]{:S(2)}) copy-start(s32[256,8,32]{0,2,1:T(8,128)} %param.7) | copy-start | bytes 786436
  24.2 1.5 %copy-start.2 = (s32[256,8]{0,1:T(8,128)S(1)}, s32[256,8]{0,1:T(8,128)}, u32[]{:S(2)}) copy-start(s32[256,8]{0,1:T(8,128)} %param.8) | copy-start | bytes 24580

commit v16 on v13

--- a/solution.py
+++ b/solution.py
@@ -112,7 +112,19 @@
     )
     every.wait_send()
     every.wait_recv()
-    out_ref[...] = recv_ref[...].astype(out_ref.dtype)
+    qt_ref[...] = recv_ref[...].T
+    width = groups * receiver_dev
+    owners = lax.broadcasted_iota(jnp.int32, (groups, width), 0)
+    places = lax.broadcasted_iota(jnp.int32, (groups, width), 1)
+    rows_out = local_bins * 2
+    for i in range(shot_dev):
+        total = None
+        for r in range(receiver_dev):
+            spread = (places == owners * receiver_dev + r).astype(jnp.bfloat16)
+            picked = qt_ref[pl.ds(i * receiver_dev + r, rows_out, stride=shot_dev * receiver_dev), :]
+            term = jnp.dot(picked.astype(jnp.bfloat16), spread, preferred_element_type=jnp.float32)
+            total = term if total is None else total + term
+        out_ref[i * rows_out : (i + 1) * rows_out, :] = total.astype(out_ref.dtype)
 
 
 def shards(traces, frequency_bins, aperture, lengths, filters):
@@ -164,7 +176,7 @@
     )
     back = pl.pallas_call(
         kernel,
-        out_shape=jax.ShapeDtypeStruct((groups, rows * receiver_dev), jnp.bfloat16),
+        out_shape=jax.ShapeDtypeStruct((shot_dev * local_bins * 2, receivers), jnp.bfloat16),
         in_specs=[pl.BlockSpec(memory_space=pltpu.VMEM)] * 2,
         out_specs=pl.BlockSpec(memory_space=pltpu.VMEM),
         scratch_shapes=[
@@ -179,8 +191,8 @@
         ),
     )(incoming, counts)
     piece = lax.all_gather(back, "freq", axis=0, tiled=False)
-    piece = piece.reshape(freq_dev, groups, local_bins, 2, shot_dev, receiver_dev)
-    piece = piece.transpose(4, 1, 5, 0, 2, 3).reshape(shot_dev, receivers, NF * 2)
+    piece = piece.reshape(freq_dev, shot_dev, local_bins * 2, receivers).transpose(1, 0, 2, 3)
+    piece = piece.reshape(shot_dev, NF * 2, receivers)
     wide = time_dev + 2 * half_taps
     wide_times = start_time - half_taps + jnp.arange(wide, dtype=jnp.int32)
     inside = (wide_times >= 0) & (wide_times < NT)
@@ -196,9 +208,9 @@
     leading = shaped.astype(jnp.bfloat16)
     trailing = (shaped - leading.astype(jnp.float32)).astype(jnp.bfloat16)
     filtered = lax.dot_general(
-        jnp.concatenate([piece, piece], axis=2),
+        jnp.concatenate([piece, piece], axis=1),
         jnp.concatenate([leading, trailing], axis=1),
-        (((2,), (1,)), ((0,), (0,))),
+        (((1,), (1,)), ((0,), (0,))),
         preferred_element_type=jnp.float32,
     )
     return filtered.astype(jnp.bfloat16)

time: 90.1 us -> 89.1 us (0.989)
  local copies, waits for them, and re-layouts: 11.2 us -> 9.12 us
  Pallas kernels: 20.9 us -> 22 us
    reshape x2 -> x0, local copies, waits for them, and re-layouts: 1.49 us -> none  [the longest x1 1.47 us: shards(): piece.transpose(4, 1, 5, 0, 2, 3).reshape(shot_dev, receivers, NF * 2)]
    pallas_call x1, Pallas kernels: 20.9 us -> 22 us  [shards(): pl.pallas_call(kernel, out_shape=jax.ShapeDtypeStruct((shot_dev * local_b...]
where the time goes in v16:
time: 89.1 us; the launch traced here: 88.8 us
  Pallas kernels  22 us (25%)
  other arithmetic  18.7 us (21%)
  starting transfers between devices  17.1 us (19%)
  waiting for transfers between devices  16 us (18%)
  local copies, waits for them, and re-layouts  9.12 us (10%)
  blocking collectives  2.94 us (3%)
  matrix products  2.71 us (3%)
    pallas_call x1, Pallas kernels, shards(): pl.pallas_call(kernel, out_shape=jax.ShapeDtypeStruct((shot_dev * local_b...  22 us
    all_to_all x1, waiting for transfers between devices, shards(): incoming = lax.all_to_all(outgoing, 'shot', 1, 1, tiled=True)  15.4 us
    reduce_sum x1, other arithmetic, shards(): jnp.sum((codes[..., None] == jnp.arange(shots, dtype=jnp.int32)).astype(j...  14.7 us
    all_to_all x1, starting transfers between devices, shards(): incoming = lax.all_to_all(outgoing, 'shot', 1, 1, tiled=True)  13.8 us
    ppermute x1, starting transfers between devices, shards(): theirs = lax.ppermute(theirs, 'freq', [(0, 1), (1, 0)])  3.33 us
    all_gather x1, blocking collectives, shards(): piece = lax.all_gather(back, 'freq', axis=0, tiled=False)  2.94 us
    select_n x1, local copies, waits for them, and re-layouts, shards(): jnp.where(used, aperture % shot_dev * groups + aperture // shot_dev, -1)  2.27 us
    dot_general x1, matrix products, shards(): lax.dot_general(jnp.concatenate([piece, piece], axis=1), jnp.concatenate(...  2.07 us
  transfers between devices with their start and end apart: 2, of which 2 were waited for; matrix products, arithmetic and copies ran while one was open for 24% of the time, Pallas kernels for 0%

profile of v16, /device:TPU:1, one launch (start us, length us, event | category | flops | bytes accessed | tf_op | source)
XLA Modules:
  0.0 88.8 jit_solution(14727698476267426334)
XLA Ops:
  0.0 1.0 %fusion.25 = (f32[8,1,512]{2,0,1:T(8,128)S(1)}, f32[8,1,512]{2,0,1:T(8,128)S(1)}) fusion(s32[512]{0:T(512)S(1)} %iota_add_fusion.1, s32[8]{0:T(128)} %param.6), kind=kLoop, calls=%fused_computation.56 | loop fusion | flops 61440 | bytes 34848 | tf_op jit(solution)/shard_map/cos | solution.py:34
  1.0 0.6 copy-done
  1.6 0.6 fusion
  2.3 3.3 %collective-permute-start = (f32[4,2,2,1024]{3,0,2,1:T(4,128)S(1)}, f32[4,2,2,1024]{3,0,2,1:T(4,128)S(1)}, u32[]{:S(2)}, u32[]{:S(2)}) collective-permute-start(f32[4,2,2,1024]{3,0,2,1:T(4,128)S(1)} %constant_dynamic-slice_fusion), channel_id=1, source_target_pairs={{0,1},{1,0},{2,3},{3,2},{4,5},{5,4},{6,7},{7,6},{8,9},{9,8},{10,11... | collective-permute-start | bytes 196616 | tf_op jit(solution)/shard_map/ppermute | solution.py:151
  5.9 0.6 collective-permute-done
  6.5 0.5 slice.193
  7.0 0.5 slice.192
  7.6 0.6 reshape.345
  8.2 0.2 copy.40
  8.7 1.7 %pad_maximum_fusion = bf16[33,128,128]{2,0,1:T(8,128)(2,1)} fusion(bf16[32,128,128]{2,0,1:T(8,128)(2,1)S(1)} %broadcast_in_dim.15, bf16[1,128,128]{2,0,1:T(2,128)(2,1)S(1)} %copy.42), kind=kLoop, calls=%fused_computation.5 | loop fusion | flops 2162688 | bytes 2162688 | tf_op jit(solution)/shard_map/concatenate | solution.py:159
  10.4 13.8 %all-to-all-start = ((bf16[33,128,128]{2,0,1:T(8,128)(2,1)}), bf16[33,128,128]{2,0,1:T(8,128)(2,1)S(1)}, u32[]{:S(2)}, u32[]{:S(2)}) async-start(bf16[33,128,128]{2,0,1:T(8,128)(2,1)} %pad_maximum_fusion), calls=%async_computation | async-start | bytes 2621440 | tf_op jit(solution)/shard_map/all_to_all | solution.py:167
  24.2 0.4 slice_reduce_fusion.29
  24.5 0.5 slice_reduce_fusion.30
  25.2 0.2 fusion.33
  25.4 0.2 subtract_convert_fusion
  25.7 1.0 %fusion.4 = s32[256,8,32]{0,2,1:T(8,128)} fusion(s32[256,8,32]{0,2,1:T(8,128)S(1)} %copy-done.1, s32[256,8]{0,1:T(8,128)S(1)} %copy-done.2), kind=kLoop, calls=%fused_computation.13 | loop fusion | flops 1507328 | bytes 532480 | tf_op jit(solution)/shard_map/jit(_where)/select_n | solution.py:169
  26.7 2.3 %copy.43 = s32[256,8,32]{2,1,0:T(8,128)} copy(s32[256,8,32]{0,2,1:T(8,128)} %fusion.4) | data formatting | bytes 524288 | tf_op jit(solution)/shard_map/jit(_where)/select_n | solution.py:169
  28.9 1.6 %copy.44 = s32[2,8,128,32]{3,2,1,0:T(8,128)S(1)} copy(s32[2,8,128,32]{3,1,0,2:T(8,128)} %bitcast.19) | data formatting | bytes 524288 | tf_op jit(solution)/shard_map/transpose | solution.py:170
  30.5 14.7 %convert_reduce_fusion.counts_ref = f32[2,8,128,256]{3,2,1,0:T(8,128)} fusion(s32[2,8,128,32]{3,2,1,0:T(8,128)S(1)} %copy.44), kind=kLoop, calls=%fused_computation | loop fusion | flops 49807360 | bytes 2359296 | tf_op jit(solution)/shard_map/reduce_sum | solution.py:171
  45.2 15.4 %all-to-all-done = bf16[33,128,128]{2,0,1:T(8,128)(2,1)S(1)} async-done(((bf16[33,128,128]{2,0,1:T(8,128)(2,1)}), bf16[33,128,128]{2,0,1:T(8,128)(2,1)S(1)}, u32[]{:S(2)}, u32[]{:S(2)}) %all-to-all-start) | async-done | bytes 1081376 | tf_op jit(solution)/shard_map/all_to_all | solution.py:167
  60.6 1.2 %copy.45.incoming_ref = bf16[33,128,128]{2,1,0:T(8,128)(2,1)} copy(bf16[33,128,128]{2,0,1:T(8,128)(2,1)S(1)} %all-to-all-done) | data formatting | bytes 2162688 | tf_op jit(solution)/shard_map/all_to_all | solution.py:167
  61.8 22.0 %shard_map.55 = bf16[16,1024]{1,0:T(8,128)(2,1)} custom-call(bf16[33,128,128]{2,1,0:T(8,128)(2,1)} %copy.45.incoming_ref, f32[2,8,128,256]{3,2,1,0:T(8,128)} %convert_reduce_fusion.counts_ref), custom_call_target="tpu_custom_call" | custom-call | flops 33554432 | bytes 4194304 | tf_op jit(solution)/shard_map/pallas_call | solution.py:177
  83.8 2.9 %all-gather = bf16[32,1024]{1,0:T(8,128)(2,1)S(1)} all-gather(bf16[16,1024]{1,0:T(8,128)(2,1)} %shard_map.55), channel_id=2, replica_groups=mesh['shot'=128,'freq'=2] {'freq'}, dimensions={0}, use_global_device_ids=true | all-gather | bytes 98304 | tf_op jit(solution)/shard_map/all_gather | solution.py:193
  86.8 2.1 %convolution_convert_fusion = bf16[2,1024,512]{2,1,0:T(8,128)(2,1)} fusion(bf16[2,16,1024]{2,1,0:T(8,128)(2,1)S(1)} %bitcast.21, bf16[2,16,512]{2,1,0:T(8,128)(2,1)S(1)} %get-tuple-element.42, bf16[2,16,512]{2,1,0:T(8,128)(2,1)S(1)} %get-tuple-element.43), kind=kOutput, calls=%fused_computation.4 | convolution fusion | flops 68550656 | bytes 2228224 | tf_op jit(solution)/shard_map/dot_general | solution.py:210
  (28 shorter events, 0.8 us)
Async XLA Ops:
  0.0 1.6 %copy-start = (bf16[2,1024,512]{2,1,0:T(8,128)(2,1)S(1)}, bf16[2,1024,512]{2,1,0:T(8,128)(2,1)}, u32[]{:S(2)}) copy-start(bf16[2,1024,512]{2,1,0:T(8,128)(2,1)} %param.5) | copy-start | bytes 6291460
  0.0 5.6 %copy-start.3 = (s32[8]{0:T(128)S(1)}, s32[8]{0:T(128)}, u32[]{:S(2)}) copy-start(s32[8]{0:T(128)} %param.6) | copy-start | bytes 100
  0.0 5.9 %copy-start.4 = (bf16[2,31]{1,0:T(2,128)(2,1)S(1)}, bf16[2,31]{1,0:T(2,128)(2,1)}, u32[]{:S(2)}) copy-start(bf16[2,31]{1,0:T(2,128)(2,1)} %param.9) | copy-start | bytes 376
  2.3 4.2 %collective-permute-start = (f32[4,2,2,1024]{3,0,2,1:T(4,128)S(1)}, f32[4,2,2,1024]{3,0,2,1:T(4,128)S(1)}, u32[]{:S(2)}, u32[]{:S(2)}) collective-permute-start(f32[4,2,2,1024]{3,0,2,1:T(4,128)S(1)} %constant_dynamic-slice_fusion), channel_id=1, source_target_pairs={{0,1},{1,0},{2,3},{3,2},{4,5},{5,4},{6,7},{7,6},{8,9},{9,8},{10,11... | collective-permute-start | bytes 196616 | tf_op jit(solution)/shard_map/ppermute | solution.py:151
  10.4 50.2 %all-to-all-start = ((bf16[33,128,128]{2,0,1:T(8,128)(2,1)}), bf16[33,128,128]{2,0,1:T(8,128)(2,1)S(1)}, u32[]{:S(2)}, u32[]{:S(2)}) async-start(bf16[33,128,128]{2,0,1:T(8,128)(2,1)} %pad_maximum_fusion), calls=%async_computation | async-start | bytes 2621440 | tf_op jit(solution)/shard_map/all_to_all | solution.py:167
  24.2 1.5 %copy-start.1 = (s32[256,8,32]{0,2,1:T(8,128)S(1)}, s32[256,8,32]{0,2,1:T(8,128)}, u32[]{:S(2)}) copy-start(s32[256,8,32]{0,2,1:T(8,128)} %param.7) | copy-start | bytes 786436
  24.2 1.5 %copy-start.2 = (s32[256,8]{0,1:T(8,128)S(1)}, s32[256,8]{0,1:T(8,128)}, u32[]{:S(2)}) copy-start(s32[256,8]{0,1:T(8,128)} %param.8) | copy-start | bytes 24580

commit v17 on v16

--- a/solution.py
+++ b/solution.py
@@ -190,9 +190,7 @@
             flops=16 * groups * shots * rows * receiver_dev // 2, transcendentals=0, bytes_accessed=4 * 1024 * 1024
         ),
     )(incoming, counts)
-    piece = lax.all_gather(back, "freq", axis=0, tiled=False)
-    piece = piece.reshape(freq_dev, shot_dev, local_bins * 2, receivers).transpose(1, 0, 2, 3)
-    piece = piece.reshape(shot_dev, NF * 2, receivers)
+    piece = lax.all_gather(back.reshape(shot_dev, local_bins * 2, receivers), "freq", axis=1, tiled=True)
     wide = time_dev + 2 * half_taps
     wide_times = start_time - half_taps + jnp.arange(wide, dtype=jnp.int32)
     inside = (wide_times >= 0) & (wide_times < NT)

time: 89.1 us -> 89.3 us (level)
  no operation moved by 1% of the time
where the time goes in v17:
time: 89.3 us; the launch traced here: 89 us
  Pallas kernels  22 us (25%)
  other arithmetic  18.7 us (21%)
  starting transfers between devices  17.1 us (19%)
  waiting for transfers between devices  16 us (18%)
  local copies, waits for them, and re-layouts  9.11 us (10%)
  blocking collectives  3.12 us (3%)
  matrix products  2.71 us (3%)
    pallas_call x1, Pallas kernels, shards(): pl.pallas_call(kernel, out_shape=jax.ShapeDtypeStruct((shot_dev * local_b...  22 us
    all_to_all x1, waiting for transfers between devices, shards(): incoming = lax.all_to_all(outgoing, 'shot', 1, 1, tiled=True)  15.4 us
    reduce_sum x1, other arithmetic, shards(): jnp.sum((codes[..., None] == jnp.arange(shots, dtype=jnp.int32)).astype(j...  14.7 us
    all_to_all x1, starting transfers between devices, shards(): incoming = lax.all_to_all(outgoing, 'shot', 1, 1, tiled=True)  13.8 us
    ppermute x1, starting transfers between devices, shards(): theirs = lax.ppermute(theirs, 'freq', [(0, 1), (1, 0)])  3.33 us
    all_gather x1, blocking collectives, shards(): lax.all_gather(back.reshape(shot_dev, local_bins * 2, receivers), 'freq',...  3.12 us
    select_n x1, local copies, waits for them, and re-layouts, shards(): jnp.where(used, aperture % shot_dev * groups + aperture // shot_dev, -1)  2.27 us
    dot_general x1, matrix products, shards(): lax.dot_general(jnp.concatenate([piece, piece], axis=1), jnp.concatenate(...  2.07 us
  transfers between devices with their start and end apart: 2, of which 2 were waited for; matrix products, arithmetic and copies ran while one was open for 24% of the time, Pallas kernels for 0%

profile of v17, /device:TPU:1, one launch (start us, length us, event | category | flops | bytes accessed | tf_op | source)
XLA Modules:
  0.0 89.0 jit_solution(7240652438592477590)
XLA Ops:
  0.0 1.0 %fusion.25 = (f32[8,1,512]{2,0,1:T(8,128)S(1)}, f32[8,1,512]{2,0,1:T(8,128)S(1)}) fusion(s32[512]{0:T(512)S(1)} %iota_add_fusion.1, s32[8]{0:T(128)} %param.6), kind=kLoop, calls=%fused_computation.55 | loop fusion | flops 61440 | bytes 34848 | tf_op jit(solution)/shard_map/cos | solution.py:34
  1.0 0.6 copy-done
  1.6 0.6 fusion
  2.3 3.3 %collective-permute-start = (f32[4,2,2,1024]{3,0,2,1:T(4,128)S(1)}, f32[4,2,2,1024]{3,0,2,1:T(4,128)S(1)}, u32[]{:S(2)}, u32[]{:S(2)}) collective-permute-start(f32[4,2,2,1024]{3,0,2,1:T(4,128)S(1)} %constant_dynamic-slice_fusion), channel_id=1, source_target_pairs={{0,1},{1,0},{2,3},{3,2},{4,5},{5,4},{6,7},{7,6},{8,9},{9,8},{10,11... | collective-permute-start | bytes 196616 | tf_op jit(solution)/shard_map/ppermute | solution.py:151
  5.9 0.6 collective-permute-done
  6.5 0.5 slice.193
  7.0 0.5 slice.192
  7.6 0.6 reshape.342
  8.2 0.2 copy.35
  8.7 1.7 %pad_maximum_fusion = bf16[33,128,128]{2,0,1:T(8,128)(2,1)} fusion(bf16[32,128,128]{2,0,1:T(8,128)(2,1)S(1)} %broadcast_in_dim.15, bf16[1,128,128]{2,0,1:T(2,128)(2,1)S(1)} %copy.37), kind=kLoop, calls=%fused_computation.5 | loop fusion | flops 2162688 | bytes 2162688 | tf_op jit(solution)/shard_map/concatenate | solution.py:159
  10.4 13.8 %all-to-all-start = ((bf16[33,128,128]{2,0,1:T(8,128)(2,1)}), bf16[33,128,128]{2,0,1:T(8,128)(2,1)S(1)}, u32[]{:S(2)}, u32[]{:S(2)}) async-start(bf16[33,128,128]{2,0,1:T(8,128)(2,1)} %pad_maximum_fusion), calls=%async_computation | async-start | bytes 2621440 | tf_op jit(solution)/shard_map/all_to_all | solution.py:167
  24.2 0.4 slice_reduce_fusion.29
  24.5 0.5 slice_reduce_fusion.30
  25.2 0.2 fusion.33
  25.4 0.2 subtract_convert_fusion
  25.7 1.0 %fusion.4 = s32[256,8,32]{0,2,1:T(8,128)} fusion(s32[256,8,32]{0,2,1:T(8,128)S(1)} %copy-done.1, s32[256,8]{0,1:T(8,128)S(1)} %copy-done.2), kind=kLoop, calls=%fused_computation.13 | loop fusion | flops 1507328 | bytes 532480 | tf_op jit(solution)/shard_map/jit(_where)/select_n | solution.py:169
  26.7 2.3 %copy.38 = s32[256,8,32]{2,1,0:T(8,128)} copy(s32[256,8,32]{0,2,1:T(8,128)} %fusion.4) | data formatting | bytes 524288 | tf_op jit(solution)/shard_map/jit(_where)/select_n | solution.py:169
  28.9 1.6 %copy.39 = s32[2,8,128,32]{3,2,1,0:T(8,128)S(1)} copy(s32[2,8,128,32]{3,1,0,2:T(8,128)} %bitcast.14) | data formatting | bytes 524288 | tf_op jit(solution)/shard_map/transpose | solution.py:170
  30.5 14.7 %convert_reduce_fusion.counts_ref = f32[2,8,128,256]{3,2,1,0:T(8,128)} fusion(s32[2,8,128,32]{3,2,1,0:T(8,128)S(1)} %copy.39), kind=kLoop, calls=%fused_computation | loop fusion | flops 49807360 | bytes 2359296 | tf_op jit(solution)/shard_map/reduce_sum | solution.py:171
  45.2 15.4 %all-to-all-done = bf16[33,128,128]{2,0,1:T(8,128)(2,1)S(1)} async-done(((bf16[33,128,128]{2,0,1:T(8,128)(2,1)}), bf16[33,128,128]{2,0,1:T(8,128)(2,1)S(1)}, u32[]{:S(2)}, u32[]{:S(2)}) %all-to-all-start) | async-done | bytes 1081376 | tf_op jit(solution)/shard_map/all_to_all | solution.py:167
  60.6 1.2 %copy.40.incoming_ref = bf16[33,128,128]{2,1,0:T(8,128)(2,1)} copy(bf16[33,128,128]{2,0,1:T(8,128)(2,1)S(1)} %all-to-all-done) | data formatting | bytes 2162688 | tf_op jit(solution)/shard_map/all_to_all | solution.py:167
  61.8 22.0 %shard_map.55 = bf16[16,1024]{1,0:T(8,128)(2,1)} custom-call(bf16[33,128,128]{2,1,0:T(8,128)(2,1)} %copy.40.incoming_ref, f32[2,8,128,256]{3,2,1,0:T(8,128)} %convert_reduce_fusion.counts_ref), custom_call_target="tpu_custom_call" | custom-call | flops 33554432 | bytes 4194304 | tf_op jit(solution)/shard_map/pallas_call | solution.py:177
  83.8 3.1 %all_gather.3 = bf16[2,16,1024]{2,1,0:T(8,128)(2,1)S(1)} all-gather(bf16[2,8,1024]{2,1,0:T(8,128)(2,1)} %bitcast.16), channel_id=1, replica_groups=mesh['shot'=128,'freq'=2] {'freq'}, dimensions={1}, use_global_device_ids=true | all-gather | bytes 98304 | tf_op jit(solution)/shard_map/all_gather | solution.py:193
  86.9 2.1 %convolution_convert_fusion = bf16[2,1024,512]{2,1,0:T(8,128)(2,1)} fusion(bf16[2,16,1024]{2,1,0:T(8,128)(2,1)S(1)} %all_gather.3, bf16[2,16,512]{2,1,0:T(8,128)(2,1)S(1)} %get-tuple-element.42, bf16[2,16,512]{2,1,0:T(8,128)(2,1)S(1)} %get-tuple-element.43), kind=kOutput, calls=%fused_computation.4 | convolution fusion | flops 68550656 | bytes 2228224 | tf_op jit(solution)/shard_map/dot_general | solution.py:208
  (27 shorter events, 0.8 us)
Async XLA Ops:
  0.0 1.6 %copy-start = (bf16[2,1024,512]{2,1,0:T(8,128)(2,1)S(1)}, bf16[2,1024,512]{2,1,0:T(8,128)(2,1)}, u32[]{:S(2)}) copy-start(bf16[2,1024,512]{2,1,0:T(8,128)(2,1)} %param.5) | copy-start | bytes 6291460
  0.0 5.6 %copy-start.3 = (s32[8]{0:T(128)S(1)}, s32[8]{0:T(128)}, u32[]{:S(2)}) copy-start(s32[8]{0:T(128)} %param.6) | copy-start | bytes 100
  0.0 5.9 %copy-start.4 = (bf16[2,31]{1,0:T(2,128)(2,1)S(1)}, bf16[2,31]{1,0:T(2,128)(2,1)}, u32[]{:S(2)}) copy-start(bf16[2,31]{1,0:T(2,128)(2,1)} %param.9) | copy-start | bytes 376
  2.3 4.2 %collective-permute-start = (f32[4,2,2,1024]{3,0,2,1:T(4,128)S(1)}, f32[4,2,2,1024]{3,0,2,1:T(4,128)S(1)}, u32[]{:S(2)}, u32[]{:S(2)}) collective-permute-start(f32[4,2,2,1024]{3,0,2,1:T(4,128)S(1)} %constant_dynamic-slice_fusion), channel_id=1, source_target_pairs={{0,1},{1,0},{2,3},{3,2},{4,5},{5,4},{6,7},{7,6},{8,9},{9,8},{10,11... | collective-permute-start | bytes 196616 | tf_op jit(solution)/shard_map/ppermute | solution.py:151
  10.4 50.2 %all-to-all-start = ((bf16[33,128,128]{2,0,1:T(8,128)(2,1)}), bf16[33,128,128]{2,0,1:T(8,128)(2,1)S(1)}, u32[]{:S(2)}, u32[]{:S(2)}) async-start(bf16[33,128,128]{2,0,1:T(8,128)(2,1)} %pad_maximum_fusion), calls=%async_computation | async-start | bytes 2621440 | tf_op jit(solution)/shard_map/all_to_all | solution.py:167
  24.2 1.5 %copy-start.1 = (s32[256,8,32]{0,2,1:T(8,128)S(1)}, s32[256,8,32]{0,2,1:T(8,128)}, u32[]{:S(2)}) copy-start(s32[256,8,32]{0,2,1:T(8,128)} %param.7) | copy-start | bytes 786436
  24.2 1.5 %copy-start.2 = (s32[256,8]{0,1:T(8,128)S(1)}, s32[256,8]{0,1:T(8,128)}, u32[]{:S(2)}) copy-start(s32[256,8]{0,1:T(8,128)} %param.8) | copy-start | bytes 24580

commit v18 on v16

--- a/solution.py
+++ b/solution.py
@@ -152,9 +152,12 @@
     spectra = (mine + theirs).astype(jnp.bfloat16)
     rows = local_bins * 2 * shot_dev
     near = spectra.reshape(rows, groups, receiver_dev).transpose(1, 0, 2).reshape(groups, rows * receiver_dev)
-    stations = jnp.concatenate(
-        [spectra[:, :, :, 0 :: 2 * stride], spectra[:, :, :, stride :: 2 * stride]], axis=-1
-    ).reshape(1, rows * shots)
+    station_of = jnp.arange(shots, dtype=jnp.int32)
+    station_of = (station_of % groups) * 2 * stride + (station_of // groups) * stride
+    selection = (jnp.arange(receivers, dtype=jnp.int32)[:, None] == station_of[None, :]).astype(jnp.bfloat16)
+    stations = jnp.dot(
+        spectra.reshape(rows, receivers), selection, preferred_element_type=jnp.float32
+    ).astype(jnp.bfloat16).reshape(1, rows * shots)
     lanes = 128
     outgoing = jnp.concatenate(
         [

time: 89.1 us -> 88.4 us (level)
  local copies, waits for them, and re-layouts: 9.12 us -> 8.17 us
    slice x2 -> x0, local copies, waits for them, and re-layouts: 0.96 us -> none  [the longest x1 0.48 us: shards(): spectra[:, :, :, stride::2 * stride]]
where the time goes in v18:
time: 88.4 us; the launch traced here: 88.1 us
  Pallas kernels  22 us (25%)
  other arithmetic  18.7 us (21%)
  starting transfers between devices  17.1 us (19%)
  waiting for transfers between devices  16 us (18%)
  local copies, waits for them, and re-layouts  8.17 us (9%)
  matrix products  3 us (3%)
  blocking collectives  2.94 us (3%)
    pallas_call x1, Pallas kernels, shards(): pl.pallas_call(kernel, out_shape=jax.ShapeDtypeStruct((shot_dev * local_b...  22 us
    all_to_all x1, waiting for transfers between devices, shards(): incoming = lax.all_to_all(outgoing, 'shot', 1, 1, tiled=True)  15.4 us
    reduce_sum x1, other arithmetic, shards(): jnp.sum((codes[..., None] == jnp.arange(shots, dtype=jnp.int32)).astype(j...  14.7 us
    all_to_all x1, starting transfers between devices, shards(): incoming = lax.all_to_all(outgoing, 'shot', 1, 1, tiled=True)  13.8 us
    ppermute x1, starting transfers between devices, shards(): theirs = lax.ppermute(theirs, 'freq', [(0, 1), (1, 0)])  3.33 us
    all_gather x1, blocking collectives, shards(): piece = lax.all_gather(back, 'freq', axis=0, tiled=False)  2.94 us
    select_n x1, local copies, waits for them, and re-layouts, shards(): jnp.where(used, aperture % shot_dev * groups + aperture // shot_dev, -1)  2.27 us
    dot_general x1, matrix products, shards(): lax.dot_general(jnp.concatenate([piece, piece], axis=1), jnp.concatenate(...  2.07 us
  transfers between devices with their start and end apart: 2, of which 2 were waited for; matrix products, arithmetic and copies ran while one was open for 24% of the time, Pallas kernels for 0%

profile of v18, /device:TPU:1, one launch (start us, length us, event | category | flops | bytes accessed | tf_op | source)
XLA Modules:
  0.0 88.1 jit_solution(16786038553986350021)
XLA Ops:
  0.0 1.0 %fusion.26 = (f32[8,1,512]{2,0,1:T(8,128)S(1)}, f32[8,1,512]{2,0,1:T(8,128)S(1)}) fusion(s32[512]{0:T(512)S(1)} %iota_add_fusion.1, s32[8]{0:T(128)} %param.6), kind=kLoop, calls=%fused_computation.58 | loop fusion | flops 61440 | bytes 34848 | tf_op jit(solution)/shard_map/cos | solution.py:34
  1.0 0.6 copy-done
  1.6 0.6 fusion
  2.3 3.3 %collective-permute-start = (f32[4,2,2,1024]{3,0,2,1:T(4,128)S(1)}, f32[4,2,2,1024]{3,0,2,1:T(4,128)S(1)}, u32[]{:S(2)}, u32[]{:S(2)}) collective-permute-start(f32[4,2,2,1024]{3,0,2,1:T(4,128)S(1)} %constant_dynamic-slice_fusion), channel_id=1, source_target_pairs={{0,1},{1,0},{2,3},{3,2},{4,5},{5,4},{6,7},{7,6},{8,9},{9,8},{10,11... | collective-permute-start | bytes 196616 | tf_op jit(solution)/shard_map/ppermute | solution.py:151
  5.6 0.2 cosine_convert_fusion
  5.9 0.6 collective-permute-done
  6.6 0.6 reshape.371
  7.2 0.3 convolution_convert_fusion.1
  7.5 0.2 copy.40
  8.0 1.7 %pad_maximum_fusion = bf16[33,128,128]{2,0,1:T(8,128)(2,1)} fusion(bf16[32,128,128]{2,0,1:T(8,128)(2,1)S(1)} %broadcast_in_dim.15, bf16[1,128,128]{2,0,1:T(2,128)(2,1)S(1)} %copy.42), kind=kLoop, calls=%fused_computation.5 | loop fusion | flops 2162688 | bytes 2162688 | tf_op jit(solution)/shard_map/concatenate | solution.py:162
  9.7 13.8 %all-to-all-start = ((bf16[33,128,128]{2,0,1:T(8,128)(2,1)}), bf16[33,128,128]{2,0,1:T(8,128)(2,1)S(1)}, u32[]{:S(2)}, u32[]{:S(2)}) async-start(bf16[33,128,128]{2,0,1:T(8,128)(2,1)} %pad_maximum_fusion), calls=%async_computation | async-start | bytes 2621440 | tf_op jit(solution)/shard_map/all_to_all | solution.py:170
  23.5 0.4 slice_reduce_fusion.29
  23.9 0.5 slice_reduce_fusion.30
  24.5 0.2 fusion.39
  24.7 0.2 subtract_convert_fusion
  25.0 1.0 %fusion.5 = s32[256,8,32]{0,2,1:T(8,128)} fusion(s32[256,8,32]{0,2,1:T(8,128)S(1)} %copy-done.1, s32[256,8]{0,1:T(8,128)S(1)} %copy-done.2), kind=kLoop, calls=%fused_computation.16 | loop fusion | flops 1507328 | bytes 532480 | tf_op jit(solution)/shard_map/jit(_where)/select_n | solution.py:172
  26.0 2.3 %copy.43 = s32[256,8,32]{2,1,0:T(8,128)} copy(s32[256,8,32]{0,2,1:T(8,128)} %fusion.5) | data formatting | bytes 524288 | tf_op jit(solution)/shard_map/jit(_where)/select_n | solution.py:172
  28.2 1.6 %copy.44 = s32[2,8,128,32]{3,2,1,0:T(8,128)S(1)} copy(s32[2,8,128,32]{3,1,0,2:T(8,128)} %bitcast.20) | data formatting | bytes 524288 | tf_op jit(solution)/shard_map/transpose | solution.py:173
  29.8 14.7 %convert_reduce_fusion.counts_ref = f32[2,8,128,256]{3,2,1,0:T(8,128)} fusion(s32[2,8,128,32]{3,2,1,0:T(8,128)S(1)} %copy.44), kind=kLoop, calls=%fused_computation | loop fusion | flops 49807360 | bytes 2359296 | tf_op jit(solution)/shard_map/reduce_sum | solution.py:174
  44.5 15.4 %all-to-all-done = bf16[33,128,128]{2,0,1:T(8,128)(2,1)S(1)} async-done(((bf16[33,128,128]{2,0,1:T(8,128)(2,1)}), bf16[33,128,128]{2,0,1:T(8,128)(2,1)S(1)}, u32[]{:S(2)}, u32[]{:S(2)}) %all-to-all-start) | async-done | bytes 1081376 | tf_op jit(solution)/shard_map/all_to_all | solution.py:170
  59.9 1.2 %copy.45.incoming_ref = bf16[33,128,128]{2,1,0:T(8,128)(2,1)} copy(bf16[33,128,128]{2,0,1:T(8,128)(2,1)S(1)} %all-to-all-done) | data formatting | bytes 2162688 | tf_op jit(solution)/shard_map/all_to_all | solution.py:170
  61.1 22.0 %shard_map.55 = bf16[16,1024]{1,0:T(8,128)(2,1)} custom-call(bf16[33,128,128]{2,1,0:T(8,128)(2,1)} %copy.45.incoming_ref, f32[2,8,128,256]{3,2,1,0:T(8,128)} %convert_reduce_fusion.counts_ref), custom_call_target="tpu_custom_call" | custom-call | flops 33554432 | bytes 4194304 | tf_op jit(solution)/shard_map/pallas_call | solution.py:180
  83.1 2.9 %all-gather = bf16[32,1024]{1,0:T(8,128)(2,1)S(1)} all-gather(bf16[16,1024]{1,0:T(8,128)(2,1)} %shard_map.55), channel_id=2, replica_groups=mesh['shot'=128,'freq'=2] {'freq'}, dimensions={0}, use_global_device_ids=true | all-gather | bytes 98304 | tf_op jit(solution)/shard_map/all_gather | solution.py:196
  86.1 2.1 %convolution_convert_fusion = bf16[2,1024,512]{2,1,0:T(8,128)(2,1)} fusion(bf16[2,16,1024]{2,1,0:T(8,128)(2,1)S(1)} %bitcast.22, bf16[2,16,512]{2,1,0:T(8,128)(2,1)S(1)} %get-tuple-element.42, bf16[2,16,512]{2,1,0:T(8,128)(2,1)S(1)} %get-tuple-element.43), kind=kOutput, calls=%fused_computation.4 | convolution fusion | flops 68550656 | bytes 2228224 | tf_op jit(solution)/shard_map/dot_general | solution.py:213
  (27 shorter events, 0.7 us)
Async XLA Ops:
  0.0 1.6 %copy-start = (bf16[2,1024,512]{2,1,0:T(8,128)(2,1)S(1)}, bf16[2,1024,512]{2,1,0:T(8,128)(2,1)}, u32[]{:S(2)}) copy-start(bf16[2,1024,512]{2,1,0:T(8,128)(2,1)} %param.5) | copy-start | bytes 6291460
  0.0 5.6 %copy-start.3 = (s32[8]{0:T(128)S(1)}, s32[8]{0:T(128)}, u32[]{:S(2)}) copy-start(s32[8]{0:T(128)} %param.6) | copy-start | bytes 100
  0.0 5.9 %copy-start.4 = (bf16[2,31]{1,0:T(2,128)(2,1)S(1)}, bf16[2,31]{1,0:T(2,128)(2,1)}, u32[]{:S(2)}) copy-start(bf16[2,31]{1,0:T(2,128)(2,1)} %param.9) | copy-start | bytes 376
  2.3 4.2 %collective-permute-start = (f32[4,2,2,1024]{3,0,2,1:T(4,128)S(1)}, f32[4,2,2,1024]{3,0,2,1:T(4,128)S(1)}, u32[]{:S(2)}, u32[]{:S(2)}) collective-permute-start(f32[4,2,2,1024]{3,0,2,1:T(4,128)S(1)} %constant_dynamic-slice_fusion), channel_id=1, source_target_pairs={{0,1},{1,0},{2,3},{3,2},{4,5},{5,4},{6,7},{7,6},{8,9},{9,8},{10,11... | collective-permute-start | bytes 196616 | tf_op jit(solution)/shard_map/ppermute | solution.py:151
  9.7 50.2 %all-to-all-start = ((bf16[33,128,128]{2,0,1:T(8,128)(2,1)}), bf16[33,128,128]{2,0,1:T(8,128)(2,1)S(1)}, u32[]{:S(2)}, u32[]{:S(2)}) async-start(bf16[33,128,128]{2,0,1:T(8,128)(2,1)} %pad_maximum_fusion), calls=%async_computation | async-start | bytes 2621440 | tf_op jit(solution)/shard_map/all_to_all | solution.py:170
  23.5 1.5 %copy-start.1 = (s32[256,8,32]{0,2,1:T(8,128)S(1)}, s32[256,8,32]{0,2,1:T(8,128)}, u32[]{:S(2)}) copy-start(s32[256,8,32]{0,2,1:T(8,128)} %param.7) | copy-start | bytes 786436
  23.5 1.5 %copy-start.2 = (s32[256,8]{0,1:T(8,128)S(1)}, s32[256,8]{0,1:T(8,128)}, u32[]{:S(2)}) copy-start(s32[256,8]{0,1:T(8,128)} %param.8) | copy-start | bytes 24580

commit v19 on v18

--- a/solution.py
+++ b/solution.py
@@ -151,7 +151,15 @@
     theirs = lax.ppermute(theirs, "freq", [(0, 1), (1, 0)])
     spectra = (mine + theirs).astype(jnp.bfloat16)
     rows = local_bins * 2 * shot_dev
-    near = spectra.reshape(rows, groups, receiver_dev).transpose(1, 0, 2).reshape(groups, rows * receiver_dev)
+    every = jnp.arange(receivers, dtype=jnp.int32)
+    flat = spectra.reshape(rows, 1, receivers)
+    spread = jnp.where(
+        (every % receiver_dev)[None, None, :] == jnp.arange(receiver_dev, dtype=jnp.int32)[None, :, None], flat, 0
+    ).reshape(rows * receiver_dev, receivers)
+    owner = (every[None, :] // receiver_dev == jnp.arange(groups, dtype=jnp.int32)[:, None]).astype(jnp.bfloat16)
+    near = lax.dot_general(
+        owner, spread, (((1,), (1,)), ((), ())), preferred_element_type=jnp.float32
+    ).astype(jnp.bfloat16)
     station_of = jnp.arange(shots, dtype=jnp.int32)
     station_of = (station_of % groups) * 2 * stride + (station_of // groups) * stride
     selection = (jnp.arange(receivers, dtype=jnp.int32)[:, None] == station_of[None, :]).astype(jnp.bfloat16)

time: 88.4 us -> 87.8 us (level)
  no operation moved by 1% of the time
where the time goes in v19:
time: 87.8 us; the launch traced here: 87.5 us
  Pallas kernels  22 us (25%)
  other arithmetic  18.8 us (21%)
  starting transfers between devices  17.1 us (19%)
  waiting for transfers between devices  15.9 us (18%)
  local copies, waits for them, and re-layouts  7.29 us (8%)
  matrix products  3.24 us (4%)
  blocking collectives  2.94 us (3%)
    pallas_call x1, Pallas kernels, shards(): pl.pallas_call(kernel, out_shape=jax.ShapeDtypeStruct((shot_dev * local_b...  22 us
    all_to_all x1, waiting for transfers between devices, shards(): incoming = lax.all_to_all(outgoing, 'shot', 1, 1, tiled=True)  15.4 us
    reduce_sum x1, other arithmetic, shards(): jnp.sum((codes[..., None] == jnp.arange(shots, dtype=jnp.int32)).astype(j...  14.7 us
    all_to_all x1, starting transfers between devices, shards(): incoming = lax.all_to_all(outgoing, 'shot', 1, 1, tiled=True)  13.8 us
    ppermute x1, starting transfers between devices, shards(): theirs = lax.ppermute(theirs, 'freq', [(0, 1), (1, 0)])  3.33 us
    all_gather x1, blocking collectives, shards(): piece = lax.all_gather(back, 'freq', axis=0, tiled=False)  2.94 us
    select_n x1, local copies, waits for them, and re-layouts, shards(): jnp.where(used, aperture % shot_dev * groups + aperture // shot_dev, -1)  2.27 us
    dot_general x1, matrix products, shards(): lax.dot_general(jnp.concatenate([piece, piece], axis=1), jnp.concatenate(...  2.07 us
  transfers between devices with their start and end apart: 2, of which 2 were waited for; matrix products, arithmetic and copies ran while one was open for 24% of the time, Pallas kernels for 0%

profile of v19, /device:TPU:1, one launch (start us, length us, event | category | flops | bytes accessed | tf_op | source)
XLA Modules:
  0.0 87.5 jit_solution(1419772823495127430)
XLA Ops:
  0.0 1.0 %fusion.33 = (f32[8,1,512]{2,0,1:T(8,128)S(1)}, f32[8,1,512]{2,0,1:T(8,128)S(1)}) fusion(s32[512]{0:T(512)S(1)} %iota_add_fusion.1, s32[8]{0:T(128)} %param.6), kind=kLoop, calls=%fused_computation.68 | loop fusion | flops 61440 | bytes 34848 | tf_op jit(solution)/shard_map/cos | solution.py:34
  1.0 0.6 copy-done
  1.6 0.6 fusion
  2.3 3.3 %collective-permute-start = (f32[4,2,2,1024]{3,0,2,1:T(4,128)S(1)}, f32[4,2,2,1024]{3,0,2,1:T(4,128)S(1)}, u32[]{:S(2)}, u32[]{:S(2)}) collective-permute-start(f32[4,2,2,1024]{3,0,2,1:T(4,128)S(1)} %constant_dynamic-slice_fusion), channel_id=1, source_target_pairs={{0,1},{1,0},{2,3},{3,2},{4,5},{5,4},{6,7},{7,6},{8,9},{9,8},{10,11... | collective-permute-start | bytes 196616 | tf_op jit(solution)/shard_map/ppermute | solution.py:151
  5.7 0.2 cosine_convert_fusion
  6.0 0.5 collective-permute-done
  6.6 0.3 convolution_convert_fusion.2
  6.9 0.2 fusion.2
  7.4 1.7 %pad_maximum_fusion = bf16[33,128,128]{2,0,1:T(8,128)(2,1)} fusion(bf16[32,128,128]{2,0,1:T(8,128)(2,1)S(1)} %broadcast_in_dim.45, bf16[1,128,128]{2,0,1:T(2,128)(2,1)S(1)} %copy.31), kind=kLoop, calls=%fused_computation.5 | loop fusion | flops 2162688 | bytes 2162688 | tf_op jit(solution)/shard_map/concatenate | solution.py:170
  9.0 13.8 %all-to-all-start = ((bf16[33,128,128]{2,0,1:T(8,128)(2,1)}), bf16[33,128,128]{2,0,1:T(8,128)(2,1)S(1)}, u32[]{:S(2)}, u32[]{:S(2)}) async-start(bf16[33,128,128]{2,0,1:T(8,128)(2,1)} %pad_maximum_fusion), calls=%async_computation | async-start | bytes 2621440 | tf_op jit(solution)/shard_map/all_to_all | solution.py:178
  22.8 0.4 slice_reduce_fusion.29
  23.2 0.5 slice_reduce_fusion.30
  23.7 0.2 fusion.55
  23.9 0.2 fusion.54
  24.1 0.2 subtract_convert_fusion
  24.4 1.0 %fusion.6 = s32[256,8,32]{0,2,1:T(8,128)} fusion(s32[256,8,32]{0,2,1:T(8,128)S(1)} %copy-done.1, s32[256,8]{0,1:T(8,128)S(1)} %copy-done.2), kind=kLoop, calls=%fused_computation.19 | loop fusion | flops 1507328 | bytes 532480 | tf_op jit(solution)/shard_map/jit(_where)/select_n | solution.py:180
  25.3 2.3 %copy.32 = s32[256,8,32]{2,1,0:T(8,128)} copy(s32[256,8,32]{0,2,1:T(8,128)} %fusion.6) | data formatting | bytes 524288 | tf_op jit(solution)/shard_map/jit(_where)/select_n | solution.py:180
  27.6 1.6 %copy.33 = s32[2,8,128,32]{3,2,1,0:T(8,128)S(1)} copy(s32[2,8,128,32]{3,1,0,2:T(8,128)} %bitcast.23) | data formatting | bytes 524288 | tf_op jit(solution)/shard_map/transpose | solution.py:181
  29.2 14.7 %convert_reduce_fusion.counts_ref = f32[2,8,128,256]{3,2,1,0:T(8,128)} fusion(s32[2,8,128,32]{3,2,1,0:T(8,128)S(1)} %copy.33), kind=kLoop, calls=%fused_computation | loop fusion | flops 49807360 | bytes 2359296 | tf_op jit(solution)/shard_map/reduce_sum | solution.py:182
  43.8 15.4 %all-to-all-done = bf16[33,128,128]{2,0,1:T(8,128)(2,1)S(1)} async-done(((bf16[33,128,128]{2,0,1:T(8,128)(2,1)}), bf16[33,128,128]{2,0,1:T(8,128)(2,1)S(1)}, u32[]{:S(2)}, u32[]{:S(2)}) %all-to-all-start) | async-done | bytes 1081376 | tf_op jit(solution)/shard_map/all_to_all | solution.py:178
  59.2 1.2 %copy.34.incoming_ref = bf16[33,128,128]{2,1,0:T(8,128)(2,1)} copy(bf16[33,128,128]{2,0,1:T(8,128)(2,1)S(1)} %all-to-all-done) | data formatting | bytes 2162688 | tf_op jit(solution)/shard_map/all_to_all | solution.py:178
  60.5 22.0 %shard_map.55 = bf16[16,1024]{1,0:T(8,128)(2,1)} custom-call(bf16[33,128,128]{2,1,0:T(8,128)(2,1)} %copy.34.incoming_ref, f32[2,8,128,256]{3,2,1,0:T(8,128)} %convert_reduce_fusion.counts_ref), custom_call_target="tpu_custom_call" | custom-call | flops 33554432 | bytes 4194304 | tf_op jit(solution)/shard_map/pallas_call | solution.py:188
  82.5 2.9 %all-gather = bf16[32,1024]{1,0:T(8,128)(2,1)S(1)} all-gather(bf16[16,1024]{1,0:T(8,128)(2,1)} %shard_map.55), channel_id=2, replica_groups=mesh['shot'=128,'freq'=2] {'freq'}, dimensions={0}, use_global_device_ids=true | all-gather | bytes 98304 | tf_op jit(solution)/shard_map/all_gather | solution.py:204
  85.4 2.1 %convolution_convert_fusion = bf16[2,1024,512]{2,1,0:T(8,128)(2,1)} fusion(bf16[2,16,1024]{2,1,0:T(8,128)(2,1)S(1)} %bitcast.24, bf16[2,16,512]{2,1,0:T(8,128)(2,1)S(1)} %get-tuple-element.42, bf16[2,16,512]{2,1,0:T(8,128)(2,1)S(1)} %get-tuple-element.43), kind=kOutput, calls=%fused_computation.4 | convolution fusion | flops 68550656 | bytes 2228224 | tf_op jit(solution)/shard_map/dot_general | solution.py:221
  (29 shorter events, 0.4 us)
Async XLA Ops:
  0.0 1.6 %copy-start = (bf16[2,1024,512]{2,1,0:T(8,128)(2,1)S(1)}, bf16[2,1024,512]{2,1,0:T(8,128)(2,1)}, u32[]{:S(2)}) copy-start(bf16[2,1024,512]{2,1,0:T(8,128)(2,1)} %param.5) | copy-start | bytes 6291460
  0.0 5.7 %copy-start.3 = (s32[8]{0:T(128)S(1)}, s32[8]{0:T(128)}, u32[]{:S(2)}) copy-start(s32[8]{0:T(128)} %param.6) | copy-start | bytes 100
  0.0 5.9 %copy-start.4 = (bf16[2,31]{1,0:T(2,128)(2,1)S(1)}, bf16[2,31]{1,0:T(2,128)(2,1)}, u32[]{:S(2)}) copy-start(bf16[2,31]{1,0:T(2,128)(2,1)} %param.9) | copy-start | bytes 376
  2.3 4.2 %collective-permute-start = (f32[4,2,2,1024]{3,0,2,1:T(4,128)S(1)}, f32[4,2,2,1024]{3,0,2,1:T(4,128)S(1)}, u32[]{:S(2)}, u32[]{:S(2)}) collective-permute-start(f32[4,2,2,1024]{3,0,2,1:T(4,128)S(1)} %constant_dynamic-slice_fusion), channel_id=1, source_target_pairs={{0,1},{1,0},{2,3},{3,2},{4,5},{5,4},{6,7},{7,6},{8,9},{9,8},{10,11... | collective-permute-start | bytes 196616 | tf_op jit(solution)/shard_map/ppermute | solution.py:151
  9.0 50.2 %all-to-all-start = ((bf16[33,128,128]{2,0,1:T(8,128)(2,1)}), bf16[33,128,128]{2,0,1:T(8,128)(2,1)S(1)}, u32[]{:S(2)}, u32[]{:S(2)}) async-start(bf16[33,128,128]{2,0,1:T(8,128)(2,1)} %pad_maximum_fusion), calls=%async_computation | async-start | bytes 2621440 | tf_op jit(solution)/shard_map/all_to_all | solution.py:178
  22.8 1.5 %copy-start.1 = (s32[256,8,32]{0,2,1:T(8,128)S(1)}, s32[256,8,32]{0,2,1:T(8,128)}, u32[]{:S(2)}) copy-start(s32[256,8,32]{0,2,1:T(8,128)} %param.7) | copy-start | bytes 786436
  22.8 1.5 %copy-start.2 = (s32[256,8]{0,1:T(8,128)S(1)}, s32[256,8]{0,1:T(8,128)}, u32[]{:S(2)}) copy-start(s32[256,8]{0,1:T(8,128)} %param.8) | copy-start | bytes 24580

commit v20 on v19

--- a/solution.py
+++ b/solution.py
@@ -35,7 +35,7 @@
 
 
 def multiply_kernel(
-    incoming_ref, counts_ref, out_ref, qt_ref, acc_ref, recv_ref, sems, *, local_bins, shot_dev, receiver_dev, groups
+    incoming_ref, counts_ref, out_ref, qt_ref, acc_ref, recv_ref, both_ref, sems, pair_sems, *, local_bins, shot_dev, receiver_dev, groups
 ):
     qt_ref[...] = incoming_ref[0].astype(jnp.float32).T
     me = lax.axis_index("shot")
@@ -124,7 +124,19 @@
             picked = qt_ref[pl.ds(i * receiver_dev + r, rows_out, stride=shot_dev * receiver_dev), :]
             term = jnp.dot(picked.astype(jnp.bfloat16), spread, preferred_element_type=jnp.float32)
             total = term if total is None else total + term
-        out_ref[i * rows_out : (i + 1) * rows_out, :] = total.astype(out_ref.dtype)
+        both_ref[i, pl.ds(half * rows_out, rows_out), :] = total
+    swap = pltpu.make_async_remote_copy(
+        src_ref=both_ref.at[:, pl.ds(half * rows_out, rows_out), :],
+        dst_ref=both_ref.at[:, pl.ds(half * rows_out, rows_out), :],
+        send_sem=pair_sems.at[0],
+        recv_sem=pair_sems.at[1],
+        device_id=(me, 1 - half),
+        device_id_type=pl.DeviceIdType.MESH,
+    )
+    swap.start()
+    swap.wait_send()
+    swap.wait_recv()
+    out_ref[...] = both_ref[...].astype(out_ref.dtype)
 
 
 def shards(traces, frequency_bins, aperture, lengths, filters):
@@ -187,13 +199,15 @@
     )
     back = pl.pallas_call(
         kernel,
-        out_shape=jax.ShapeDtypeStruct((shot_dev * local_bins * 2, receivers), jnp.bfloat16),
+        out_shape=jax.ShapeDtypeStruct((shot_dev, NF * 2, receivers), jnp.bfloat16),
         in_specs=[pl.BlockSpec(memory_space=pltpu.VMEM)] * 2,
         out_specs=pl.BlockSpec(memory_space=pltpu.VMEM),
         scratch_shapes=[
             pltpu.VMEM((rows * receiver_dev, groups), jnp.float32),
             pltpu.VMEM((groups, rows * receiver_dev), jnp.float32),
             pltpu.VMEM((groups, rows * receiver_dev), jnp.float32),
+            pltpu.VMEM((shot_dev, NF * 2, receivers), jnp.float32),
+            pltpu.SemaphoreType.DMA((2,)),
             pltpu.SemaphoreType.DMA((2,)),
         ],
         compiler_params=pltpu.CompilerParams(has_side_effects=True),
@@ -201,9 +215,7 @@
             flops=16 * groups * shots * rows * receiver_dev // 2, transcendentals=0, bytes_accessed=4 * 1024 * 1024
         ),
     )(incoming, counts)
-    piece = lax.all_gather(back, "freq", axis=0, tiled=False)
-    piece = piece.reshape(freq_dev, shot_dev, local_bins * 2, receivers).transpose(1, 0, 2, 3)
-    piece = piece.reshape(shot_dev, NF * 2, receivers)
+    piece = back
     wide = time_dev + 2 * half_taps
     wide_times = start_time - half_taps + jnp.arange(wide, dtype=jnp.int32)
     inside = (wide_times >= 0) & (wide_times < NT)

time: 87.8 us -> 87.8 us (level)
  blocking collectives: 2.94 us -> 0 us
  Pallas kernels: 22 us -> 24 us
  matrix products: 3.24 us -> 4.16 us
    all_gather x1 -> x0, blocking collectives: 2.94 us -> none  [shards(): piece = lax.all_gather(back, 'freq', axis=0, tiled=False)]
    pallas_call x1, Pallas kernels: 22 us -> 24 us  [shards(): pl.pallas_call(kernel, out_shape=jax.ShapeDtypeStruct((shot_dev, NF * 2,...]
    dot_general x1, matrix products: 2.07 us -> 2.99 us  [shards(): lax.dot_general(jnp.concatenate([piece, piece], axis=1), jnp.concatenate(...]
where the time goes in v20:
time: 87.8 us; the launch traced here: 87.5 us
  Pallas kernels  24 us (27%)
  other arithmetic  18.8 us (21%)
  starting transfers between devices  17.1 us (19%)
  waiting for transfers between devices  15.9 us (18%)
  local copies, waits for them, and re-layouts  7.28 us (8%)
  matrix products  4.16 us (5%)
    pallas_call x1, Pallas kernels, shards(): pl.pallas_call(kernel, out_shape=jax.ShapeDtypeStruct((shot_dev, NF * 2,...  24 us
    all_to_all x1, waiting for transfers between devices, shards(): incoming = lax.all_to_all(outgoing, 'shot', 1, 1, tiled=True)  15.4 us
    reduce_sum x1, other arithmetic, shards(): jnp.sum((codes[..., None] == jnp.arange(shots, dtype=jnp.int32)).astype(j...  14.7 us
    all_to_all x1, starting transfers between devices, shards(): incoming = lax.all_to_all(outgoing, 'shot', 1, 1, tiled=True)  13.8 us
    ppermute x1, starting transfers between devices, shards(): theirs = lax.ppermute(theirs, 'freq', [(0, 1), (1, 0)])  3.33 us
    dot_general x1, matrix products, shards(): lax.dot_general(jnp.concatenate([piece, piece], axis=1), jnp.concatenate(...  2.99 us
    select_n x1, local copies, waits for them, and re-layouts, shards(): jnp.where(used, aperture % shot_dev * groups + aperture // shot_dev, -1)  2.27 us
  transfers between devices with their start and end apart: 2, of which 2 were waited for; matrix products, arithmetic and copies ran while one was open for 24% of the time, Pallas kernels for 0%

profile of v20, /device:TPU:1, one launch (start us, length us, event | category | flops | bytes accessed | tf_op | source)
XLA Modules:
  0.0 87.5 jit_solution(3529587363098484776)
XLA Ops:
  0.0 1.0 %fusion.33 = (f32[8,1,512]{2,0,1:T(8,128)S(1)}, f32[8,1,512]{2,0,1:T(8,128)S(1)}) fusion(s32[512]{0:T(512)S(1)} %iota_add_fusion.1, s32[8]{0:T(128)} %param.6), kind=kLoop, calls=%fused_computation.67 | loop fusion | flops 61440 | bytes 34848 | tf_op jit(solution)/shard_map/cos | solution.py:34
  1.0 0.6 copy-done
  1.6 0.6 fusion
  2.3 3.3 %collective-permute-start = (f32[4,2,2,1024]{3,0,2,1:T(4,128)S(1)}, f32[4,2,2,1024]{3,0,2,1:T(4,128)S(1)}, u32[]{:S(2)}, u32[]{:S(2)}) collective-permute-start(f32[4,2,2,1024]{3,0,2,1:T(4,128)S(1)} %constant_dynamic-slice_fusion), channel_id=1, source_target_pairs={{0,1},{1,0},{2,3},{3,2},{4,5},{5,4},{6,7},{7,6},{8,9},{9,8},{10,11... | collective-permute-start | bytes 196616 | tf_op jit(solution)/shard_map/ppermute | solution.py:163
  5.7 0.2 cosine_convert_fusion
  6.0 0.5 collective-permute-done
  6.6 0.3 convolution_convert_fusion.2
  6.9 0.2 fusion.2
  7.2 0.1 broadcast_in_dim.45
  7.4 1.7 %pad_maximum_fusion = bf16[33,128,128]{2,0,1:T(8,128)(2,1)} fusion(bf16[32,128,128]{2,0,1:T(8,128)(2,1)S(1)} %broadcast_in_dim.45, bf16[1,128,128]{2,0,1:T(2,128)(2,1)S(1)} %copy.26), kind=kLoop, calls=%fused_computation.5 | loop fusion | flops 2162688 | bytes 2162688 | tf_op jit(solution)/shard_map/concatenate | solution.py:182
  9.0 13.8 %all-to-all-start = ((bf16[33,128,128]{2,0,1:T(8,128)(2,1)}), bf16[33,128,128]{2,0,1:T(8,128)(2,1)S(1)}, u32[]{:S(2)}, u32[]{:S(2)}) async-start(bf16[33,128,128]{2,0,1:T(8,128)(2,1)} %pad_maximum_fusion), calls=%async_computation | async-start | bytes 2621440 | tf_op jit(solution)/shard_map/all_to_all | solution.py:190
  22.8 0.4 slice_reduce_fusion.29
  23.2 0.5 slice_reduce_fusion.30
  23.7 0.2 fusion.55
  23.9 0.2 fusion.54
  24.1 0.2 subtract_convert_fusion
  24.4 1.0 %fusion.6 = s32[256,8,32]{0,2,1:T(8,128)} fusion(s32[256,8,32]{0,2,1:T(8,128)S(1)} %copy-done.1, s32[256,8]{0,1:T(8,128)S(1)} %copy-done.2), kind=kLoop, calls=%fused_computation.19 | loop fusion | flops 1507328 | bytes 532480 | tf_op jit(solution)/shard_map/jit(_where)/select_n | solution.py:192
  25.3 2.3 %copy.27 = s32[256,8,32]{2,1,0:T(8,128)} copy(s32[256,8,32]{0,2,1:T(8,128)} %fusion.6) | data formatting | bytes 524288 | tf_op jit(solution)/shard_map/jit(_where)/select_n | solution.py:192
  27.6 1.6 %copy.28 = s32[2,8,128,32]{3,2,1,0:T(8,128)S(1)} copy(s32[2,8,128,32]{3,1,0,2:T(8,128)} %bitcast.17) | data formatting | bytes 524288 | tf_op jit(solution)/shard_map/transpose | solution.py:193
  29.2 14.7 %convert_reduce_fusion.counts_ref = f32[2,8,128,256]{3,2,1,0:T(8,128)} fusion(s32[2,8,128,32]{3,2,1,0:T(8,128)S(1)} %copy.28), kind=kLoop, calls=%fused_computation | loop fusion | flops 49807360 | bytes 2359296 | tf_op jit(solution)/shard_map/reduce_sum | solution.py:194
  43.8 15.4 %all-to-all-done = bf16[33,128,128]{2,0,1:T(8,128)(2,1)S(1)} async-done(((bf16[33,128,128]{2,0,1:T(8,128)(2,1)}), bf16[33,128,128]{2,0,1:T(8,128)(2,1)S(1)}, u32[]{:S(2)}, u32[]{:S(2)}) %all-to-all-start) | async-done | bytes 1081376 | tf_op jit(solution)/shard_map/all_to_all | solution.py:190
  59.2 1.2 %copy.29.incoming_ref = bf16[33,128,128]{2,1,0:T(8,128)(2,1)} copy(bf16[33,128,128]{2,0,1:T(8,128)(2,1)S(1)} %all-to-all-done) | data formatting | bytes 2162688 | tf_op jit(solution)/shard_map/all_to_all | solution.py:190
  60.5 24.0 %shard_map.55 = bf16[2,16,1024]{2,1,0:T(8,128)(2,1)} custom-call(bf16[33,128,128]{2,1,0:T(8,128)(2,1)} %copy.29.incoming_ref, f32[2,8,128,256]{3,2,1,0:T(8,128)} %convert_reduce_fusion.counts_ref), custom_call_target="tpu_custom_call" | custom-call | flops 33554432 | bytes 4194304 | tf_op jit(solution)/shard_map/pallas_call | solution.py:200
  84.5 3.0 %convolution_convert_fusion = bf16[2,1024,512]{2,1,0:T(8,128)(2,1)} fusion(bf16[2,16,1024]{2,1,0:T(8,128)(2,1)} %shard_map.55, bf16[2,16,512]{2,1,0:T(8,128)(2,1)S(1)} %get-tuple-element.42, bf16[2,16,512]{2,1,0:T(8,128)(2,1)S(1)} %get-tuple-element.43), kind=kOutput, calls=%fused_computation.4 | convolution fusion | flops 68550656 | bytes 2228224 | tf_op jit(solution)/shard_map/dot_general | solution.py:233
  (27 shorter events, 0.3 us)
Async XLA Ops:
  0.0 1.6 %copy-start = (bf16[2,1024,512]{2,1,0:T(8,128)(2,1)S(1)}, bf16[2,1024,512]{2,1,0:T(8,128)(2,1)}, u32[]{:S(2)}) copy-start(bf16[2,1024,512]{2,1,0:T(8,128)(2,1)} %param.5) | copy-start | bytes 6291460
  0.0 5.7 %copy-start.3 = (s32[8]{0:T(128)S(1)}, s32[8]{0:T(128)}, u32[]{:S(2)}) copy-start(s32[8]{0:T(128)} %param.6) | copy-start | bytes 100
  0.0 5.9 %copy-start.4 = (bf16[2,31]{1,0:T(2,128)(2,1)S(1)}, bf16[2,31]{1,0:T(2,128)(2,1)}, u32[]{:S(2)}) copy-start(bf16[2,31]{1,0:T(2,128)(2,1)} %param.9) | copy-start | bytes 376
  2.3 4.2 %collective-permute-start = (f32[4,2,2,1024]{3,0,2,1:T(4,128)S(1)}, f32[4,2,2,1024]{3,0,2,1:T(4,128)S(1)}, u32[]{:S(2)}, u32[]{:S(2)}) collective-permute-start(f32[4,2,2,1024]{3,0,2,1:T(4,128)S(1)} %constant_dynamic-slice_fusion), channel_id=1, source_target_pairs={{0,1},{1,0},{2,3},{3,2},{4,5},{5,4},{6,7},{7,6},{8,9},{9,8},{10,11... | collective-permute-start | bytes 196616 | tf_op jit(solution)/shard_map/ppermute | solution.py:163
  9.0 50.2 %all-to-all-start = ((bf16[33,128,128]{2,0,1:T(8,128)(2,1)}), bf16[33,128,128]{2,0,1:T(8,128)(2,1)S(1)}, u32[]{:S(2)}, u32[]{:S(2)}) async-start(bf16[33,128,128]{2,0,1:T(8,128)(2,1)} %pad_maximum_fusion), calls=%async_computation | async-start | bytes 2621440 | tf_op jit(solution)/shard_map/all_to_all | solution.py:190
  22.8 1.5 %copy-start.1 = (s32[256,8,32]{0,2,1:T(8,128)S(1)}, s32[256,8,32]{0,2,1:T(8,128)}, u32[]{:S(2)}) copy-start(s32[256,8,32]{0,2,1:T(8,128)} %param.7) | copy-start | bytes 786436
  22.8 1.5 %copy-start.2 = (s32[256,8]{0,1:T(8,128)S(1)}, s32[256,8]{0,1:T(8,128)}, u32[]{:S(2)}) copy-start(s32[256,8]{0,1:T(8,128)} %param.8) | copy-start | bytes 24580

commit v21 on v20

--- a/solution.py
+++ b/solution.py
@@ -58,7 +58,9 @@
         rows = pl.ds(top, block)
         for i in range(shot_dev):
             for r in range(receiver_dev):
-                weights = [counts_ref[i, r, rows, h * groups : (h + 1) * groups] for h in range(shot_dev)]
+                weights = [
+                    counts_ref[i, r, rows, h * groups : (h + 1) * groups].astype(jnp.float32) for h in range(shot_dev)
+                ]
                 for f in range(local_bins):
                     real_sum = None
                     imag_sum = None
@@ -193,7 +195,7 @@
     codes = codes.reshape(groups, shot_dev, receiver_dev, KMAX).transpose(1, 2, 0, 3)
     counts = jnp.sum(
         (codes[..., None] == jnp.arange(shots, dtype=jnp.int32)).astype(jnp.float32), axis=3
-    )
+    ).astype(jnp.bfloat16)
     kernel = functools.partial(
         multiply_kernel, local_bins=local_bins, shot_dev=shot_dev, receiver_dev=receiver_dev, groups=groups
     )

time: 87.8 us -> 87.5 us (level)
  no operation moved by 1% of the time
where the time goes in v21:
time: 87.5 us; the launch traced here: 87.1 us
  Pallas kernels  23.7 us (27%)
  other arithmetic  18.5 us (21%)
  starting transfers between devices  17.1 us (20%)
  waiting for transfers between devices  16.1 us (18%)
  local copies, waits for them, and re-layouts  7.29 us (8%)
  matrix products  4.16 us (5%)
    pallas_call x1, Pallas kernels, shards(): pl.pallas_call(kernel, out_shape=jax.ShapeDtypeStruct((shot_dev, NF * 2,...  23.7 us
    all_to_all x1, waiting for transfers between devices, shards(): incoming = lax.all_to_all(outgoing, 'shot', 1, 1, tiled=True)  15.6 us
    reduce_sum x1, other arithmetic, shards(): jnp.sum((codes[..., None] == jnp.arange(shots, dtype=jnp.int32)).astype(j...  14.4 us
    all_to_all x1, starting transfers between devices, shards(): incoming = lax.all_to_all(outgoing, 'shot', 1, 1, tiled=True)  13.8 us
    ppermute x1, starting transfers between devices, shards(): theirs = lax.ppermute(theirs, 'freq', [(0, 1), (1, 0)])  3.33 us
    dot_general x1, matrix products, shards(): lax.dot_general(jnp.concatenate([piece, piece], axis=1), jnp.concatenate(...  2.99 us
    select_n x1, local copies, waits for them, and re-layouts, shards(): jnp.where(used, aperture % shot_dev * groups + aperture // shot_dev, -1)  2.29 us
  transfers between devices with their start and end apart: 2, of which 2 were waited for; matrix products, arithmetic and copies ran while one was open for 24% of the time, Pallas kernels for 0%

profile of v21, /device:TPU:1, one launch (start us, length us, event | category | flops | bytes accessed | tf_op | source)
XLA Modules:
  0.0 87.1 jit_solution(7033736585949660306)
XLA Ops:
  0.0 1.0 %fusion.33 = (f32[8,1,512]{2,0,1:T(8,128)S(1)}, f32[8,1,512]{2,0,1:T(8,128)S(1)}) fusion(s32[512]{0:T(512)S(1)} %iota_add_fusion.1, s32[8]{0:T(128)} %param.6), kind=kLoop, calls=%fused_computation.67 | loop fusion | flops 61440 | bytes 34848 | tf_op jit(solution)/shard_map/cos | solution.py:34
  1.0 0.6 copy-done
  1.6 0.6 fusion
  2.3 3.3 %collective-permute-start = (f32[4,2,2,1024]{3,0,2,1:T(4,128)S(1)}, f32[4,2,2,1024]{3,0,2,1:T(4,128)S(1)}, u32[]{:S(2)}, u32[]{:S(2)}) collective-permute-start(f32[4,2,2,1024]{3,0,2,1:T(4,128)S(1)} %constant_dynamic-slice_fusion), channel_id=1, source_target_pairs={{0,1},{1,0},{2,3},{3,2},{4,5},{5,4},{6,7},{7,6},{8,9},{9,8},{10,11... | collective-permute-start | bytes 196616 | tf_op jit(solution)/shard_map/ppermute | solution.py:165
  5.7 0.2 cosine_convert_fusion
  6.0 0.5 collective-permute-done
  6.6 0.3 convolution_convert_fusion.2
  6.9 0.2 fusion.2
  7.2 0.1 broadcast_in_dim.45
  7.4 1.7 %pad_maximum_fusion = bf16[33,128,128]{2,0,1:T(8,128)(2,1)} fusion(bf16[32,128,128]{2,0,1:T(8,128)(2,1)S(1)} %broadcast_in_dim.45, bf16[1,128,128]{2,0,1:T(2,128)(2,1)S(1)} %copy.26), kind=kLoop, calls=%fused_computation.5 | loop fusion | flops 2162688 | bytes 2162688 | tf_op jit(solution)/shard_map/concatenate | solution.py:184
  9.0 13.8 %all-to-all-start = ((bf16[33,128,128]{2,0,1:T(8,128)(2,1)}), bf16[33,128,128]{2,0,1:T(8,128)(2,1)S(1)}, u32[]{:S(2)}, u32[]{:S(2)}) async-start(bf16[33,128,128]{2,0,1:T(8,128)(2,1)} %pad_maximum_fusion), calls=%async_computation | async-start | bytes 2621440 | tf_op jit(solution)/shard_map/all_to_all | solution.py:192
  22.8 0.4 slice_reduce_fusion.29
  23.2 0.5 slice_reduce_fusion.30
  23.7 0.2 fusion.55
  23.9 0.2 fusion.54
  24.1 0.2 subtract_convert_fusion
  24.4 1.0 %fusion.6 = s32[256,8,32]{0,2,1:T(8,128)} fusion(s32[256,8,32]{0,2,1:T(8,128)S(1)} %copy-done.1, s32[256,8]{0,1:T(8,128)S(1)} %copy-done.2), kind=kLoop, calls=%fused_computation.19 | loop fusion | flops 1507328 | bytes 532480 | tf_op jit(solution)/shard_map/jit(_where)/select_n | solution.py:194
  25.3 2.3 %copy.27 = s32[256,8,32]{2,1,0:T(8,128)} copy(s32[256,8,32]{0,2,1:T(8,128)} %fusion.6) | data formatting | bytes 524288 | tf_op jit(solution)/shard_map/jit(_where)/select_n | solution.py:194
  27.6 1.6 %copy.28 = s32[2,8,128,32]{3,2,1,0:T(8,128)S(1)} copy(s32[2,8,128,32]{3,1,0,2:T(8,128)} %bitcast.17) | data formatting | bytes 524288 | tf_op jit(solution)/shard_map/transpose | solution.py:195
  29.2 14.4 %convert_reduce_fusion.counts_ref = bf16[2,8,128,256]{3,2,1,0:T(8,128)(2,1)} fusion(s32[2,8,128,32]{3,2,1,0:T(8,128)S(1)} %copy.28), kind=kLoop, calls=%fused_computation | loop fusion | flops 49807360 | bytes 1310720 | tf_op jit(solution)/shard_map/reduce_sum | solution.py:196
  43.6 15.6 %all-to-all-done = bf16[33,128,128]{2,0,1:T(8,128)(2,1)S(1)} async-done(((bf16[33,128,128]{2,0,1:T(8,128)(2,1)}), bf16[33,128,128]{2,0,1:T(8,128)(2,1)S(1)}, u32[]{:S(2)}, u32[]{:S(2)}) %all-to-all-start) | async-done | bytes 1081376 | tf_op jit(solution)/shard_map/all_to_all | solution.py:192
  59.2 1.2 %copy.29.incoming_ref = bf16[33,128,128]{2,1,0:T(8,128)(2,1)} copy(bf16[33,128,128]{2,0,1:T(8,128)(2,1)S(1)} %all-to-all-done) | data formatting | bytes 2162688 | tf_op jit(solution)/shard_map/all_to_all | solution.py:192
  60.5 23.7 %shard_map.55 = bf16[2,16,1024]{2,1,0:T(8,128)(2,1)} custom-call(bf16[33,128,128]{2,1,0:T(8,128)(2,1)} %copy.29.incoming_ref, bf16[2,8,128,256]{3,2,1,0:T(8,128)(2,1)} %convert_reduce_fusion.counts_ref), custom_call_target="tpu_custom_call" | custom-call | flops 33554432 | bytes 4194304 | tf_op jit(solution)/shard_map/pallas_call | solution.py:202
  84.1 3.0 %convolution_convert_fusion = bf16[2,1024,512]{2,1,0:T(8,128)(2,1)} fusion(bf16[2,16,1024]{2,1,0:T(8,128)(2,1)} %shard_map.55, bf16[2,16,512]{2,1,0:T(8,128)(2,1)S(1)} %get-tuple-element.42, bf16[2,16,512]{2,1,0:T(8,128)(2,1)S(1)} %get-tuple-element.43), kind=kOutput, calls=%fused_computation.4 | convolution fusion | flops 68550656 | bytes 2228224 | tf_op jit(solution)/shard_map/dot_general | solution.py:235
  (27 shorter events, 0.3 us)
Async XLA Ops:
  0.0 1.6 %copy-start = (bf16[2,1024,512]{2,1,0:T(8,128)(2,1)S(1)}, bf16[2,1024,512]{2,1,0:T(8,128)(2,1)}, u32[]{:S(2)}) copy-start(bf16[2,1024,512]{2,1,0:T(8,128)(2,1)} %param.5) | copy-start | bytes 6291460
  0.0 5.7 %copy-start.3 = (s32[8]{0:T(128)S(1)}, s32[8]{0:T(128)}, u32[]{:S(2)}) copy-start(s32[8]{0:T(128)} %param.6) | copy-start | bytes 100
  0.0 5.9 %copy-start.4 = (bf16[2,31]{1,0:T(2,128)(2,1)S(1)}, bf16[2,31]{1,0:T(2,128)(2,1)}, u32[]{:S(2)}) copy-start(bf16[2,31]{1,0:T(2,128)(2,1)} %param.9) | copy-start | bytes 376
  2.3 4.2 %collective-permute-start = (f32[4,2,2,1024]{3,0,2,1:T(4,128)S(1)}, f32[4,2,2,1024]{3,0,2,1:T(4,128)S(1)}, u32[]{:S(2)}, u32[]{:S(2)}) collective-permute-start(f32[4,2,2,1024]{3,0,2,1:T(4,128)S(1)} %constant_dynamic-slice_fusion), channel_id=1, source_target_pairs={{0,1},{1,0},{2,3},{3,2},{4,5},{5,4},{6,7},{7,6},{8,9},{9,8},{10,11... | collective-permute-start | bytes 196616 | tf_op jit(solution)/shard_map/ppermute | solution.py:165
  9.0 50.2 %all-to-all-start = ((bf16[33,128,128]{2,0,1:T(8,128)(2,1)}), bf16[33,128,128]{2,0,1:T(8,128)(2,1)S(1)}, u32[]{:S(2)}, u32[]{:S(2)}) async-start(bf16[33,128,128]{2,0,1:T(8,128)(2,1)} %pad_maximum_fusion), calls=%async_computation | async-start | bytes 2621440 | tf_op jit(solution)/shard_map/all_to_all | solution.py:192
  22.8 1.5 %copy-start.1 = (s32[256,8,32]{0,2,1:T(8,128)S(1)}, s32[256,8,32]{0,2,1:T(8,128)}, u32[]{:S(2)}) copy-start(s32[256,8,32]{0,2,1:T(8,128)} %param.7) | copy-start | bytes 786436
  22.8 1.5 %copy-start.2 = (s32[256,8]{0,1:T(8,128)S(1)}, s32[256,8]{0,1:T(8,128)}, u32[]{:S(2)}) copy-start(s32[256,8]{0,1:T(8,128)} %param.8) | copy-start | bytes 24580
